TPU v7x, 32 devices: a whole 2x2x4 slice. The times are simulated.
32 devices in a mesh: wide: 8 (over z, x), narrow: 4 (over y, core).
Axes of the slice: x: 2, y: 2, z: 4, core: 2. Of those that a mesh axis runs over, the one named last changes fastest.
Arguments:
- tokens: bfloat16 [32768, 768], P(('wide', 'narrow')), may hold values from -6 to 6
- norm1_gain: bfloat16 [768], P(('wide', 'narrow')), may hold values from 0.25 to 1.75
- norm1_bias: bfloat16 [768], P(('wide', 'narrow')), may hold values from -2.5 to 2.5
- qkv_weight: bfloat16 [768, 2304], P(('wide', 'narrow')), may hold values from -0.21875 to 0.21875
- qkv_bias: bfloat16 [1536], P(('wide', 'narrow')), may hold values from -2.5 to 2.5
- out_weight: bfloat16 [768, 768], P(('wide', 'narrow')), may hold values from -9 to 9
- out_bias: bfloat16 [768], P(('wide', 'narrow')), may hold values from -12 to 12
- norm2_gain: bfloat16 [768], P(('wide', 'narrow')), may hold values from 0.25 to 1.75
- norm2_bias: bfloat16 [768], P(('wide', 'narrow')), may hold values from -2.5 to 2.5
- fc_weight: bfloat16 [768, 3072], P(('wide', 'narrow')), may hold values from -0.21875 to 0.21875
- fc_bias: bfloat16 [3072], P(('wide', 'narrow')), may hold values from -3 to 3
- proj_weight: bfloat16 [3072, 768], P(('wide', 'narrow')), may hold values from -2.5 to 2.5
- proj_bias: bfloat16 [768], P(('wide', 'narrow')), may hold values from -12 to 12
- seq_lengths: int32 [32], P(('wide', 'narrow')), may hold values from 64 to 1024, as said below
- out_cotangent: bfloat16 [32768, 768], P(('wide', 'narrow')), may hold values from -6 to 6
Outputs:
- layer_out: bfloat16 [32768, 768], P(('wide', 'narrow'))
- input_grad: bfloat16 [32768, 768], P(('wide', 'narrow'))
- norm1_gain_grad: float32 [768], P(('wide', 'narrow'))
- norm1_bias_grad: float32 [768], P(('wide', 'narrow'))
- qkv_weight_grad: float32 [768, 2304], P(('wide', 'narrow'))
- qkv_bias_grad: float32 [1536], P(('wide', 'narrow'))
- out_weight_grad: float32 [768, 768], P(('wide', 'narrow'))
- out_bias_grad: float32 [768], P(('wide', 'narrow'))
- norm2_gain_grad: float32 [768], P(('wide', 'narrow'))
- norm2_bias_grad: float32 [768], P(('wide', 'narrow'))
- fc_weight_grad: float32 [768, 3072], P(('wide', 'narrow'))
- fc_bias_grad: float32 [3072], P(('wide', 'narrow'))
- proj_weight_grad: float32 [3072, 768], P(('wide', 'narrow'))
- proj_bias_grad: float32 [768], P(('wide', 'narrow'))
Inputs may be any that keep to these rules, and one draw needn't show every extreme that they name: Each slot holds one sequence of seq_lengths tokens from its first position on; the rest of the slot is padding. Some slot is full in every draw.
All inputs are finite; a program needn't handle non-finite values.
Results may differ from a plain program's by a relative error of at most 0.013.
Values may be sent and summed in bfloat16 or wider, within the bound.
No kernel may reach another device: no remote copies, remote signals or barrier semaphores. Data moves between devices by JAX's collectives and lax.ppermute only.
A program may use at most 256 MiB of HBM per device.

v0:
```python
import math

import jax
import jax.numpy as jnp
from jax import lax
from jax.sharding import PartitionSpec as P

D = 768
H = 12
HD = 64


branch_scale = 1.0 / math.sqrt(48.0)
norm_epsilon = 1e-05
masked_value = -1e30


def layer_norm(values_in, gain_vec, shift_vec):
    row_mean = jnp.mean(values_in, axis=-1, keepdims=True)
    centred = values_in - row_mean
    row_var = jnp.mean(centred * centred, axis=-1, keepdims=True)
    return centred * lax.rsqrt(row_var + norm_epsilon) * gain_vec + shift_vec


def gelu_tanh(pre_act):
    inner = 0.7978845608028654 * (pre_act + 0.044715 * pre_act * pre_act * pre_act)
    return 0.5 * pre_act * (1.0 + jnp.tanh(inner))


def product(left, right):
    return jnp.dot(left, right, preferred_element_type=jnp.float32)


def left_product(left, right):
    return lax.dot_general(
        left, right, (((0,), (0,)), ((), ())), preferred_element_type=jnp.float32
    )


def right_product(left, right):
    return lax.dot_general(
        left, right, (((1,), (1,)), ((), ())), preferred_element_type=jnp.float32
    )


def split_heads(packed_slot):
    slot_size = packed_slot.shape[0]
    query_rows = packed_slot[:, :D].reshape(slot_size, H, HD)
    key_rows = packed_slot[:, D : 2 * D].reshape(slot_size, H, HD)
    value_rows = packed_slot[:, 2 * D :].reshape(slot_size, H, HD)
    return (query_rows, key_rows, value_rows)


def block_scores(query_block, key_block, block_start):
    score_scale = 1.0 / math.sqrt(HD)
    raw_scores = (
        jnp.einsum("qhd,khd->hqk", query_block, key_block, preferred_element_type=jnp.float32)
        * score_scale
    )
    row_place = block_start + jnp.arange(query_block.shape[0])
    col_place = jnp.arange(key_block.shape[0])
    causal = col_place[None, :] <= row_place[:, None]
    return (jnp.where(causal[None], raw_scores, masked_value), causal)


def forward_block(query_block, key_block, value_block, block_start):
    scores, causal = block_scores(query_block, key_block, block_start)
    row_max = jnp.max(scores, axis=-1, keepdims=True)
    shifted = jnp.exp(scores - row_max)
    row_total = jnp.sum(shifted, axis=-1, keepdims=True)
    soft_probs = (shifted / row_total).astype(jnp.bfloat16)
    mixed_rows = jnp.einsum(
        "hqk,khd->qhd", soft_probs, value_block, preferred_element_type=jnp.float32
    )
    return (mixed_rows, (row_max + jnp.log(row_total))[:, :, 0])


def slot_forward(item):
    packed_slot, seq_length = item
    query_rows, key_rows, value_rows = split_heads(packed_slot)
    slot_size = packed_slot.shape[0]
    block_rows = min(512, slot_size)
    mixed_parts = []
    stats_parts = []
    for block_index in range(slot_size // block_rows):
        block_start = block_index * block_rows
        block_end = block_start + block_rows
        query_block = query_rows[block_start:block_end]
        key_block = key_rows[:block_end]
        value_block = value_rows[:block_end]

        def compute_block():
            return forward_block(query_block, key_block, value_block, block_start)

        mixed_block, block_stats = compute_block()
        mixed_parts.append(mixed_block)
        stats_parts.append(block_stats)
    mixed_rows = jnp.concatenate(mixed_parts, 0)
    valid_rows = (jnp.arange(slot_size) < seq_length).astype(jnp.float32)
    mixed_rows = mixed_rows * valid_rows[:, None, None]
    return (mixed_rows.reshape(slot_size, D), jnp.concatenate(stats_parts, 1))


def slot_backward(item):
    packed_slot, grad_slot, slot_stats, seq_length = item
    query_rows, key_rows, value_rows = split_heads(packed_slot)
    slot_size = packed_slot.shape[0]
    grad_rows = grad_slot.reshape(slot_size, H, HD)
    score_scale = 1.0 / math.sqrt(HD)
    block_rows = min(512, slot_size)
    query_parts = []
    key_grad = jnp.zeros((slot_size, H, HD), jnp.float32)
    value_grad = jnp.zeros((slot_size, H, HD), jnp.float32)
    for block_index in range(slot_size // block_rows):
        block_start = block_index * block_rows
        block_end = block_start + block_rows
        query_block = query_rows[block_start:block_end]
        key_block = key_rows[:block_end]
        value_block = value_rows[:block_end]
        grad_block = grad_rows[block_start:block_end]
        stats_block = slot_stats[:, block_start:block_end]

        def compute_block():
            scores, causal = block_scores(query_block, key_block, block_start)
            soft_probs = jnp.where(causal[None], jnp.exp(scores - stats_block[:, :, None]), 0.0)
            low_probs = soft_probs.astype(jnp.bfloat16)
            value_part = jnp.einsum(
                "hqk,qhd->khd", low_probs, grad_block, preferred_element_type=jnp.float32
            )
            prob_grad = jnp.einsum(
                "qhd,khd->hqk", grad_block, value_block, preferred_element_type=jnp.float32
            )
            row_delta = jnp.sum(soft_probs * prob_grad, axis=-1, keepdims=True)
            score_grad = (soft_probs * (prob_grad - row_delta)).astype(jnp.bfloat16)
            query_part = (
                jnp.einsum(
                    "hqk,khd->qhd", score_grad, key_block, preferred_element_type=jnp.float32
                )
                * score_scale
            )
            key_part = (
                jnp.einsum(
                    "hqk,qhd->khd", score_grad, query_block, preferred_element_type=jnp.float32
                )
                * score_scale
            )
            return (query_part, key_part, value_part)

        query_part, key_part, value_part = compute_block()
        pad_rows = ((0, slot_size - block_end), (0, 0), (0, 0))
        key_grad = key_grad + jnp.pad(key_part, pad_rows)
        value_grad = value_grad + jnp.pad(value_part, pad_rows)
        query_parts.append(query_part)
    query_grad = jnp.concatenate(query_parts, 0)
    return jnp.concatenate(
        [
            query_grad.reshape(slot_size, D),
            key_grad.reshape(slot_size, D),
            value_grad.reshape(slot_size, D),
        ],
        axis=1,
    )


def local(
    tokens,
    norm1_gain,
    norm1_bias,
    qkv_weight,
    qkv_bias,
    out_weight,
    out_bias,
    norm2_gain,
    norm2_bias,
    fc_weight,
    fc_bias,
    proj_weight,
    proj_bias,
    seq_lengths,
    out_cotangent,
):
    attn_full = (
        lax.all_gather(norm1_gain, ("wide", "narrow"), axis=0, tiled=True),
        lax.all_gather(norm1_bias, ("wide", "narrow"), axis=0, tiled=True),
        lax.all_gather(qkv_weight, ("wide", "narrow"), axis=0, tiled=True),
        lax.all_gather(qkv_bias, ("wide", "narrow"), axis=0, tiled=True),
        lax.all_gather(out_weight, ("wide", "narrow"), axis=0, tiled=True),
        lax.all_gather(out_bias, ("wide", "narrow"), axis=0, tiled=True),
    )
    gain_one, shift_one, qkv_full, qkv_bias_full, out_full, out_bias_full = attn_full
    slot_count = seq_lengths.shape[0]
    slot_size = tokens.shape[0] // slot_count
    position = jnp.arange(slot_size)
    valid_rows = (position[None, :] < seq_lengths[:, None]).reshape(-1, 1).astype(jnp.float32)
    input_rows = tokens.astype(jnp.float32)
    gain_one_f = gain_one.astype(jnp.float32)
    shift_one_f = shift_one.astype(jnp.float32)
    norm_one = layer_norm(input_rows, gain_one_f, shift_one_f)
    low_one = norm_one.astype(jnp.bfloat16)
    bias_full = jnp.concatenate(
        [
            qkv_bias_full[:D].astype(jnp.float32),
            jnp.zeros((D,), jnp.float32),
            qkv_bias_full[D:].astype(jnp.float32),
        ]
    )
    packed = (product(low_one, qkv_full) + bias_full).astype(jnp.bfloat16)
    slot_packed = packed.reshape(slot_count, slot_size, 3 * D)
    mixed_all, stats_all = lax.map(slot_forward, (slot_packed, seq_lengths))
    low_mixed = mixed_all.reshape(-1, D).astype(jnp.bfloat16)
    branch = product(low_mixed, out_full) + out_bias_full.astype(jnp.float32)
    middle = input_rows + branch_scale * branch
    mlp_full = (
        lax.all_gather(norm2_gain, ("wide", "narrow"), axis=0, tiled=True),
        lax.all_gather(norm2_bias, ("wide", "narrow"), axis=0, tiled=True),
        lax.all_gather(fc_weight, ("wide", "narrow"), axis=0, tiled=True),
        lax.all_gather(fc_bias, ("wide", "narrow"), axis=0, tiled=True),
        lax.all_gather(proj_weight, ("wide", "narrow"), axis=0, tiled=True),
        lax.all_gather(proj_bias, ("wide", "narrow"), axis=0, tiled=True),
    )
    gain_two, shift_two, fc_full, fc_bias_full, proj_full, proj_bias_full = mlp_full
    gain_two_f = gain_two.astype(jnp.float32)
    shift_two_f = shift_two.astype(jnp.float32)
    norm_two = layer_norm(middle, gain_two_f, shift_two_f)
    low_two = norm_two.astype(jnp.bfloat16)
    hidden = product(low_two, fc_full) + fc_bias_full.astype(jnp.float32)
    low_active = gelu_tanh(hidden).astype(jnp.bfloat16)
    second = product(low_active, proj_full) + proj_bias_full.astype(jnp.float32)
    layer_out = (middle + branch_scale * second).astype(jnp.bfloat16)
    mlp_back = (
        lax.all_gather(norm2_gain, ("wide", "narrow"), axis=0, tiled=True),
        lax.all_gather(norm2_bias, ("wide", "narrow"), axis=0, tiled=True),
        lax.all_gather(fc_weight, ("wide", "narrow"), axis=0, tiled=True),
        lax.all_gather(fc_bias, ("wide", "narrow"), axis=0, tiled=True),
        lax.all_gather(proj_weight, ("wide", "narrow"), axis=0, tiled=True),
        lax.all_gather(proj_bias, ("wide", "narrow"), axis=0, tiled=True),
    )
    fc_back = mlp_back[2]
    proj_back = mlp_back[4]
    cotangent = out_cotangent.astype(jnp.float32) * valid_rows
    grad_second = (branch_scale * cotangent).astype(jnp.bfloat16)
    proj_weight_term = left_product(low_active, grad_second)
    proj_bias_term = jnp.sum(grad_second.astype(jnp.float32), axis=0)
    grad_active = right_product(grad_second, proj_back)
    unused_value, gelu_pull = jax.vjp(gelu_tanh, hidden)
    grad_hidden = gelu_pull(grad_active)[0].astype(jnp.bfloat16)
    fc_weight_term = left_product(low_two, grad_hidden)
    fc_bias_term = jnp.sum(grad_hidden.astype(jnp.float32), axis=0)
    grad_norm_two = right_product(grad_hidden, fc_back)
    unused_norm, norm_two_pull = jax.vjp(layer_norm, middle, gain_two_f, shift_two_f)
    middle_part, gain_two_term, shift_two_term = norm_two_pull(grad_norm_two)
    grad_middle = cotangent + middle_part
    mlp_grads = (
        lax.psum_scatter(gain_two_term, ("wide", "narrow"), scatter_dimension=0, tiled=True),
        lax.psum_scatter(shift_two_term, ("wide", "narrow"), scatter_dimension=0, tiled=True),
        lax.psum_scatter(fc_weight_term, ("wide", "narrow"), scatter_dimension=0, tiled=True),
        lax.psum_scatter(fc_bias_term, ("wide", "narrow"), scatter_dimension=0, tiled=True),
        lax.psum_scatter(proj_weight_term, ("wide", "narrow"), scatter_dimension=0, tiled=True),
        lax.psum_scatter(proj_bias_term, ("wide", "narrow"), scatter_dimension=0, tiled=True),
    )
    attn_back = (
        lax.all_gather(norm1_gain, ("wide", "narrow"), axis=0, tiled=True),
        lax.all_gather(norm1_bias, ("wide", "narrow"), axis=0, tiled=True),
        lax.all_gather(qkv_weight, ("wide", "narrow"), axis=0, tiled=True),
        lax.all_gather(qkv_bias, ("wide", "narrow"), axis=0, tiled=True),
        lax.all_gather(out_weight, ("wide", "narrow"), axis=0, tiled=True),
        lax.all_gather(out_bias, ("wide", "narrow"), axis=0, tiled=True),
    )
    qkv_back = attn_back[2]
    out_back = attn_back[4]
    grad_branch = (branch_scale * grad_middle).astype(jnp.bfloat16)
    out_weight_term = left_product(low_mixed, grad_branch)
    out_bias_term = jnp.sum(grad_branch.astype(jnp.float32), axis=0)
    grad_mixed = right_product(grad_branch, out_back).astype(jnp.bfloat16) * valid_rows.astype(
        jnp.bfloat16
    )
    grad_packed = lax.map(
        slot_backward,
        (slot_packed, grad_mixed.reshape(slot_count, slot_size, D), stats_all, seq_lengths),
    )
    low_grad_packed = grad_packed.reshape(-1, 3 * D).astype(jnp.bfloat16)
    qkv_weight_term = left_product(low_one, low_grad_packed)
    column_sums = jnp.sum(low_grad_packed.astype(jnp.float32), axis=0)
    qkv_bias_term = jnp.concatenate([column_sums[:D], column_sums[2 * D :]])
    grad_norm_one = right_product(low_grad_packed, qkv_back)
    unused_first, norm_one_pull = jax.vjp(layer_norm, input_rows, gain_one_f, shift_one_f)
    input_part, gain_one_term, shift_one_term = norm_one_pull(grad_norm_one)
    input_grad = (grad_middle + input_part).astype(jnp.bfloat16)
    attn_grads = (
        lax.psum_scatter(gain_one_term, ("wide", "narrow"), scatter_dimension=0, tiled=True),
        lax.psum_scatter(shift_one_term, ("wide", "narrow"), scatter_dimension=0, tiled=True),
        lax.psum_scatter(qkv_weight_term, ("wide", "narrow"), scatter_dimension=0, tiled=True),
        lax.psum_scatter(qkv_bias_term, ("wide", "narrow"), scatter_dimension=0, tiled=True),
        lax.psum_scatter(out_weight_term, ("wide", "narrow"), scatter_dimension=0, tiled=True),
        lax.psum_scatter(out_bias_term, ("wide", "narrow"), scatter_dimension=0, tiled=True),
    )
    return (
        layer_out,
        input_grad,
        attn_grads[0],
        attn_grads[1],
        attn_grads[2],
        attn_grads[3],
        attn_grads[4],
        attn_grads[5],
        mlp_grads[0],
        mlp_grads[1],
        mlp_grads[2],
        mlp_grads[3],
        mlp_grads[4],
        mlp_grads[5],
    )


def solution(mesh):
    placed = (
        P(("wide", "narrow"), None),
        P(("wide", "narrow")),
        P(("wide", "narrow")),
        P(("wide", "narrow"), None),
        P(("wide", "narrow")),
        P(("wide", "narrow"), None),
        P(("wide", "narrow")),
        P(("wide", "narrow")),
        P(("wide", "narrow")),
        P(("wide", "narrow"), None),
        P(("wide", "narrow")),
        P(("wide", "narrow"), None),
        P(("wide", "narrow")),
        P(("wide", "narrow")),
        P(("wide", "narrow"), None),
    )
    return jax.shard_map(
        local,
        mesh=mesh,
        in_specs=placed,
        out_specs=(
            P(("wide", "narrow"), None),
            P(("wide", "narrow"), None),
            P(("wide", "narrow")),
            P(("wide", "narrow")),
            P(("wide", "narrow"), None),
            P(("wide", "narrow")),
            P(("wide", "narrow"), None),
            P(("wide", "narrow")),
            P(("wide", "narrow")),
            P(("wide", "narrow")),
            P(("wide", "narrow"), None),
            P(("wide", "narrow")),
            P(("wide", "narrow"), None),
            P(("wide", "narrow")),
        ),
        check_vma=False,
    )
```

profile of v0, /device:TPU:9, one launch (start us, length us, event | category | flops | bytes accessed | tf_op | source)
XLA Modules:
  0.0 829.3 jit_solution(7919244227806289655)
XLA Ops:
  17.8 0.8 dynamic-update-slice.6
  18.7 40.8 %all-reduce.19 = (bf16[768]{0:T(1024)(128)(2,1)S(1)}, bf16[1536]{0:T(1024)(128)(2,1)S(1)}, bf16[768]{0:T(1024)(128)(2,1)S(1)}, bf16[768]{0:T(1024)(128)(2,1)S(1)...) all-reduce(bf16[768]{0:T(1024)(128)(2,1)S(1)} %dynamic-update-slice, ...), channel_id=1, replica_groups=mesh['wide'=8,'narrow'=4] {'wide','narrow'}, use_global_device_ids=true, to_apply=%add.5 | all-reduce | flops 9216 | bytes 36864
  60.7 1.2 iota_compare_fusion
  61.9 1.7 copy.73
  65.0 1.7 copy.82
  66.7 5.8 all-gather.5.cloned.1.call-done
  72.6 6.4 add_convert_fusion
  79.0 1.7 fusion.72
  80.7 1.9 fusion.73
  82.6 2.7 copy.80
  85.2 2.3 copy.76
  87.5 2.3 copy.79
  89.9 2.3 copy.75
  92.2 2.3 copy.74
  94.5 2.7 copy.78
  97.2 3.4 fusion.14
  100.7 2.6 fusion.13
  103.2 2.0 copy-done
  105.3 14.6 %fusion.2 = (f32[12,512]{1,0:T(8,128)S(1)}, f32[12,512,1024]{2,1,0:T(8,128)}) fusion(pred[512,1024]{1,0:T(8,128)(4,1)} %iota_compare_fusion, bf16[512,12,64]{0,2,1:T(8,128)(2,1)} %bitcast.76, bf16[1024,12,64]{0,2,1:T(8,128)(2,1)} %bitcast.72), kind=kOutput, calls=%fused_computation.11 | convolution fusion | flops 824174592 | bytes 28073984 | tf_op jit(solution)/shard_map/while/body/eval_jaxpr/qhd,khd->hqk/dot_general | solution.py:57
  119.9 13.4 %fusion = f32[12,512]{1,0:T(8,128)S(1)} fusion(f32[12,512,1024]{2,1,0:T(8,128)} %get-tuple-element.124, f32[12,512]{1,0:T(8,128)S(1)} %get-tuple-element.123, pred[512,1024]{1,0:T(8,128)(4,1)S(1)} %copy-done.11), kind=kLoop, calls=%fused_computation.6 | loop fusion | flops 25159680 | bytes 25739264 | tf_op jit(solution)/shard_map/while/body/eval_jaxpr/reduce_sum | solution.py:70
  133.3 8.1 fusion.17
  142.3 1.2 slice-done.5
  143.5 9.7 %fusion.12 = f32[12,64,512]{2,1,0:T(8,128)} fusion(bf16[1024,12,64]{0,2,1:T(8,128)(2,1)} %bitcast.86, f32[12,512,1024]{2,1,0:T(8,128)S(1)} %bitcast.69, f32[12,512]{1,0:T(8,128)S(1)} %fusion, f32[12,512]{1,0:T(8,128)S(1)} %get-tuple-element.123, pred[512,1024]{1,0:T(8,128)(4,1)S(1)} %copy-done.11), kind=kOutput, calls=%fused_computation.29 | convolution fusion | flops 836763648 | bytes 28884992 | tf_op jit(solution)/shard_map/while/body/eval_jaxpr/hqk,khd->qhd/dot_general | solution.py:72
  153.2 5.6 fusion.76
  158.7 2.3 multiply_reduce_fusion.4
  161.7 33.0 %all-gather.9.cloned.1.call-done = bf16[768,3072]{1,0:T(8,128)(2,1)} async-done(((bf16[24,3072]{1,0:T(8,128)(2,1)}), bf16[768,3072]{1,0:T(8,128)(2,1)}) %all-gather.9.cloned.1.call-update) | async-done | bytes 4718608 | tf_op jit(solution)/shard_map/all_gather | solution.py:216
  194.7 11.0 %fusion.68 = f32[1024,3072]{1,0:T(8,128)} fusion(bf16[768,3072]{1,0:T(8,128)(2,1)} %all-gather.9.cloned.1.call-done, f32[1024,768]{0,1:T(8,128)} %get-tuple-element.128, f32[768]{0:T(1024)S(1)} %convert_element_type.145, f32[768]{0:T(1024)S(1)} %convert_element_type.144, f32[1024]{0:T(1024)S(1)} %fusion.47, f32[1024]{0:T(1024)S(1)} %broadcast_multiply_fusion), kind=kOutput, calls=%fused_computation.123 | convolution fusion | flops 4835770368 | bytes 20461568 | tf_op jit(solution)/shard_map/dot_general | solution.py:31
  205.7 54.2 %all-gather.11.cloned.1.call-done = bf16[3072,768]{1,0:T(8,128)(2,1)} async-done(((bf16[96,768]{1,0:T(8,128)(2,1)}), bf16[3072,768]{1,0:T(8,128)(2,1)}) %all-gather.11.cloned.1.call-update) | async-done | bytes 4718608 | tf_op jit(solution)/shard_map/all_gather | solution.py:218
  259.9 18.6 %convert_reduce_fusion = (f32[3072]{0:T(1024)}, bf16[1024,3072]{1,0:T(8,128)(2,1)S(1)}) fusion(f32[1024,3072]{1,0:T(8,128)} %fusion.68, f32[3072]{0:T(1024)S(1)} %copy-done.44, bf16[3072,768]{1,0:T(8,128)(2,1)} %all-gather.11.cloned.1.call-done, bf16[1024,768]{0,1:T(8,128)(2,1)S(1)} %copy.82, f32[1024]{0:T(1024)S(1)} %copy-done.32), kind=kOutput, calls=%fused_computation.18 | convolution fusion | flops 4919915520 | bytes 25194496 | tf_op jit(solution)/shard_map/dot_general | solution.py:41
  278.5 7.3 fusion.78
  285.9 2.5 copy.83
  288.4 3.4 multiply_reduce_fusion.2
  291.8 2.8 fusion.71
  294.7 1.6 convert_reduce_fusion.4
  296.3 0.9 copy-done.53
  297.7 2.9 fusion.42
  300.6 1.4 fusion.34
  302.1 7.8 fusion.35
  310.0 7.0 multiply_reduce_fusion.1
  317.1 10.2 %multiply_convert_fusion.1 = bf16[12,512,512]{1,2,0:T(8,128)(2,1)S(1)} fusion(f32[12,512,512]{1,2,0:T(8,128)} %get-tuple-element.130, f32[12,512]{1,0:T(8,128)S(1)} %get-tuple-element.129, f32[12,512]{1,0:T(8,128)S(1)} %copy-done.26, f32[12,512,512]{1,2,0:T(8,128)} %copy-done, pred[512,512]{0,1:T(8,128)(4,1)S(1)} %iota_compare_fusion.1), kind=kLoop, calls=%fused_computation.21 | loop fusion | flops 22020096 | bytes 31768576 | tf_op jit(solution)/shard_map/while/body/eval_jaxpr/convert_element_type | solution.py:134
  327.4 3.2 multiply_bitcast_fusion
  330.8 22.1 %multiply_reduce_fusion = (f32[12,512]{1,0:T(8,128)S(1)}, f32[12,512,1024]{2,1,0:T(8,128)}) fusion(f32[12,512]{1,0:T(8,128)S(1)} %log_add_fusion, f32[12,512,1024]{2,1,0:T(8,128)} %get-tuple-element.124, pred[512,1024]{1,0:T(8,128)(4,1)S(1)} %copy-done.12, bf16[512,12,64]{0,2,1:T(8,128)(2,1)S(1)} %bitcast.93, bf16[1024,12,64]{0,2,1:T(8,128)(2,1)S(1)} %bitcast.87), kind=kOutput, calls=%fused_computation.1 | convolution fusion | flops 843048960 | bytes 53264384 | tf_op jit(solution)/shard_map/while/body/eval_jaxpr/qhd,khd->hqk/dot_general | solution.py:130
  352.9 18.1 %multiply_convert_fusion = bf16[12,512,1024]{2,1,0:T(8,128)(2,1)S(1)} fusion(f32[12,512,1024]{2,1,0:T(8,128)} %get-tuple-element.132, f32[12,512]{1,0:T(8,128)S(1)} %get-tuple-element.131, f32[12,512]{1,0:T(8,128)S(1)} %log_add_fusion, f32[12,512,1024]{2,1,0:T(8,128)} %get-tuple-element.124, pred[512,1024]{1,0:T(8,128)(4,1)} %iota_compare_fusion), kind=kLoop, calls=%fused_computation | loop fusion | flops 44040192 | bytes 63488000 | tf_op jit(solution)/shard_map/while/body/eval_jaxpr/convert_element_type | solution.py:134
  371.1 6.2 fusion.38
  377.3 4.0 fusion.31
  381.4 4.6 fusion.39
  387.9 12.8 %fusion.30 = bf16[1024,12,64]{0,2,1:T(8,128)(2,1)S(1)} fusion(f32[512,12,64]{0,2,1:T(8,128)S(1)} %copy-done.56, bf16[512,12,64]{0,2,1:T(8,128)(2,1)S(1)} %bitcast.94, f32[12,512]{1,0:T(8,128)S(1)} %log_add_fusion, f32[12,512,1024]{2,1,0:T(8,128)} %get-tuple-element.124, pred[512,1024]{1,0:T(8,128)(4,1)S(1)} %copy-done.13), kind=kOutput, calls=%fused_computation.57 | convolution fusion | flops 838336512 | bytes 29646848 | tf_op jit(solution)/shard_map/while/body/eval_jaxpr/hqk,qhd->khd/dot_general | solution.py:127
  400.7 1.1 copy-done.19
  401.8 7.0 fusion.63
  408.9 1.3 copy-done.8
  410.3 14.1 %fusion.40 = f32[3072,768]{1,0:T(8,128)} fusion(bf16[1024,768]{0,1:T(8,128)(2,1)S(1)} %copy-done.8, f32[1024]{0:T(1024)S(1)} %copy-done.32, f32[1024,3072]{1,0:T(8,128)} %fusion.68, f32[3072]{0:T(1024)S(1)} %copy-done.44), kind=kOutput, calls=%fused_computation.83 | convolution fusion | flops 4866441216 | bytes 23609344 | tf_op jit(solution)/shard_map/dot_general | solution.py:35
  425.1 10.7 %fusion.67 = f32[768,3072]{1,0:T(8,128)} fusion(bf16[1024,3072]{1,0:T(8,128)(2,1)} %copy-done.55, f32[1024,768]{0,1:T(8,128)} %get-tuple-element.128, f32[768]{0:T(1024)S(1)} %copy-done.25, f32[768]{0:T(1024)S(1)} %convert_element_type.144, f32[1024]{0:T(1024)S(1)} %fusion.47, f32[1024]{0:T(1024)S(1)} %broadcast_multiply_fusion), kind=kOutput, calls=%fused_computation.122 | convolution fusion | flops 4835770368 | bytes 18888704 | tf_op jit(solution)/shard_map/dot_general | solution.py:35
  436.5 12.4 %add_convert_fusion.2 = bf16[1024,768]{0,1:T(8,128)(2,1)} fusion(f32[1024,768]{0,1:T(8,128)} %get-tuple-element.128, bf16[3072,768]{1,0:T(8,128)(2,1)} %all-gather.11.cloned.1.call-done, f32[768]{0:T(1024)S(1)} %convert_element_type.149, f32[1024,3072]{1,0:T(8,128)} %fusion.68, f32[3072]{0:T(1024)S(1)} %copy-done.44), kind=kOutput, calls=%fused_computation.69 | convolution fusion | flops 4866441216 | bytes 22035456 | tf_op jit(solution)/shard_map/dot_general | solution.py:31
  448.8 2.6 copy.90
  451.4 9.2 %fusion.77 = (f32[768]{0:T(1024)S(1)}, f32[1024,768]{1,0:T(8,128)}) fusion(bf16[768,2304]{1,0:T(8,128)(2,1)} %all-gather.5.cloned.1.call-done, bf16[1024,768]{0,1:T(8,128)(2,1)} %bitcast.89, bf16[1024,768]{0,1:T(8,128)(2,1)} %bitcast.79, bf16[1024,768]{0,1:T(8,128)(2,1)} %bitcast.84), kind=kOutput, calls=%fused_computation.130 | convolution fusion | flops 3638820096 | bytes 11406336 | tf_op jit(solution)/shard_map/dot_general | solution.py:41
  460.7 3.6 copy.87
  464.3 3.1 convert_reduce_fusion.1
  468.2 1.3 fusion.26
  469.6 39.5 %all-reduce.18 = (f32[768]{0:T(1024)S(1)}, f32[768]{0:T(1024)S(1)}, f32[1536]{0:T(1024)S(1)}, f32[768]{0:T(1024)S(1)}, f32[768]{0:T(1024)S(1)}, /*index=5*/f32[7...) all-reduce(f32[768]{0:T(1024)S(1)} %get-tuple-element.88, ...), channel_id=2, replica_groups=mesh['wide'=8,'narrow'=4] {'wide','narrow'}, use_global_device_ids=true, to_apply=%region_15.16.clone | all-reduce | flops 9216 | bytes 73728
  512.6 5.6 add_convert_fusion.1
  518.2 2.6 copy.91
  521.9 17.1 %reduce-scatter.5.cloned.1.call-done = f32[24,2304]{1,0:T(8,128)} async-done(((f32[768,2304]{1,0:T(8,128)}), f32[24,2304]{1,0:T(8,128)}) %reduce-scatter.5.cloned.1.call-update) | async-done | bytes 221200 | tf_op jit(solution)/shard_map/reduce_scatter | solution.py:292
  539.1 141.1 %reduce-scatter.11.cloned.1.call-done = f32[96,768]{1,0:T(8,128)} async-done(((f32[3072,768]{1,0:T(8,128)}), f32[96,768]{1,0:T(8,128)}) %reduce-scatter.11.cloned.1.call-update) | async-done | bytes 294928 | tf_op jit(solution)/shard_map/reduce_scatter | solution.py:258
  680.2 142.0 %reduce-scatter.9.cloned.1.call-done = f32[24,3072]{1,0:T(8,128)} async-done(((f32[768,3072]{1,0:T(8,128)}), f32[24,3072]{1,0:T(8,128)}) %reduce-scatter.9.cloned.1.call-update) | async-done | bytes 294928 | tf_op jit(solution)/shard_map/reduce_scatter | solution.py:256
  (201 shorter events, 23.7 us)
Async XLA Ops:
  7.2 65.4 %all-gather.5.cloned.1.call-start = ((), (), s32[]{:S(2)}) async-start(), calls=%async_computation.4 | async-start | bytes 3649536 | tf_op jit(solution)/shard_map/all_gather | solution.py:185
  7.9 145.2 %all-gather.7.cloned.1.call-start = ((), (), s32[]{:S(2)}) async-start(), calls=%async_computation.5 | async-start | bytes 1216512 | tf_op jit(solution)/shard_map/all_gather | solution.py:187
  8.7 186.0 %all-gather.9.cloned.1.call-start = ((), (), s32[]{:S(2)}) async-start(), calls=%async_computation.6 | async-start | bytes 4866048 | tf_op jit(solution)/shard_map/all_gather | solution.py:216
  9.4 250.5 %all-gather.11.cloned.1.call-start = ((), (), s32[]{:S(2)}) async-start(), calls=%async_computation.7 | async-start | bytes 4866048 | tf_op jit(solution)/shard_map/all_gather | solution.py:218
  10.0 512.0 %reduce-scatter.7.cloned.1.call-start = ((), (), s32[]{:S(2)}) async-start(), calls=%async_computation.9 | async-start | bytes 2433024 | tf_op jit(solution)/shard_map/reduce_scatter | solution.py:294
  60.1 12.5 %copy-start.29 = (f32[768]{0:T(1024)}, f32[768]{0:T(1024)S(1)}, u32[]{:S(2)}) copy-start(f32[768]{0:T(1024)S(1)} %convert_element_type.133) | copy-start | bytes 9220
  60.1 12.5 %copy-start.46 = (f32[768]{0:T(1024)}, f32[768]{0:T(1024)S(1)}, u32[]{:S(2)}) copy-start(f32[768]{0:T(1024)S(1)} %convert_element_type.134) | copy-start | bytes 9220
  60.1 134.6 %copy-start.24 = (f32[768]{0:T(1024)}, f32[768]{0:T(1024)S(1)}, u32[]{:S(2)}) copy-start(f32[768]{0:T(1024)S(1)} %convert_element_type.145) | copy-start | bytes 9220
  63.6 89.5 %copy-start.2 = (bf16[1024,768]{0,1:T(8,128)(2,1)}, bf16[1024,768]{0,1:T(8,128)(2,1)S(1)}, u32[]{:S(2)}) copy-start(bf16[1024,768]{0,1:T(8,128)(2,1)S(1)} %copy.73) | copy-start | bytes 4718596
  63.9 15.0 %copy-start.27 = (f32[1024]{0:T(1024)}, f32[1024]{0:T(1024)S(1)}, u32[]{:S(2)}) copy-start(f32[1024]{0:T(1024)S(1)} %broadcast_multiply_fusion.1) | copy-start | bytes 12292
  65.0 14.0 %copy-start.33 = (f32[1024]{0:T(1024)}, f32[1024]{0:T(1024)S(1)}, u32[]{:S(2)}) copy-start(f32[1024]{0:T(1024)S(1)} %fusion.46) | copy-start | bytes 12292
  66.7 193.2 %copy-start.6 = (bf16[1024,768]{0,1:T(8,128)(2,1)}, bf16[1024,768]{0,1:T(8,128)(2,1)S(1)}, u32[]{:S(2)}) copy-start(bf16[1024,768]{0,1:T(8,128)(2,1)S(1)} %copy.82) | copy-start | bytes 4718596
  100.7 4.6 copy-start
  105.3 14.6 %copy-start.11 = (pred[512,1024]{1,0:T(8,128)(4,1)S(1)}, pred[512,1024]{1,0:T(8,128)(4,1)}, u32[]{:S(2)}) copy-start(pred[512,1024]{1,0:T(8,128)(4,1)} %iota_compare_fusion) | copy-start | bytes 1572868
  119.9 13.4 %copy-start.20 = (bf16[512,768]{0,1:T(8,128)(2,1)S(1)}, bf16[512,768]{0,1:T(8,128)(2,1)}, u32[]{:S(2)}) copy-start(bf16[512,768]{0,1:T(8,128)(2,1)} %copy.74) | copy-start | bytes 2359300
  119.9 21.6 %slice-start = ((s8[25165824]{0:T(1024)(128)(4,1)}), s8[4194304]{0:T(1024)(128)(4,1)S(1)}, s32[]{:S(2)}) async-start(s8[25165824]{0:T(1024)(128)(4,1)} %bitcast.68), calls=%async_computation.12 | async-start | bytes 8388608
  119.9 21.6 %slice-start.1 = ((s8[25165824]{0:T(1024)(128)(4,1)}), s8[4194304]{0:T(1024)(128)(4,1)S(1)}, s32[]{:S(2)}) async-start(s8[25165824]{0:T(1024)(128)(4,1)} %bitcast.68), calls=%async_computation.13 | async-start | bytes 8388608
  133.3 8.2 slice-start.2
  133.3 8.2 slice-start.3
  133.3 9.0 %slice-start.4 = ((s8[25165824]{0:T(1024)(128)(4,1)}), s8[4194304]{0:T(1024)(128)(4,1)S(1)}, s32[]{:S(2)}) async-start(s8[25165824]{0:T(1024)(128)(4,1)} %bitcast.68), calls=%async_computation.16 | async-start | bytes 8388608
  133.3 10.2 %slice-start.5 = ((s8[25165824]{0:T(1024)(128)(4,1)}), s8[4194304]{0:T(1024)(128)(4,1)S(1)}, s32[]{:S(2)}) async-start(s8[25165824]{0:T(1024)(128)(4,1)} %bitcast.68), calls=%async_computation.17 | async-start | bytes 8388608
  143.5 9.7 %copy-start.31 = (f32[1024]{0:T(1024)S(1)}, f32[1024]{0:T(1024)}, u32[]{:S(2)}) copy-start(f32[1024]{0:T(1024)} %fusion.45) | copy-start | bytes 12292
  143.5 9.7 %copy-start.48 = (f32[768]{0:T(1024)S(1)}, f32[768]{0:T(1024)}, u32[]{:S(2)}) copy-start(f32[768]{0:T(1024)} %convert_element_type.143) | copy-start | bytes 9220
  161.7 98.2 %copy-start.32 = (f32[1024]{0:T(1024)S(1)}, f32[1024]{0:T(1024)}, u32[]{:S(2)}) copy-start(f32[1024]{0:T(1024)} %fusion.45) | copy-start | bytes 12292
  161.7 98.2 %copy-start.44 = (f32[3072]{0:T(1024)S(1)}, f32[3072]{0:T(1024)}, u32[]{:S(2)}) copy-start(f32[3072]{0:T(1024)} %convert_element_type.147) | copy-start | bytes 36868
  259.9 18.6 %copy-start.16 = (bf16[768,3072]{1,0:T(8,128)(2,1)S(1)}, bf16[768,3072]{1,0:T(8,128)(2,1)}, u32[]{:S(2)}) copy-start(bf16[768,3072]{1,0:T(8,128)(2,1)} %all-gather.9.cloned.1.call-done) | copy-start | bytes 14155780
  278.5 7.3 copy-start.55
  288.4 3.4 copy-start.40
  291.8 2.9 copy-start.7
  294.7 1.7 copy-start.5
  294.7 1.7 copy-start.35
  294.7 2.5 copy-start.53
  294.7 3.0 copy-start.54
  297.7 2.9 copy-start.51
  297.7 2.9 copy-start.52
  300.6 1.5 copy-start.26
  300.6 9.4 %slice-start.6 = ((s8[12582912]{0:T(1024)(128)(4,1)}), s8[4194304]{0:T(1024)(128)(4,1)S(1)}, s32[]{:S(2)}) async-start(s8[12582912]{0:T(1024)(128)(4,1)} %bitcast.70), calls=%async_computation.18 | async-start | bytes 8388608
  302.0 8.0 slice-start.7
  302.1 28.7 %copy-start.22 = (bf16[512,768]{0,1:T(8,128)(2,1)}, bf16[512,768]{0,1:T(8,128)(2,1)S(1)}, u32[]{:S(2)}) copy-start(bf16[512,768]{0,1:T(8,128)(2,1)S(1)} %get-tuple-element.117) | copy-start | bytes 2359300
  302.1 7.9 slice-start.8
  302.1 7.9 copy-start.21
  317.1 222.0 %reduce-scatter.5.cloned.1.call-start = ((), (), s32[]{:S(2)}) async-start(), calls=%async_computation.8 | async-start | bytes 7299072 | tf_op jit(solution)/shard_map/reduce_scatter | solution.py:292
  317.1 10.2 %copy-start.14 = (bf16[512,768]{0,1:T(8,128)(2,1)S(1)}, bf16[512,768]{0,1:T(8,128)(2,1)}, u32[]{:S(2)}) copy-start(bf16[512,768]{0,1:T(8,128)(2,1)} %copy.75) | copy-start | bytes 2359300
  327.4 3.4 copy-start.1
  327.4 3.4 copy-start.12
  327.4 3.4 copy-start.18
  377.3 4.0 copy-start.9
  381.3 19.3 %copy-start.10 = (bf16[1024,12,64]{0,2,1:T(8,128)(2,1)}, bf16[1024,12,64]{0,2,1:T(8,128)(2,1)S(1)}, u32[]{:S(2)}) copy-start(bf16[1024,12,64]{0,2,1:T(8,128)(2,1)S(1)} %fusion.31) | copy-start | bytes 4718596
  381.4 4.6 copy-start.17
  386.0 1.8 copy-start.56
  387.8 12.8 %copy-start.15 = (bf16[1024,12,64]{0,2,1:T(8,128)(2,1)}, bf16[1024,12,64]{0,2,1:T(8,128)(2,1)S(1)}, u32[]{:S(2)}) copy-start(bf16[1024,12,64]{0,2,1:T(8,128)(2,1)S(1)} %pad_maximum_fusion.1) | copy-start | bytes 4718596
  387.8 14.0 %copy-start.3 = (bf16[1024,768]{0,1:T(8,128)(2,1)S(1)}, bf16[1024,768]{0,1:T(8,128)(2,1)}, u32[]{:S(2)}) copy-start(bf16[1024,768]{0,1:T(8,128)(2,1)} %copy-done.2) | copy-start | bytes 4718596
  387.8 14.0 %copy-start.28 = (f32[1024]{0:T(1024)S(1)}, f32[1024]{0:T(1024)}, u32[]{:S(2)}) copy-start(f32[1024]{0:T(1024)} %copy-done.27) | copy-start | bytes 12292
  387.8 14.0 %copy-start.30 = (f32[768]{0:T(1024)S(1)}, f32[768]{0:T(1024)}, u32[]{:S(2)}) copy-start(f32[768]{0:T(1024)} %copy-done.29) | copy-start | bytes 9220
  387.8 14.0 %copy-start.34 = (f32[1024]{0:T(1024)S(1)}, f32[1024]{0:T(1024)}, u32[]{:S(2)}) copy-start(f32[1024]{0:T(1024)} %copy-done.33) | copy-start | bytes 12292
  387.8 14.0 %copy-start.47 = (f32[768]{0:T(1024)S(1)}, f32[768]{0:T(1024)}, u32[]{:S(2)}) copy-start(f32[768]{0:T(1024)} %copy-done.46) | copy-start | bytes 9220
  408.9 1.4 copy-start.8
  408.9 271.3 %reduce-scatter.11.cloned.1.call-start = ((), (), s32[]{:S(2)}) async-start(), calls=%async_computation.11 | async-start | bytes 9732096 | tf_op jit(solution)/shard_map/reduce_scatter | solution.py:258
  424.4 397.8 %reduce-scatter.9.cloned.1.call-start = ((), (), s32[]{:S(2)}) async-start(), calls=%async_computation.10 | async-start | bytes 9732096 | tf_op jit(solution)/shard_map/reduce_scatter | solution.py:256
  464.3 3.3 copy-start.4
  468.1 1.4 copy-start.41
  468.2 1.4 copy-start.42
  468.2 1.4 copy-start.43
  468.2 44.4 %copy-start.36 = (f32[1024]{0:T(1024)S(1)}, f32[1024]{0:T(1024)}, u32[]{:S(2)}) copy-start(f32[1024]{0:T(1024)} %copy-done.35) | copy-start | bytes 12292
  (10 other events, 9.7 us)
Sparse Core Ops, SparseCore 0:
  10.9 61.5 all-gather.4
  75.5 52.3 all-gather.6
  130.8 63.8 all-gather.8
  197.5 62.3 all-gather.10
  317.2 95.1 reduce-scatter.6
  419.4 119.5 reduce-scatter.4
  545.5 134.6 reduce-scatter.10
  687.7 134.4 reduce-scatter.8
where the time goes:
time: 840 us; the launch traced here: 829 us
  waiting for transfers between devices  396 us (47%)
  matrix products  210 us (25%)
  blocking collectives  80.3 us (10%)
  other arithmetic  70.2 us (8%)
  local copies, waits for them, and re-layouts  56.5 us (7%)
  between operations  15.9 us (2%)
    reduce_scatter x1, waiting for transfers between devices, local(): lax.psum_scatter(fc_weight_term, ('wide', 'narrow'), scatter_dimension=0,...  142 us
    reduce_scatter x1, waiting for transfers between devices, local(): lax.psum_scatter(proj_weight_term, ('wide', 'narrow'), scatter_dimension=...  141 us
    unnamed x2, blocking collectives  80.3 us
    all_gather x1, waiting for transfers between devices, local(): lax.all_gather(proj_weight, ('wide', 'narrow'), axis=0, tiled=True)  54.2 us
    dot_general x4, matrix products, right_product(): lax.dot_general(left, right, (((1,), (1,)), ((), ())), preferred_element_...  36.6 us
    dot_general x4, matrix products, product(): return jnp.dot(left, right, preferred_element_type=jnp.float32)  35.3 us
    dot_general x4, matrix products, left_product(): lax.dot_general(left, right, (((0,), (0,)), ((), ())), preferred_element_...  34.7 us
    all_gather x1, waiting for transfers between devices, local(): lax.all_gather(fc_weight, ('wide', 'narrow'), axis=0, tiled=True)  33 us
  transfers between devices with their start and end apart: 8, of which 6 were waited for; matrix products, arithmetic and copies ran while one was open for 32% of the time, Pallas kernels for 0%

commit v1 on v0

v1 whole, which is shorter than its diff:
```python
import functools
import math

import jax
import jax.numpy as jnp
import numpy as np
from jax import lax
from jax.experimental import pallas as pl
from jax.experimental.pallas import tpu as pltpu
from jax.sharding import PartitionSpec as P

AXES = ("wide", "narrow")
BF, F32 = jnp.bfloat16, jnp.float32
VMEM_CAP = 58 << 20
LOG2E = 1.4426950408889634

def params(n=1, cap=VMEM_CAP):
    return pltpu.CompilerParams(dimension_semantics=("arbitrary",) * n, vmem_limit_bytes=cap)

def cost(flops, bytes_accessed, trans=0):
    return pl.CostEstimate(flops=int(flops), bytes_accessed=int(bytes_accessed), transcendentals=int(trans))

def mm(a, b):
    return jnp.dot(a, b, preferred_element_type=F32)

def diagonal_mask(rows, cols):
    key_at = lax.broadcasted_iota(jnp.int32, (rows, cols), 0)
    query_at = lax.broadcasted_iota(jnp.int32, (rows, cols), 1)
    return key_at <= query_at

def attend_kernel(qb, len_ref, qkv_ref, out_t_ref, out_ref, stat_ref, v_t, q_t):
    slot = qkv_ref.shape[1]
    q_t[...] = (qkv_ref[0] * jnp.asarray(0.125, BF)).T
    v_t[...] = qkv_ref[2].T
    half = lax.broadcasted_iota(jnp.int32, (128, 1), 0) < 64
    causal = diagonal_mask(qb, qb)
    length = len_ref[0]
    for i in range(slot // qb):
        cols = slice(i * qb, (i + 1) * qb)
        parts = []
        for head in range(2):
            mine = half if head == 0 else jnp.logical_not(half)
            qh = jnp.where(mine, q_t[:, cols], jnp.zeros((), BF))
            s_low = mm(qkv_ref[1, : i * qb, :], qh) if i else None
            s_dia = jnp.where(causal, mm(qkv_ref[1, cols, :], qh), -1e30)
            top = jnp.max(s_dia, axis=0, keepdims=True)
            if i:
                top = jnp.maximum(top, jnp.max(s_low, axis=0, keepdims=True))
            e_dia = jnp.exp(s_dia - top)
            total = jnp.sum(e_dia, axis=0, keepdims=True)
            vh = v_t[head * 64 : head * 64 + 64, :]
            acc = mm(vh[:, cols], e_dia.astype(BF))
            if i:
                e_low = jnp.exp(s_low - top)
                total = total + jnp.sum(e_low, axis=0, keepdims=True)
                acc = acc + mm(vh[:, : i * qb], e_low.astype(BF))
            stat_ref[0, head : head + 1, cols] = top + jnp.log(total)
            parts.append(acc / total)
        both = jnp.concatenate(parts, axis=0)
        seen = (i * qb + lax.broadcasted_iota(jnp.int32, (1, qb), 1)) < length
        both = jnp.where(seen, both, 0.0)
        out_t_ref[:, cols] = both
        out_ref[cols, :] = both.T.astype(BF)

def attend(lengths, qkv, pairs, first, qb=256):
    slot, width = qkv.shape[1], qkv.shape[2]
    return pl.pallas_call(
        functools.partial(attend_kernel, qb),
        name="attend",
        grid=(pairs,),
        in_specs=[
            pl.BlockSpec(memory_space=pltpu.SMEM),
            pl.BlockSpec((3, slot, 128), lambda j: (0, 0, j + first)),
        ],
        out_specs=[
            pl.BlockSpec((128, slot), lambda j: (j, 0)),
            pl.BlockSpec((slot, 128), lambda j: (0, j)),
            pl.BlockSpec((1, 2, slot), lambda j: (j, 0, 0)),
        ],
        out_shape=[
            jax.ShapeDtypeStruct((pairs * 128, slot), F32),
            jax.ShapeDtypeStruct((slot, pairs * 128), BF),
            jax.ShapeDtypeStruct((pairs, 2, slot), F32),
        ],
        scratch_shapes=[pltpu.VMEM((128, slot), BF), pltpu.VMEM((128, slot), BF)],
        compiler_params=params(),
        cost_estimate=cost(pairs * 2 * slot * slot * 256, 8e6 * pairs / 6, pairs * slot * slot),
    )(lengths, qkv)

def attend_grad_kernel(qb, qkv_ref, grad_ref, out_t_ref, stat_ref, g_ref, q_t, do_t, k_t, qs, dq_t, dk_s, dv_s):
    slot = qkv_ref.shape[1]
    qs[...] = qkv_ref[0] * jnp.asarray(0.125, BF)
    q_t[...] = qs[...].T
    k_t[...] = qkv_ref[1].T
    do_t[...] = grad_ref[...].T
    half = lax.broadcasted_iota(jnp.int32, (128, 1), 0) < 64
    half_lane = lax.broadcasted_iota(jnp.int32, (1, 128), 1) < 64
    causal = diagonal_mask(qb, qb)
    zero = jnp.zeros((), BF)
    prod = do_t[...].astype(F32) * out_t_ref[...]
    delta = [jnp.sum(prod[h * 64 : h * 64 + 64], axis=0, keepdims=True) for h in range(2)]
    for i in range(slot // qb):
        cols = slice(i * qb, (i + 1) * qb)
        end = (i + 1) * qb
        dv_new = dk_new = None
        for head in range(2):
            mine = half if head == 0 else jnp.logical_not(half)
            mine_lane = half_lane if head == 0 else jnp.logical_not(half_lane)
            qh_t = jnp.where(mine, q_t[:, cols], zero)
            doh_t = jnp.where(mine, do_t[:, cols], zero)
            qh = jnp.where(mine_lane, qs[cols, :], zero)
            doh = jnp.where(mine_lane, grad_ref[cols, :], zero)
            stat = stat_ref[0, head : head + 1, cols]
            dl = delta[head][:, cols]
            s = mm(qkv_ref[1, :end, :], qh_t)
            dp = mm(qkv_ref[2, :end, :], doh_t)
            p = jnp.exp(s - stat)
            p_dia = jnp.where(causal, p[i * qb :], 0.0)
            p = jnp.concatenate([p[: i * qb], p_dia], axis=0) if i else p_dia
            ds = (p * (dp - dl)).astype(BF)
            pb = p.astype(BF)
            dv_h = mm(pb, doh)
            dk_h = mm(ds, qh)
            dv_new = dv_h if head == 0 else dv_new + dv_h
            dk_new = dk_h if head == 0 else dk_new + dk_h
            dq_t[head * 64 : head * 64 + 64, cols] = mm(k_t[head * 64 : head * 64 + 64, :end], ds)
        if i:
            dv_s[: i * qb] += dv_new[: i * qb]
            dk_s[: i * qb] += dk_new[: i * qb]
        dv_s[cols] = dv_new[i * qb :]
        dk_s[cols] = dk_new[i * qb :]
    g_ref[0] = (dq_t[...] * 0.125).T.astype(BF)
    g_ref[1] = dk_s[...].astype(BF)
    g_ref[2] = dv_s[...].astype(BF)

def attend_grad(qkv, grad, out_t, stat, qb=256):
    slot, width = qkv.shape[1], qkv.shape[2]
    pairs = width // 128
    return pl.pallas_call(
        functools.partial(attend_grad_kernel, qb),
        name="attend_grad",
        grid=(pairs,),
        in_specs=[
            pl.BlockSpec((3, slot, 128), lambda j: (0, 0, j)),
            pl.BlockSpec((slot, 128), lambda j: (0, j)),
            pl.BlockSpec((128, slot), lambda j: (j, 0)),
            pl.BlockSpec((1, 2, slot), lambda j: (j, 0, 0)),
        ],
        out_specs=pl.BlockSpec((3, slot, 128), lambda j: (0, 0, j)),
        out_shape=jax.ShapeDtypeStruct((3, slot, width), BF),
        scratch_shapes=[
            pltpu.VMEM((128, slot), BF),
            pltpu.VMEM((128, slot), BF),
            pltpu.VMEM((128, slot), BF),
            pltpu.VMEM((slot, 128), BF),
            pltpu.VMEM((128, slot), F32),
            pltpu.VMEM((slot, 128), F32),
            pltpu.VMEM((slot, 128), F32),
        ],
        compiler_params=params(),
        cost_estimate=cost(pairs * 5 * slot * slot * 256, 16e6, pairs * 2 * slot * slot),
    )(qkv, grad, out_t, stat)
branch_scale = 1.0 / math.sqrt(48.0)
norm_epsilon = 1e-05
WHOLE = dict(pipeline_mode=pl.Buffered(1))

def mm_nt(a, b):
    return lax.dot_general(a, b, (((1,), (1,)), ((), ())), preferred_element_type=F32)

def mm_tn(a, b):
    return lax.dot_general(a, b, (((0,), (0,)), ((), ())), preferred_element_type=F32)

def normalised(v):
    mean = jnp.mean(v, axis=-1, keepdims=True)
    centred = v - mean
    var = jnp.mean(centred * centred, axis=-1, keepdims=True)
    scale = lax.rsqrt(var + norm_epsilon)
    return centred * scale, scale

def norm_pull(n, scale, gain, u):
    ug = u * gain
    a = jnp.mean(ug, axis=-1, keepdims=True)
    b = jnp.mean(ug * n, axis=-1, keepdims=True)
    return (ug - a - n * b) * scale

def whole(shape, index=None):
    zeros = (0,) * len(shape)
    return pl.BlockSpec(shape, (lambda *_: index or zeros), **WHOLE)

def assemble(place, sources, target, at=0):
    wide = sources[0].shape[2]
    for s, source in enumerate(sources):
        for half in range(2):
            @pl.when(place[s, 0] == half)
            def _():
                for p in range(source.shape[0]):
                    target[place[s, 1 + p], :, half * wide : (half + 1) * wide] = source[p]

def assemble_chunks(place, sources, target):
    wide = sources[0].shape[2] // 4
    for s, source in enumerate(sources):
        for half in range(2):
            @pl.when(place[s, 0] == half)
            def _():
                for p in range(source.shape[0]):
                    for j in range(4):
                        target[place[s, 1 + p], j, :, half * wide : (half + 1) * wide] = source[p, :, j * wide : (j + 1) * wide]

def project_kernel(n_src, place, x_ref, gain_ref, shift_ref, bias_ref, *rest):
    sources, (qkv_ref, low_ref, w_ref) = rest[:n_src], rest[n_src:]
    @pl.when(pl.program_id(0) == 0)
    def _():
        assemble(place, sources, w_ref)
    n, _ = normalised(x_ref[...].astype(F32))
    low = (n * gain_ref[...] + shift_ref[...]).astype(BF)
    low_ref[...] = low
    d = low.shape[1]
    for part in range(3):
        w = w_ref[:, :, part * d : (part + 1) * d].reshape(d, d)
        qkv_ref[part] = (mm(low, w) + bias_ref[part : part + 1]).astype(BF)

def project(place, x, gain, shift, bias, sources, blocks, rows=256):
    t, d = x.shape
    r, wide = d // blocks, sources[0].shape[2]
    return pl.pallas_call(
        functools.partial(project_kernel, len(sources)),
        name="project",
        grid_spec=pltpu.PrefetchScalarGridSpec(
            num_scalar_prefetch=1,
            grid=(t // rows,),
            in_specs=[
                pl.BlockSpec((rows, d), lambda i, p: (i, 0)),
                whole((1, d)), whole((1, d)), whole((3, d)),
                *[whole(s.shape) for s in sources],
            ],
            out_specs=[
                pl.BlockSpec((3, rows, d), lambda i, p: (0, i, 0)),
                pl.BlockSpec((rows, d), lambda i, p: (i, 0)),
                whole((blocks, r, 2 * wide)),
            ],
        ),
        out_shape=[
            jax.ShapeDtypeStruct((3, t, d), BF),
            jax.ShapeDtypeStruct((t, d), BF),
            jax.ShapeDtypeStruct((blocks, r, 2 * wide), BF),
        ],
        compiler_params=params(),
        cost_estimate=cost(2 * t * d * 3 * d, 18e6),
    )(place, x, gain, shift, bias, *sources)

def mix_kernel(n_src, place, attn_ref, x_ref, bias_ref, gain_ref, shift_ref, *rest):
    sources, (mid_ref, low_ref, w_ref) = rest[:n_src], rest[n_src:]
    @pl.when(pl.program_id(0) == 0)
    def _():
        assemble(place, sources, w_ref)
    d = x_ref.shape[1]
    w = w_ref[...].reshape(d, d)
    mid = x_ref[...].astype(F32) + branch_scale * (mm(attn_ref[...], w) + bias_ref[...])
    mid_ref[...] = mid
    n, _ = normalised(mid)
    low_ref[...] = (n * gain_ref[...] + shift_ref[...]).astype(BF)

def mix(place, attn, x, bias, gain, shift, sources, blocks, column, rows=256):
    t, d = x.shape
    r, np_ = d // blocks, sources[0].shape[0]
    return pl.pallas_call(
        functools.partial(mix_kernel, len(sources)),
        name="mix",
        grid_spec=pltpu.PrefetchScalarGridSpec(
            num_scalar_prefetch=1,
            grid=(t // rows,),
            in_specs=[
                pl.BlockSpec((rows, d), lambda i, p: (i, 0)),
                pl.BlockSpec((rows, d), lambda i, p: (i, 0)),
                whole((1, d)), whole((1, d)), whole((1, d)),
                *[whole((np_, r, d // 2), (0, 0, column)) for s in sources],
            ],
            out_specs=[
                pl.BlockSpec((rows, d), lambda i, p: (i, 0)),
                pl.BlockSpec((rows, d), lambda i, p: (i, 0)),
                whole((blocks, r, d)),
            ],
        ),
        out_shape=[
            jax.ShapeDtypeStruct((t, d), F32),
            jax.ShapeDtypeStruct((t, d), BF),
            jax.ShapeDtypeStruct((blocks, r, d), BF),
        ],
        compiler_params=params(),
        cost_estimate=cost(2 * t * d * d, 9e6),
    )(place, attn, x, bias, gain, shift, *sources)

def mlp_kernel(n_src, blocks, rb, core, place, lens, mid_ref, low_ref, cot_ref, fb_ref, pb_ref, gain_ref, *rest):
    fcs, projs, rest = rest[:n_src], rest[n_src : 2 * n_src], rest[2 * n_src :]
    (out_ref, gmid_ref, gbr_ref, fsend_ref, fkeep_ref, psend_ref, pkeep_ref, fbg_ref, vec_ref,
     fc_s, proj_s, low_t, g2_s, second_s, gh_s, act_s, gpre_s) = rest
    t, d = mid_ref.shape
    r = d // blocks
    step = pl.program_id(0)
    mine = core[0]
    chunk = lax.rem(step + 2 * (1 - mine), 4)
    def valid_rows(at):
        return (at * rb + lax.broadcasted_iota(jnp.int32, (rb, 1), 0)) < lens[0]
    @pl.when(step == 0)
    def _():
        assemble(place, fcs, fc_s)
        assemble_chunks(place, projs, proj_s)
        low_t[...] = low_ref[...].T
        def begin(i, total):
            at = pl.ds(pl.multiple_of(i * rb, rb), rb)
            g = jnp.where(valid_rows(i), branch_scale * cot_ref[at, :].astype(F32), 0.0).astype(BF)
            g2_s[at, :] = g
            second_s[at, :] = jnp.zeros((rb, d), F32)
            gh_s[at, :] = jnp.zeros((rb, d), F32)
            return total + jnp.sum(g.astype(F32), axis=0, keepdims=True)
        vec_ref[0:1] = lax.fori_loop(0, t // rb, begin, jnp.zeros((1, d), F32))
    fcol = pl.ds(pl.multiple_of(chunk * d, d), d)
    fc = fc_s.at[:, :, fcol]
    bias = fb_ref[pl.ds(chunk, 1), :]
    if blocks % 4 == 0:
        per = blocks // 4
        proj = proj_s.at[pl.ds(chunk * per, per)]
    else:
        proj = proj_s.at[:, pl.ds(chunk, 1)]
    def rows_step(i, total):
        at = pl.ds(pl.multiple_of(i * rb, rb), rb)
        u = mm(low_ref[at, :], fc[...].reshape(d, d)) + bias
        sq = u * u
        th = jnp.tanh(0.7978845608028654 * u * (1.0 + 0.044715 * sq))
        up = 0.5 * (1.0 + th)
        act = (u * up).astype(BF)
        act_s[at, :] = act
        slope = up + u * (0.5 * 0.7978845608028654) * (1.0 - th * th) * (1.0 + 3 * 0.044715 * sq)
        w = proj[...].reshape(d, d)
        second_s[at, :] += mm(act, w)
        gp = mm_nt(g2_s[at, :], w) * slope
        gpb = gp.astype(BF)
        gpre_s[at, :] = gpb
        gh_s[at, :] += mm_nt(gpb, fc[...].reshape(d, d))
        return total + jnp.sum(gpb.astype(F32), axis=0, keepdims=True)
    fbg_ref[pl.ds(chunk, 1), :] = lax.fori_loop(0, t // rb, rows_step, jnp.zeros((1, d), F32))
    dfc = mm(low_t[...], gpre_s[...]).astype(BF).reshape(blocks, r, d)
    @pl.when(step < 2)
    def _():
        fsend_ref[...] = dfc
    @pl.when(step >= 2)
    def _():
        fkeep_ref[...] = dfc
    dproj = mm_tn(act_s[...], g2_s[...]).astype(BF)
    h = d // 2
    for half in range(2):
        @pl.when(mine == half)
        def _():
            for ref, cols in ((pkeep_ref, half), (psend_ref, 1 - half)):
                piece = dproj[:, cols * h : (cols + 1) * h]
                if blocks % 4 == 0:
                    for b in range(blocks // 4):
                        for j in range(4):
                            ref[b, :, j * h : (j + 1) * h] = piece[(b * 4 + j) * r : (b * 4 + j + 1) * r]
                else:
                    ref[0] = piece
    @pl.when(step == 3)
    def _():
        def finish(i, carry):
            at = pl.ds(pl.multiple_of(i * rb, rb), rb)
            mid = mid_ref[at, :]
            out_ref[at, :] = (mid + branch_scale * (second_s[at, :] + pb_ref[...])).astype(BF)
            n, scale = normalised(mid)
            gh = gh_s[at, :]
            cot = jnp.where(valid_rows(i), cot_ref[at, :].astype(F32), 0.0)
            gm = cot + norm_pull(n, scale, gain_ref[...], gh)
            gmid_ref[at, :] = gm
            gb = (branch_scale * gm).astype(BF)
            gbr_ref[at, :] = gb
            return (carry[0] + jnp.sum(gh * n, axis=0, keepdims=True),
                    carry[1] + jnp.sum(gh, axis=0, keepdims=True),
                    carry[2] + jnp.sum(gb.astype(F32), axis=0, keepdims=True))
        zero = jnp.zeros((1, d), F32)
        a, b, c = lax.fori_loop(0, t // rb, finish, (zero, zero, zero))
        vec_ref[1:2] = a
        vec_ref[2:3] = b
        vec_ref[3:4] = c

def mlp(core, place, lens, mid, low, cot, fb, pb, gain, fcs, projs, blocks, rb=256):
    t, d = mid.shape
    r, np_ = d // blocks, fcs[0][0].shape[0]
    smem = pl.BlockSpec(memory_space=pltpu.SMEM)
    if blocks % 4 == 0:
        pspec = pl.BlockSpec((blocks // 4, r, 2 * d), lambda i, c: (lax.rem(i + 2 * (1 - c[0]), 4), 0, 0))
    else:
        pspec = pl.BlockSpec((1, r, d // 2), lambda i, c: (0, 0, lax.rem(i + 2 * (1 - c[0]), 4)))
    big = jax.ShapeDtypeStruct((blocks, r, 2 * d), BF)
    return pl.pallas_call(
        functools.partial(mlp_kernel, len(fcs), blocks, rb),
        name="mlp",
        grid_spec=pltpu.PrefetchScalarGridSpec(
            num_scalar_prefetch=1,
            grid=(4,),
            in_specs=[
                smem, smem, whole((t, d)), whole((t, d)), whole((t, d)), whole((4, d)), whole((1, d)), whole((1, d)),
                *[whole((np_, r, 2 * d), (0, 0, at)) for _, at in fcs],
                *[whole((np_, r, 2 * d), (0, 0, at)) for _, at in projs],
            ],
            out_specs=[
                whole((t, d)), whole((t, d)), whole((t, d)),
                pl.BlockSpec((blocks, r, d), lambda i, c: (0, 0, jnp.minimum(i, 1))),
                pl.BlockSpec((blocks, r, d), lambda i, c: (0, 0, jnp.maximum(i - 2, 0))),
                pspec, pspec,
                whole((4, d)), whole((4, d)),
            ],
            scratch_shapes=[
                pltpu.VMEM((blocks, r, 4 * d), BF),
                pltpu.VMEM((blocks, 4, r, d), BF),
                pltpu.VMEM((d, t), BF),
                pltpu.VMEM((t, d), BF),
                pltpu.VMEM((t, d), F32),
                pltpu.VMEM((t, d), F32),
                pltpu.VMEM((t, d), BF),
                pltpu.VMEM((t, d), BF),
            ],
        ),
        out_shape=[
            jax.ShapeDtypeStruct((t, d), BF), jax.ShapeDtypeStruct((t, d), F32), jax.ShapeDtypeStruct((t, d), BF),
            big, big, big, big,
            jax.ShapeDtypeStruct((4, d), F32), jax.ShapeDtypeStruct((4, d), F32),
        ],
        compiler_params=params(),
        cost_estimate=cost(12 * t * d * 4 * d, 40e6, t * 4 * d),
    )(core, place, lens, mid, low, cot, fb, pb, gain, *[a for a, _ in fcs], *[a for a, _ in projs])

def unmix_kernel(blocks, core, lens, gbr_ref, attn_ref, w_ref, ga_ref, send_ref, keep_ref):
    t, d = gbr_ref.shape
    w = w_ref[...].reshape(d, d)
    seen = lax.broadcasted_iota(jnp.int32, (t, 1), 0) < lens[0]
    ga_ref[...] = jnp.where(seen, mm_nt(gbr_ref[...], w), 0.0).astype(BF)
    dw = mm_tn(attn_ref[...], gbr_ref[...]).astype(BF)
    h = d // 2
    for half in range(2):
        @pl.when(core[0] == half)
        def _():
            keep_ref[...] = dw[:, half * h : (half + 1) * h].reshape(keep_ref.shape)
            send_ref[...] = dw[:, (1 - half) * h : (2 - half) * h].reshape(send_ref.shape)

def unmix(core, lens, gbr, attn, w, blocks):
    t, d = gbr.shape
    smem = pl.BlockSpec(memory_space=pltpu.SMEM)
    piece = jax.ShapeDtypeStruct((blocks, d // blocks, d // 2), BF)
    return pl.pallas_call(
        functools.partial(unmix_kernel, blocks),
        name="unmix",
        in_specs=[smem, smem] + [pl.BlockSpec(memory_space=pltpu.VMEM)] * 3,
        out_shape=[jax.ShapeDtypeStruct((t, d), BF), piece, piece],
        compiler_params=params(0),
        cost_estimate=cost(4 * t * d * d, 9e6),
    )(core, lens, gbr, attn, w)

def unproject_kernel(blocks, core, low_ref, g_ref, send_ref, keep_ref, sums_ref):
    d = low_ref.shape[1]
    r = d // blocks
    low_t = low_ref[...].T
    q = mm(low_t, g_ref[0]).astype(BF).reshape(blocks, r, d)
    v = mm(low_t, g_ref[2]).astype(BF).reshape(blocks, r, d)
    k = mm(low_t, g_ref[1]).astype(BF).reshape(blocks, r, d)
    h = d // 2
    for half, refs in ((0, (keep_ref, send_ref)), (1, (send_ref, keep_ref))):
        @pl.when(core[0] == half)
        def _():
            refs[0][:, :, :d] = q
            refs[0][:, :, d:] = k[:, :, :h]
            refs[1][:, :, :h] = k[:, :, h:]
            refs[1][:, :, h:] = v
    for part in range(3):
        sums_ref[part : part + 1] = jnp.sum(g_ref[part].astype(F32), axis=0, keepdims=True)

def unproject(core, low, g, blocks):
    t, d = low.shape
    piece = jax.ShapeDtypeStruct((blocks, d // blocks, d // 2 * 3), BF)
    return pl.pallas_call(
        functools.partial(unproject_kernel, blocks),
        name="unproject",
        in_specs=[pl.BlockSpec(memory_space=pltpu.SMEM)] + [pl.BlockSpec(memory_space=pltpu.VMEM)] * 2,
        out_shape=[piece, piece, jax.ShapeDtypeStruct((3, d), F32)],
        compiler_params=params(0),
        cost_estimate=cost(6 * t * d * d, 10e6),
    )(core, low, g)

def final_kernel(x_ref, g_ref, w_ref, gmid_ref, gain_ref, out_ref, vec_ref):
    d = x_ref.shape[1]
    w = w_ref[...].reshape(d, 3 * d)
    gh = mm_nt(g_ref[0], w[:, :d]) + mm_nt(g_ref[1], w[:, d : 2 * d]) + mm_nt(g_ref[2], w[:, 2 * d :])
    n, scale = normalised(x_ref[...].astype(F32))
    out_ref[...] = (gmid_ref[...] + norm_pull(n, scale, gain_ref[...], gh)).astype(BF)
    @pl.when(pl.program_id(0) == 0)
    def _():
        vec_ref[...] = jnp.zeros_like(vec_ref)
    vec_ref[0:1] += jnp.sum(gh * n, axis=0, keepdims=True)
    vec_ref[1:2] += jnp.sum(gh, axis=0, keepdims=True)

def final(x, g, w, gmid, gain, rows=256):
    t, d = x.shape
    return pl.pallas_call(
        final_kernel,
        name="final",
        grid=(t // rows,),
        in_specs=[
            pl.BlockSpec((rows, d), lambda i: (i, 0)),
            pl.BlockSpec((3, rows, d), lambda i: (0, i, 0)),
            whole(w.shape),
            pl.BlockSpec((rows, d), lambda i: (i, 0)),
            whole((1, d)),
        ],
        out_specs=[pl.BlockSpec((rows, d), lambda i: (i, 0)), whole((2, d))],
        out_shape=[jax.ShapeDtypeStruct((t, d), BF), jax.ShapeDtypeStruct((2, d), F32)],
        compiler_params=params(),
        cost_estimate=cost(6 * t * d * d, 15e6),
    )(x, g, w, gmid, gain)


class Grid:
    def __init__(self, mesh, rows):
        wide, narrow = mesh.shape["wide"], mesh.shape["narrow"]
        self.count = wide * narrow
        self.paired = narrow == 4 and wide % 2 == 0 and rows % 8 == 0
        self.blocks = self.count // 2 if self.paired else 1
        self.z = wide // 2

    def index(self, z, x, y, c):
        return ((z * 2 + x) * 2 + y) * 2 + c

    def places(self):
        return [
            (z, x, y, c) for z in range(self.z) for x in range(2) for y in range(2) for c in range(2)
        ]

    def perm(self, target):
        return [(self.index(*at), self.index(*target(*at))) for at in self.places()]

    def here(self):
        w, n = lax.axis_index("wide"), lax.axis_index("narrow")
        return w // 2, w % 2, n // 2, n % 2

    def table(self):
        rows = []
        for z0, x0, y0, c0 in self.places():
            mine = []
            for half in (c0, 1 - c0):
                for kb in range(2):
                    line = [half]
                    for ka in range(2):
                        for kz in range(self.z):
                            kx, ky = (ka, kb) if half == 0 else (kb, ka)
                            line.append((((z0 - kz) % self.z) * 2 + (x0 ^ kx)) * 2 + (y0 ^ ky))
                    mine.append(line)
            rows.append(mine)
        return np.array(rows, np.int32)

    def send(self, value, target):
        return lax.ppermute(value, AXES, self.perm(target))

    def other_core(self, value):
        return self.send(value, lambda z, x, y, c: (z, x, y, 1 - c))

    def along(self, value, turn):
        return self.send(
            value,
            lambda z, x, y, c: (z, 1 - x, y, c) if c == turn else (z, x, 1 - y, c),
        )

    def up(self, value, k):
        return self.send(value, lambda z, x, y, c: ((z + k) % self.z, x, y, c))


def both(first, own, other, axis):
    return jnp.where(
        first, jnp.concatenate([own, other], axis), jnp.concatenate([other, own], axis)
    )


def pair_rows(grid, shard):
    c = grid.here()[3]
    h = shard.shape[1] // 2
    other = grid.other_core(lax.dynamic_slice_in_dim(shard, (1 - c) * h, h, 1))
    return both(c == 0, lax.dynamic_slice_in_dim(shard, c * h, h, 1), other, 0)


def spread_z(grid, pair):
    return jnp.stack([pair] + [grid.up(pair, k) for k in range(1, grid.z)])


def spread_rest(grid, stack):
    two = jnp.concatenate([stack, grid.along(stack, 0)], 0)
    far = grid.along(two, 1)
    return [two, far, grid.other_core(two), grid.other_core(far)]


def after(value, *earlier):
    return lax.optimization_barrier((value, *earlier))[0]


def add(a, b):
    return (a.astype(F32) + b.astype(F32)).astype(BF)


def collect(grid, sends, keeps):
    z, x, y, c = grid.here()
    got = [grid.other_core(s) for s in sends]
    own = jnp.concatenate([add(k, g) for k, g in zip(keeps, got)], 2)
    blocks, r, w = own.shape
    own = own.reshape(grid.z, 2, 2, r, w)
    pick = lambda v, at, axis: lax.dynamic_index_in_dim(v, at, axis, keepdims=False)
    away = jnp.where(c == 0, pick(own, 1 - x, 1), pick(own, 1 - y, 2))
    stay = jnp.where(c == 0, pick(own, x, 1), pick(own, y, 2))
    own = add(stay, grid.along(away, 0))
    left = jnp.where(c == 0, y, x)
    own = add(pick(own, left, 1), grid.along(pick(own, 1 - left, 1), 1))
    total = pick(own, z, 0).astype(F32)
    for k in range(1, grid.z):
        total = total + grid.up(pick(own, (z + k) % grid.z, 0), k).astype(F32)
    return total


def own_rows(grid, total):
    c = grid.here()[3]
    r = total.shape[0] // 2
    other = grid.other_core(lax.dynamic_slice_in_dim(total, (1 - c) * r, r, 0))
    return both(c == 0, lax.dynamic_slice_in_dim(total, c * r, r, 0), other, 1)


def to_chunks(pair):
    r = pair.shape[0] // 4
    return jnp.concatenate([pair[j * r : (j + 1) * r] for j in range(4)], 1)


def from_chunks(total):
    w = total.shape[1] // 4
    return jnp.concatenate([total[:, j * w : (j + 1) * w] for j in range(4)], 0)


def gather_small(vectors):
    flat = jnp.concatenate([v.astype(F32) for v in vectors]).astype(BF)
    full = lax.all_gather(flat, AXES, axis=0, tiled=False).astype(F32)
    out, at = [], 0
    for v in vectors:
        out.append(full[:, at : at + v.shape[0]].reshape(-1))
        at += v.shape[0]
    return out


def scatter_small(count, vectors):
    parts = [v.reshape(count, -1) for v in vectors]
    got = lax.all_to_all(jnp.concatenate(parts, 1), AXES, 0, 0, tiled=True)
    total = jnp.sum(got, axis=0)
    out, at = [], 0
    for p in parts:
        out.append(total[at : at + p.shape[1]])
        at += p.shape[1]
    return out


def halves_of(weight):
    h = weight.shape[1] // 2
    return [weight[None, :, :h], weight[None, :, h:]]


def local(
    mesh,
    tokens,
    norm1_gain,
    norm1_bias,
    qkv_weight,
    qkv_bias,
    out_weight,
    out_bias,
    norm2_gain,
    norm2_bias,
    fc_weight,
    fc_bias,
    proj_weight,
    proj_bias,
    seq_lengths,
    out_cotangent,
):
    d = tokens.shape[1]
    grid = Grid(mesh, out_weight.shape[0])
    blocks = grid.blocks
    if grid.paired:
        place = jnp.asarray(grid.table())[lax.axis_index(AXES)]
        core = grid.here()[3].reshape(1).astype(jnp.int32)
        stack_qkv = spread_z(grid, pair_rows(grid, qkv_weight))
        first = jnp.concatenate([pair_rows(grid, fc_weight), pair_rows(grid, out_weight)], 1)
        second = to_chunks(pair_rows(grid, proj_weight))
        stack_qkv, first, second = lax.optimization_barrier((stack_qkv, first, second))
        stack_first = spread_z(grid, first)
        qkv_sources = spread_rest(grid, stack_qkv)
        first_sources = spread_rest(grid, stack_first)
        second_sources = spread_rest(grid, spread_z(grid, after(second, stack_first)))
        fcs, outs = [(s, 0) for s in first_sources], first_sources
        out_at = 4
        projs = [(s, 0) for s in second_sources]
    else:
        place = jnp.asarray(np.array([[0, 0], [1, 0]], np.int32))
        core = jnp.zeros((1,), jnp.int32)
        full = lambda v: lax.all_gather(v, AXES, axis=0, tiled=True)
        qkv_sources = halves_of(full(qkv_weight))
        fcs = [(s, 0) for s in halves_of(full(fc_weight))]
        outs, out_at = halves_of(full(out_weight)), 0
        wide = full(proj_weight)
        projs = [(to_chunks(s[0])[None], 0) for s in halves_of(wide)]
    gain_one, shift_one, bias_qv, bias_out, gain_two, shift_two, bias_fc, bias_proj = gather_small(
        [norm1_gain, norm1_bias, qkv_bias, out_bias, norm2_gain, norm2_bias, fc_bias, proj_bias]
    )
    row = lambda v: v.reshape(1, d)
    bias_qkv = jnp.stack([bias_qv[:d], jnp.zeros((d,), F32), bias_qv[d:]])
    qkv, low_one, qkv_full = project(
        place, tokens, row(gain_one), row(shift_one), bias_qkv, qkv_sources, blocks
    )
    mixed_t, mixed, stats = attend(seq_lengths, qkv, d // 128, 0, 512)
    middle, low_two, out_full = mix(
        place, mixed, tokens, row(bias_out), row(gain_two), row(shift_two), outs, blocks, out_at
    )
    (layer_out, grad_middle, grad_branch, fc_send, fc_keep, proj_send, proj_keep, fc_bias_term, sums) = mlp(
        core, place, seq_lengths, middle, low_two, out_cotangent, bias_fc.reshape(4, d), row(bias_proj),
        row(gain_two), fcs, projs, blocks,
    )
    grad_mixed, out_send, out_keep = unmix(core, seq_lengths, grad_branch, mixed, out_full, blocks)
    grad_qkv = attend_grad(qkv, grad_mixed, mixed_t, stats)
    qkv_send, qkv_keep, qkv_sums = unproject(core, low_one, grad_qkv, blocks)
    input_grad, first_sums = final(tokens, grad_qkv, qkv_full, grad_middle, row(gain_one))
    if grid.paired:
        total = collect(grid, [fc_send, proj_send, out_send], [fc_keep, proj_keep, out_keep])
        fc_wide, out_wide = fc_keep.shape[2], out_keep.shape[2]
        fc_weight_grad = own_rows(grid, total[:, :fc_wide])
        proj_weight_grad = own_rows(grid, from_chunks(total[:, fc_wide : 2 * fc_wide]))
        out_weight_grad = own_rows(grid, total[:, 2 * fc_wide :])
        qkv_weight_grad = own_rows(grid, collect(grid, [qkv_send], [qkv_keep]))
    else:
        reduce = lambda v: lax.psum_scatter(v.astype(F32), AXES, scatter_dimension=0, tiled=True)
        side = lambda k, s: jnp.concatenate([k[0], s[0]], 1)
        fc_weight_grad = reduce(side(fc_keep, fc_send))
        out_weight_grad = reduce(side(out_keep, out_send))
        qkv_weight_grad = reduce(side(qkv_keep, qkv_send))
        proj_weight_grad = reduce(
            jnp.concatenate([from_chunks(proj_keep[0]), from_chunks(proj_send[0])], 1)
        )
    small = scatter_small(
        grid.count,
        [
            first_sums[0], first_sums[1], jnp.concatenate([qkv_sums[0], qkv_sums[2]]), sums[3],
            sums[1], sums[2], fc_bias_term.reshape(-1), sums[0],
        ],
    )
    return (
        layer_out,
        input_grad,
        small[0],
        small[1],
        qkv_weight_grad,
        small[2],
        out_weight_grad,
        small[3],
        small[4],
        small[5],
        fc_weight_grad,
        small[6],
        proj_weight_grad,
        small[7],
    )


def solution(mesh):
    matrix, vector = P(AXES, None), P(AXES)
    ins = (
        matrix, vector, vector, matrix, vector, matrix, vector, vector,
        vector, matrix, vector, matrix, vector, vector, matrix,
    )
    outs = (
        matrix, matrix, vector, vector, matrix, vector, matrix, vector,
        vector, vector, matrix, vector, matrix, vector,
    )
    return jax.shard_map(
        functools.partial(local, mesh), mesh=mesh, in_specs=ins, out_specs=outs, check_vma=False
    )
```

time: 840 us -> 407 us (0.48)
  waiting for transfers between devices: 396 us -> 110 us
  matrix products: 210 us -> 0 us
  Pallas kernels: 0 us -> 144 us
  other arithmetic: 70.2 us -> 20.6 us
  starting transfers between devices: 0.32 us -> 48 us
  blocking collectives: 80.3 us -> 37.5 us
  local copies, waits for them, and re-layouts: 56.5 us -> 37.4 us
  between operations: 15.9 us -> 2.46 us
    reduce_scatter x4 -> x0, waiting for transfers between devices: 300 us -> none  [the longest x1 142 us: local(): lax.psum_scatter(fc_weight_term, ('wide', 'narrow'), scatter_dimension=0,...]
    dot_general x24 -> x0, matrix products: 210 us -> none  [the longest x4 36.6 us: right_product(): lax.dot_general(left, right, (((1,), (1,)), ((), ())), preferred_element_...]
    pallas_call x0 -> x8, Pallas kernels: none -> 144 us  [the longest x1 58.9 us: mlp(): pl.pallas_call(functools.partial(mlp_kernel, len(fcs), blocks, rb), name=...]
    ppermute x0 -> x43, waiting for transfers between devices: none -> 104 us  [send(): return lax.ppermute(value, AXES, self.perm(target))]
    all_gather x4 -> x0, waiting for transfers between devices: 93 us -> none  [the longest x1 54.2 us: local(): lax.all_gather(proj_weight, ('wide', 'narrow'), axis=0, tiled=True)]
    unnamed x2 -> x0, blocking collectives: 80.3 us -> none
    ppermute x0 -> x43, starting transfers between devices: none -> 37.9 us  [send(): return lax.ppermute(value, AXES, self.perm(target))]
    all_gather x0 -> x1, blocking collectives: none -> 37.5 us  [gather_small(): full = lax.all_gather(flat, AXES, axis=0, tiled=False).astype(F32)]
  transfers between devices with their start and end apart: 8 -> 44, of which waited for: 6 -> 20; matrix products, arithmetic and copies ran while one was open for 32% -> 12% of each run, Pallas kernels for 0% -> 11%
where the time goes in v1:
time: 407 us; the launch traced here: 399 us
  Pallas kernels  144 us (35%)
  waiting for transfers between devices  110 us (27%)
  starting transfers between devices  48 us (12%)
  blocking collectives  37.5 us (9%)
  local copies, waits for them, and re-layouts  37.4 us (9%)
  other arithmetic  20.6 us (5%)
    ppermute x43, waiting for transfers between devices, send(): return lax.ppermute(value, AXES, self.perm(target))  104 us
    pallas_call x1, Pallas kernels, mlp(): pl.pallas_call(functools.partial(mlp_kernel, len(fcs), blocks, rb), name=...  58.9 us
    ppermute x43, starting transfers between devices, send(): return lax.ppermute(value, AXES, self.perm(target))  37.9 us
    all_gather x1, blocking collectives, gather_small(): full = lax.all_gather(flat, AXES, axis=0, tiled=False).astype(F32)  37.5 us
    pallas_call x1, Pallas kernels, attend_grad(): pl.pallas_call(functools.partial(attend_grad_kernel, qb), name='attend_gr...  24.8 us
    pallas_call x1, Pallas kernels, attend(): pl.pallas_call(functools.partial(attend_kernel, qb), name='attend', grid=...  17.1 us
    pallas_call x1, Pallas kernels, project(): pl.pallas_call(functools.partial(project_kernel, len(sources)), name='pro...  10.9 us
    convert_element_type x8, other arithmetic, add(): return (a.astype(F32) + b.astype(F32)).astype(BF)  10.7 us
  transfers between devices with their start and end apart: 44, of which 20 were waited for; matrix products, arithmetic and copies ran while one was open for 12% of the time, Pallas kernels for 11%

profile of v1, /device:TPU:9, one launch (start us, length us, event | category | flops | bytes accessed | tf_op | source)
XLA Modules:
  0.0 399.2 jit_solution(14774840652057763981)
XLA Ops:
  5.6 1.3 collective-permute-start.1
  7.0 1.1 collective-permute-start.2
  8.1 1.4 collective-permute-start.3
  9.8 6.2 %collective-permute-done.2 = bf16[48,1152]{1,0:T(8,128)(2,1)S(1)} collective-permute-done((bf16[48,1152]{1,0:T(8,128)(2,1)S(1)}, bf16[48,1152]{1,0:T(8,128)(2,1)S(1)}, u32[]{:S(2)}, u32[]{:S(2)}) %collective-permute-start.2) | collective-permute-done | bytes 110624 | tf_op jit(solution)/shard_map/ppermute | solution.py:558
  16.0 2.6 collective-permute-done.3
  19.6 1.1 collective-permute-start.13
  20.7 1.3 collective-permute-start.7
  22.8 1.6 collective-permute-done.11
  24.5 10.0 %collective-permute-done.12 = bf16[48,1920]{1,0:T(8,128)(2,1)S(1)} collective-permute-done((bf16[48,1920]{1,0:T(8,128)(2,1)S(1)}, bf16[48,1920]{1,0:T(8,128)(2,1)S(1)}, u32[]{:S(2)}, u32[]{:S(2)}) %collective-permute-start.12) | collective-permute-done | bytes 184352 | tf_op jit(solution)/shard_map/ppermute | solution.py:558
  34.4 2.2 collective-permute-done.13
  36.8 1.0 collective-permute-start.19
  37.8 1.4 collective-permute-start.20
  39.8 1.2 collective-permute-start.14
  41.7 7.6 %collective-permute-done.19 = bf16[48,1536]{1,0:T(8,128)(2,1)S(1)} collective-permute-done((bf16[48,1536]{1,0:T(8,128)(2,1)S(1)}, bf16[48,1536]{1,0:T(8,128)(2,1)S(1)}, u32[]{:S(2)}, u32[]{:S(2)}) %collective-permute-start.19) | collective-permute-done | bytes 147488 | tf_op jit(solution)/shard_map/ppermute | solution.py:558
  49.3 2.2 collective-permute-done.20
  51.7 1.3 collective-permute-start.21
  54.4 1.3 collective-permute-start.15
  57.6 5.4 %collective-permute-done.21 = bf16[4,48,1536]{2,1,0:T(8,128)(2,1)S(1)} collective-permute-done((bf16[4,48,1536]{2,1,0:T(8,128)(2,1)S(1)}, bf16[4,48,1536]{2,1,0:T(8,128)(2,1)S(1)}, u32[]{:S(2)}, u32[]{:S(2)}) %collective-permute-start.21) | collective-permute-done | bytes 589856 | tf_op jit(solution)/shard_map/ppermute | solution.py:558
  63.9 2.2 collective-permute-start.22
  66.1 4.0 collective-permute-start.9
  70.1 17.0 %collective-permute-done.8.rest_1_ = bf16[8,48,1152]{2,1,0:T(8,128)(2,1)} collective-permute-done((bf16[8,48,1152]{2,1,0:T(8,128)(2,1)}, bf16[8,48,1152]{2,1,0:T(8,128)(2,1)}, u32[]{:S(2)}, u32[]{:S(2)}) %collective-permute-start.8) | collective-permute-done | bytes 884768 | tf_op jit(solution)/shard_map/ppermute | solution.py:558
  87.8 37.5 %all-gather = bf16[32,1,288]{2,1,0:T(2,128)(2,1)S(1)} all-gather(bf16[1,1,288]{2,1,0:T(2,128)(2,1)S(1)} %bitcast.107), channel_id=1, replica_groups=mesh['wide'=8,'narrow'=4] {'wide','narrow'}, dimensions={0}, use_global_device_ids=true | all-gather | bytes 19008 | tf_op jit(solution)/shard_map/all_gather | solution.py:641
  131.8 1.3 fusion.6.place
  133.7 10.9 %project.1 = (bf16[3,1024,768]{2,1,0:T(8,128)(2,1)}, bf16[1024,768]{1,0:T(8,128)(2,1)}, bf16[16,48,2304]{2,1,0:T(8,128)(2,1)}) custom-call(s32[4,9]{1,0:T(4,128)} %fusion.6.place, bf16[1024,768]{1,0:T(8,128)(2,1)} %x_ref.5, f32[1,768]{1,0:T(1,128)} %reshape_reshape.26.gain_ref, f32[1,768]{1,0:T(1,128)} %reshape_reshape.27.shift_ref, ...), custom_call_target="tpu_custom_call" | custom-call | flops 3623878656 | bytes 18000000 | tf_op jit(solution)/shard_map/project/pallas_call | solution.py:225
  144.7 17.1 %attend.1 = (f32[768,1024]{1,0:T(8,128)}, bf16[1024,768]{1,0:T(8,128)(2,1)}, f32[6,2,1024]{2,1,0:T(2,128)}) custom-call(s32[1]{0:T(128)S(6)} %copy.74.len_ref.lens, bf16[3,1024,768]{2,1,0:T(8,128)(2,1)} %get-tuple-element.45.qkv_ref), custom_call_target="tpu_custom_call" | custom-call | flops 3221225472 | bytes 8000000 | tf_op jit(solution)/shard_map/attend/pallas_call | solution.py:67
  161.8 7.0 %mix.1 = (f32[1024,768]{1,0:T(8,128)}, bf16[1024,768]{1,0:T(8,128)(2,1)}, bf16[16,48,768]{2,1,0:T(8,128)(2,1)}) custom-call(s32[4,9]{1,0:T(4,128)} %fusion.6.place, bf16[1024,768]{1,0:T(8,128)(2,1)} %get-tuple-element.46.attn_ref, bf16[1024,768]{1,0:T(8,128)(2,1)} %x_ref.5, f32[1,768]{1,0:T(1,128)} %reshape_reshape.28.bias_ref, ...), custom_call_target="tpu_custom_call" | custom-call | flops 1207959552 | bytes 9000000 | tf_op jit(solution)/shard_map/mix/pallas_call | solution.py:266
  168.9 58.9 %mlp.1 = (bf16[1024,768]{1,0:T(8,128)(2,1)}, f32[1024,768]{1,0:T(8,128)}, bf16[1024,768]{1,0:T(8,128)(2,1)}, bf16[16,48,1536]{2,1,0:T(8,128)(2,1)}, bf16[16,48,1...) custom-call(s32[1]{0:T(128)} %bitcast.core, ...), custom_call_target="tpu_custom_call" | custom-call | flops 28991029248 | bytes 40000000 | tf_op jit(solution)/shard_map/mlp/pallas_call | solution.py:393
  227.8 6.5 %unmix.1 = (bf16[1024,768]{1,0:T(8,128)(2,1)}, bf16[16,48,384]{2,1,0:T(8,128)(2,1)}, bf16[16,48,384]{2,1,0:T(8,128)(2,1)}) custom-call(s32[1]{0:T(128)} %bitcast.core, s32[1]{0:T(128)S(6)} %copy.74.len_ref.lens, bf16[1024,768]{1,0:T(8,128)(2,1)} %get-tuple-element.53.gbr_ref, bf16[1024,768]{1,0:T(8,128)(2,1)} %get-tuple-element.46.attn_ref, ...), custom_call_target="tpu_custom_call" | custom-call | flops 2415919104 | bytes 9000000 | tf_op jit(solution)/shard_map/unmix/pallas_call | solution.py:448
  234.3 24.8 %attend_grad.1.g_ref = bf16[3,1024,768]{2,1,0:T(8,128)(2,1)} custom-call(bf16[3,1024,768]{2,1,0:T(8,128)(2,1)} %get-tuple-element.45.qkv_ref, bf16[1024,768]{1,0:T(8,128)(2,1)} %get-tuple-element.55.grad_ref, f32[768,1024]{1,0:T(8,128)} %get-tuple-element.56.out_t_ref, f32[6,2,1024]{2,1,0:T(2,128)} %get-tuple-element.57.stat_ref), custom_call_target="tpu_custom_call" | custom-call | flops 8053063680 | bytes 16000000 | tf_op jit(solution)/shard_map/attend_grad/pallas_call | solution.py:139
  259.0 8.9 %unproject.1 = (bf16[16,48,1152]{2,1,0:T(8,128)(2,1)}, bf16[16,48,1152]{2,1,0:T(8,128)(2,1)}, f32[3,768]{1,0:T(4,128)}) custom-call(s32[1]{0:T(128)} %bitcast.core, bf16[1024,768]{1,0:T(8,128)(2,1)} %get-tuple-element.62.low_ref, bf16[3,1024,768]{2,1,0:T(8,128)(2,1)} %attend_grad.1.g_ref), custom_call_target="tpu_custom_call" | custom-call | flops 3623878656 | bytes 10000000 | tf_op jit(solution)/shard_map/unproject/pallas_call | solution.py:478
  269.0 10.5 %collective-permute-done.34 = bf16[16,48,384]{2,1,0:T(8,128)(2,1)S(1)} collective-permute-done((bf16[16,48,384]{2,1,0:T(8,128)(2,1)}, bf16[16,48,384]{2,1,0:T(8,128)(2,1)S(1)}, u32[]{:S(2)}, u32[]{:S(2)}) %collective-permute-start.34) | collective-permute-done | bytes 589856 | tf_op jit(solution)/shard_map/ppermute | solution.py:558
  279.7 2.1 add_convert_fusion.3
  281.8 2.5 add_convert_fusion.2
  286.2 1.9 constant_dynamic-slice_fusion.8
  288.1 1.8 bitcast_select_fusion
  290.1 1.1 constant_dynamic-slice_fusion.14
  291.2 1.0 bitcast_select_fusion.2
  292.2 1.5 collective-permute-start.26
  295.0 9.6 %final.1 = (bf16[1024,768]{1,0:T(8,128)(2,1)}, f32[2,768]{1,0:T(2,128)}) custom-call(bf16[1024,768]{1,0:T(8,128)(2,1)} %x_ref.5, bf16[3,1024,768]{2,1,0:T(8,128)(2,1)} %attend_grad.1.g_ref, bf16[16,48,2304]{2,1,0:T(8,128)(2,1)} %get-tuple-element.58.w_ref, f32[1024,768]{1,0:T(8,128)} %get-tuple-element.59.gmid_ref, f32[1,768]{1,0:T(1,128)} %reshape_reshape.26.gain_ref), custom_call_target="tpu_custom_call" | custom-call | flops 3623878656 | bytes 15000000 | tf_op jit(solution)/shard_map/final/pallas_call | solution.py:501
  304.6 1.4 slice_reduce_fusion.6
  306.8 1.4 reshape_squeeze.19
  308.1 1.5 slice_reduce_fusion
  309.6 1.4 reshape_squeeze.20
  311.0 1.4 reshape_squeeze.21
  312.3 1.4 reshape_squeeze.22
  313.7 1.4 reshape_squeeze.23
  315.0 1.4 reshape_reshape.33
  316.4 1.3 pad_maximum_fusion.7
  317.8 1.5 concatenate.160
  319.3 1.5 all_to_all.6
  320.7 10.1 %all-to-all-start = ((f32[32,1,288]{2,1,0:T(1,128)}), f32[32,1,288]{2,1,0:T(1,128)}, u32[]{:S(2)}, u32[]{:S(2)}) async-start(f32[32,1,288]{2,1,0:T(1,128)} %all_to_all.6), calls=%async_computation | async-start | bytes 98304 | tf_op jit(solution)/shard_map/all_to_all | solution.py:651
  331.0 5.6 %all-to-all-done = f32[32,1,288]{2,1,0:T(1,128)} async-done(((f32[32,1,288]{2,1,0:T(1,128)}), f32[32,1,288]{2,1,0:T(1,128)}, u32[]{:S(2)}, u32[]{:S(2)}) %all-to-all-start) | async-done | bytes 36896 | tf_op jit(solution)/shard_map/all_to_all | solution.py:651
  337.4 1.9 add_convert_fusion.4
  340.3 2.8 add_convert_fusion
  343.9 3.0 collective-permute-done.27
  347.5 3.8 collective-permute-start.29
  353.0 5.0 %collective-permute-done.29 = bf16[48,1152]{1,0:T(8,128)(2,1)S(1)} collective-permute-done((bf16[48,1152]{1,0:T(8,128)(2,1)S(1)}, bf16[48,1152]{1,0:T(8,128)(2,1)S(1)}, u32[]{:S(2)}, u32[]{:S(2)}) %collective-permute-start.29) | collective-permute-done | bytes 110624 | tf_op jit(solution)/shard_map/ppermute | solution.py:558
  358.0 2.2 collective-permute-done.30
  360.3 1.4 collective-permute-start.31
  362.3 3.5 collective-permute-start.38
  366.5 3.9 collective-permute-done.37
  370.4 18.8 %collective-permute-done.38 = bf16[48,3456]{1,0:T(8,128)(2,1)S(1)} collective-permute-done((bf16[48,3456]{1,0:T(8,128)(2,1)S(1)}, bf16[48,3456]{1,0:T(8,128)(2,1)S(1)}, u32[]{:S(2)}, u32[]{:S(2)}) %collective-permute-start.38) | collective-permute-done | bytes 331808 | tf_op jit(solution)/shard_map/ppermute | solution.py:558
  389.2 4.5 %collective-permute-done.39 = bf16[48,3456]{1,0:T(8,128)(2,1)S(1)} collective-permute-done((bf16[48,3456]{1,0:T(8,128)(2,1)S(1)}, bf16[48,3456]{1,0:T(8,128)(2,1)S(1)}, u32[]{:S(2)}, u32[]{:S(2)}) %collective-permute-start.39) | collective-permute-done | bytes 331808 | tf_op jit(solution)/shard_map/ppermute | solution.py:558
  394.0 1.4 collective-permute-start.42
  (160 shorter events, 35.2 us)
Async XLA Ops:
  1.6 7.9 %collective-permute-start.6 = (bf16[96,384]{1,0:T(8,128)(2,1)S(1)}, bf16[96,384]{1,0:T(8,128)(2,1)S(1)}, u32[]{:S(2)}, u32[]{:S(2)}) collective-permute-start(bf16[96,384]{1,0:T(8,128)(2,1)S(1)} %get-tuple-element.112), channel_id=1, source_target_pairs={{0,1},{1,0},{2,3},{3,2},{4,5},{5,4},{6,7},{7,6},{8,9},{9,8},{10,11... | collective-permute-start | bytes 221192 | tf_op jit(solution)/shard_map/ppermute | solution.py:558
  3.2 2.4 collective-permute-start
  4.1 1.5 collective-permute-start.5
  5.5 4.1 %collective-permute-start.4 = (bf16[24,1536]{1,0:T(8,128)(2,1)S(1)}, bf16[24,1536]{1,0:T(8,128)(2,1)S(1)}, u32[]{:S(2)}, u32[]{:S(2)}) collective-permute-start(bf16[24,1536]{1,0:T(8,128)(2,1)S(1)} %get-tuple-element.114), channel_id=1, source_target_pairs={{0,1},{1,0},{2,3},{3,2},{4,5},{5,4},{6,7},{7,6},{8,9},{9,8},{10,11... | collective-permute-start | bytes 221192 | tf_op jit(solution)/shard_map/ppermute | solution.py:558
  5.6 4.2 %collective-permute-start.1 = (bf16[48,1152]{1,0:T(8,128)(2,1)S(1)}, bf16[48,1152]{1,0:T(8,128)(2,1)S(1)}, u32[]{:S(2)}, u32[]{:S(2)}) collective-permute-start(bf16[48,1152]{1,0:T(8,128)(2,1)S(1)} %maximum_select_fusion.6), channel_id=1, source_target_pairs={{0,8},{1,9},{2,10},{3,11},{4,12},{5,13},{6,14},{7,15},{8,16},{9,17... | collective-permute-start | bytes 331784 | tf_op jit(solution)/shard_map/ppermute | solution.py:558
  7.0 9.1 %collective-permute-start.2 = (bf16[48,1152]{1,0:T(8,128)(2,1)S(1)}, bf16[48,1152]{1,0:T(8,128)(2,1)S(1)}, u32[]{:S(2)}, u32[]{:S(2)}) collective-permute-start(bf16[48,1152]{1,0:T(8,128)(2,1)S(1)} %maximum_select_fusion.6), channel_id=1, source_target_pairs={{0,16},{1,17},{2,18},{3,19},{4,20},{5,21},{6,22},{7,23},{8,24},{9,... | collective-permute-start | bytes 331784 | tf_op jit(solution)/shard_map/ppermute | solution.py:558
  8.1 10.6 %collective-permute-start.3 = (bf16[48,1152]{1,0:T(8,128)(2,1)S(1)}, bf16[48,1152]{1,0:T(8,128)(2,1)S(1)}, u32[]{:S(2)}, u32[]{:S(2)}) collective-permute-start(bf16[48,1152]{1,0:T(8,128)(2,1)S(1)} %maximum_select_fusion.6), channel_id=1, source_target_pairs={{0,24},{1,25},{2,26},{3,27},{4,28},{5,29},{6,30},{7,31},{8,0},{9,1... | collective-permute-start | bytes 331784 | tf_op jit(solution)/shard_map/ppermute | solution.py:558
  18.7 5.8 %collective-permute-start.11 = (bf16[48,1920]{1,0:T(8,128)(2,1)S(1)}, bf16[48,1920]{1,0:T(8,128)(2,1)S(1)}, u32[]{:S(2)}, u32[]{:S(2)}) collective-permute-start(bf16[48,1920]{1,0:T(8,128)(2,1)S(1)} %pad_maximum_fusion.5), channel_id=1, source_target_pairs={{0,8},{1,9},{2,10},{3,11},{4,12},{5,13},{6,14},{7,15},{8,16},{9,17... | collective-permute-start | bytes 552968 | tf_op jit(solution)/shard_map/ppermute | solution.py:558
  18.8 15.7 %collective-permute-start.12 = (bf16[48,1920]{1,0:T(8,128)(2,1)S(1)}, bf16[48,1920]{1,0:T(8,128)(2,1)S(1)}, u32[]{:S(2)}, u32[]{:S(2)}) collective-permute-start(bf16[48,1920]{1,0:T(8,128)(2,1)S(1)} %pad_maximum_fusion.5), channel_id=1, source_target_pairs={{0,16},{1,17},{2,18},{3,19},{4,20},{5,21},{6,22},{7,23},{8,24},{9,... | collective-permute-start | bytes 552968 | tf_op jit(solution)/shard_map/ppermute | solution.py:558
  19.6 16.9 %collective-permute-start.13 = (bf16[48,1920]{1,0:T(8,128)(2,1)S(1)}, bf16[48,1920]{1,0:T(8,128)(2,1)S(1)}, u32[]{:S(2)}, u32[]{:S(2)}) collective-permute-start(bf16[48,1920]{1,0:T(8,128)(2,1)S(1)} %pad_maximum_fusion.5), channel_id=1, source_target_pairs={{0,24},{1,25},{2,26},{3,27},{4,28},{5,29},{6,30},{7,31},{8,0},{9,1... | collective-permute-start | bytes 552968 | tf_op jit(solution)/shard_map/ppermute | solution.py:558
  20.7 35.6 %collective-permute-start.7 = (bf16[4,48,1152]{2,1,0:T(8,128)(2,1)S(1)}, bf16[4,48,1152]{2,1,0:T(8,128)(2,1)S(1)}, u32[]{:S(2)}, u32[]{:S(2)}) collective-permute-start(bf16[4,48,1152]{2,1,0:T(8,128)(2,1)S(1)} %pad_maximum_fusion.3), channel_id=1, source_target_pairs={{0,4},{1,3},{2,6},{3,1},{4,0},{5,7},{6,2},{7,5},{8,12},{9,11},{10,... | collective-permute-start | bytes 1327112 | tf_op jit(solution)/shard_map/ppermute | solution.py:558
  36.7 5.0 %collective-permute-start.18 = (bf16[48,1536]{1,0:T(8,128)(2,1)S(1)}, bf16[48,1536]{1,0:T(8,128)(2,1)S(1)}, u32[]{:S(2)}, u32[]{:S(2)}) collective-permute-start(bf16[48,1536]{1,0:T(8,128)(2,1)S(1)} %pad_maximum_fusion.6), channel_id=1, source_target_pairs={{0,8},{1,9},{2,10},{3,11},{4,12},{5,13},{6,14},{7,15},{8,16},{9,17... | collective-permute-start | bytes 442376 | tf_op jit(solution)/shard_map/ppermute | solution.py:558
  36.8 12.5 %collective-permute-start.19 = (bf16[48,1536]{1,0:T(8,128)(2,1)S(1)}, bf16[48,1536]{1,0:T(8,128)(2,1)S(1)}, u32[]{:S(2)}, u32[]{:S(2)}) collective-permute-start(bf16[48,1536]{1,0:T(8,128)(2,1)S(1)} %pad_maximum_fusion.6), channel_id=1, source_target_pairs={{0,16},{1,17},{2,18},{3,19},{4,20},{5,21},{6,22},{7,23},{8,24},{9,... | collective-permute-start | bytes 442376 | tf_op jit(solution)/shard_map/ppermute | solution.py:558
  37.8 13.7 %collective-permute-start.20 = (bf16[48,1536]{1,0:T(8,128)(2,1)S(1)}, bf16[48,1536]{1,0:T(8,128)(2,1)S(1)}, u32[]{:S(2)}, u32[]{:S(2)}) collective-permute-start(bf16[48,1536]{1,0:T(8,128)(2,1)S(1)} %pad_maximum_fusion.6), channel_id=1, source_target_pairs={{0,24},{1,25},{2,26},{3,27},{4,28},{5,29},{6,30},{7,31},{8,0},{9,1... | collective-permute-start | bytes 442376 | tf_op jit(solution)/shard_map/ppermute | solution.py:558
  39.8 14.5 %collective-permute-start.14 = (bf16[4,48,1920]{2,1,0:T(8,128)(2,1)S(1)}, bf16[4,48,1920]{2,1,0:T(8,128)(2,1)S(1)}, u32[]{:S(2)}, u32[]{:S(2)}) collective-permute-start(bf16[4,48,1920]{2,1,0:T(8,128)(2,1)S(1)} %pad_maximum_fusion.1), channel_id=1, source_target_pairs={{0,4},{1,3},{2,6},{3,1},{4,0},{5,7},{6,2},{7,5},{8,12},{9,11},{10,... | collective-permute-start | bytes 2211848 | tf_op jit(solution)/shard_map/ppermute | solution.py:558
  51.6 36.1 %copy-start.8 = (bf16[24]{0:T(256)(128)(2,1)S(1)}, bf16[24]{0:T(256)(128)(2,1)}, u32[]{:S(2)}) copy-start(bf16[24]{0:T(256)(128)(2,1)} %param.17) | copy-start | bytes 148
  51.6 36.1 %copy-start.9 = (bf16[24]{0:T(256)(128)(2,1)S(1)}, bf16[24]{0:T(256)(128)(2,1)}, u32[]{:S(2)}) copy-start(bf16[24]{0:T(256)(128)(2,1)} %param.18) | copy-start | bytes 148
  51.6 36.1 %copy-start.10 = (bf16[48]{0:T(256)(128)(2,1)S(1)}, bf16[48]{0:T(256)(128)(2,1)}, u32[]{:S(2)}) copy-start(bf16[48]{0:T(256)(128)(2,1)} %param.20) | copy-start | bytes 292
  51.6 36.1 %copy-start.11 = (bf16[24]{0:T(256)(128)(2,1)S(1)}, bf16[24]{0:T(256)(128)(2,1)}, u32[]{:S(2)}) copy-start(bf16[24]{0:T(256)(128)(2,1)} %param.22) | copy-start | bytes 148
  51.6 36.1 %copy-start.12 = (bf16[24]{0:T(256)(128)(2,1)S(1)}, bf16[24]{0:T(256)(128)(2,1)}, u32[]{:S(2)}) copy-start(bf16[24]{0:T(256)(128)(2,1)} %param.23) | copy-start | bytes 148
  51.6 36.1 %copy-start.13 = (bf16[24]{0:T(256)(128)(2,1)S(1)}, bf16[24]{0:T(256)(128)(2,1)}, u32[]{:S(2)}) copy-start(bf16[24]{0:T(256)(128)(2,1)} %param.24) | copy-start | bytes 148
  51.6 36.1 %copy-start.14 = (bf16[96]{0:T(256)(128)(2,1)S(1)}, bf16[96]{0:T(256)(128)(2,1)}, u32[]{:S(2)}) copy-start(bf16[96]{0:T(256)(128)(2,1)} %param.26) | copy-start | bytes 580
  51.7 36.1 %copy-start.15 = (bf16[24]{0:T(256)(128)(2,1)S(1)}, bf16[24]{0:T(256)(128)(2,1)}, u32[]{:S(2)}) copy-start(bf16[24]{0:T(256)(128)(2,1)} %param.28) | copy-start | bytes 148
  51.7 11.4 %collective-permute-start.21 = (bf16[4,48,1536]{2,1,0:T(8,128)(2,1)S(1)}, bf16[4,48,1536]{2,1,0:T(8,128)(2,1)S(1)}, u32[]{:S(2)}, u32[]{:S(2)}) collective-permute-start(bf16[4,48,1536]{2,1,0:T(8,128)(2,1)S(1)} %pad_maximum_fusion.2), channel_id=1, source_target_pairs={{0,4},{1,3},{2,6},{3,1},{4,0},{5,7},{6,2},{7,5},{8,12},{9,11},{10,... | collective-permute-start | bytes 1769480 | tf_op jit(solution)/shard_map/ppermute | solution.py:558
  54.4 90.2 %copy-start.3 = (bf16[8,48,1920]{2,1,0:T(8,128)(2,1)}, bf16[8,48,1920]{2,1,0:T(8,128)(2,1)S(1)}, u32[]{:S(2)}) copy-start(bf16[8,48,1920]{2,1,0:T(8,128)(2,1)S(1)} %constant_dynamic-update-slice_fusion.2.rest_0_) | copy-start | bytes 4423684
  54.4 33.2 %collective-permute-start.15 = (bf16[8,48,1920]{2,1,0:T(8,128)(2,1)S(1)}, bf16[8,48,1920]{2,1,0:T(8,128)(2,1)S(1)}, u32[]{:S(2)}, u32[]{:S(2)}) collective-permute-start(bf16[8,48,1920]{2,1,0:T(8,128)(2,1)S(1)} %constant_dynamic-update-slice_fusion.2.rest_0_), channel_id=1, source_target_pairs={{0,2},{1,5},{2,0},{3,7},{4,6},{5,1},{6,4},{7,3},{8,10},{9,13},{10,... | collective-permute-start | bytes 4423688 | tf_op jit(solution)/shard_map/ppermute | solution.py:558
  57.2 29.9 %collective-permute-start.8 = (bf16[8,48,1152]{2,1,0:T(8,128)(2,1)}, bf16[8,48,1152]{2,1,0:T(8,128)(2,1)}, u32[]{:S(2)}, u32[]{:S(2)}) collective-permute-start(bf16[8,48,1152]{2,1,0:T(8,128)(2,1)} %constant_dynamic-update-slice_fusion.rest_0_), channel_id=1, source_target_pairs={{0,2},{1,5},{2,0},{3,7},{4,6},{5,1},{6,4},{7,3},{8,10},{9,13},{10,... | collective-permute-start | bytes 2654216 | tf_op jit(solution)/shard_map/ppermute | solution.py:558
  63.9 61.8 %collective-permute-start.22 = (bf16[8,48,1536]{2,1,0:T(8,128)(2,1)}, bf16[8,48,1536]{2,1,0:T(8,128)(2,1)}, u32[]{:S(2)}, u32[]{:S(2)}) collective-permute-start(bf16[8,48,1536]{2,1,0:T(8,128)(2,1)} %constant_dynamic-update-slice_fusion.7.rest_4_), channel_id=1, source_target_pairs={{0,2},{1,5},{2,0},{3,7},{4,6},{5,1},{6,4},{7,3},{8,10},{9,13},{10,... | collective-permute-start | bytes 3538952 | tf_op jit(solution)/shard_map/ppermute | solution.py:558
  66.1 59.3 %collective-permute-start.9 = (bf16[8,48,1152]{2,1,0:T(8,128)(2,1)}, bf16[8,48,1152]{2,1,0:T(8,128)(2,1)}, u32[]{:S(2)}, u32[]{:S(2)}) collective-permute-start(bf16[8,48,1152]{2,1,0:T(8,128)(2,1)} %constant_dynamic-update-slice_fusion.rest_0_), channel_id=1, source_target_pairs={{0,1},{1,0},{2,3},{3,2},{4,5},{5,4},{6,7},{7,6},{8,9},{9,8},{10,11... | collective-permute-start | bytes 2654216 | tf_op jit(solution)/shard_map/ppermute | solution.py:558
  87.1 46.6 %collective-permute-start.10 = (bf16[8,48,1152]{2,1,0:T(8,128)(2,1)}, bf16[8,48,1152]{2,1,0:T(8,128)(2,1)}, u32[]{:S(2)}, u32[]{:S(2)}) collective-permute-start(bf16[8,48,1152]{2,1,0:T(8,128)(2,1)} %collective-permute-done.8.rest_1_), channel_id=1, source_target_pairs={{0,1},{1,0},{2,3},{3,2},{4,5},{5,4},{6,7},{7,6},{8,9},{9,8},{10,11... | collective-permute-start | bytes 2654216 | tf_op jit(solution)/shard_map/ppermute | solution.py:558
  87.1 74.7 %collective-permute-start.16 = (bf16[8,48,1920]{2,1,0:T(8,128)(2,1)S(1)}, bf16[8,48,1920]{2,1,0:T(8,128)(2,1)}, u32[]{:S(2)}, u32[]{:S(2)}) collective-permute-start(bf16[8,48,1920]{2,1,0:T(8,128)(2,1)S(1)} %constant_dynamic-update-slice_fusion.2.rest_0_), channel_id=1, source_target_pairs={{0,1},{1,0},{2,3},{3,2},{4,5},{5,4},{6,7},{7,6},{8,9},{9,8},{10,11... | collective-permute-start | bytes 4423688 | tf_op jit(solution)/shard_map/ppermute | solution.py:558
  87.6 57.0 %copy-start.5 = (bf16[8,48,1920]{2,1,0:T(8,128)(2,1)}, bf16[8,48,1920]{2,1,0:T(8,128)(2,1)S(1)}, u32[]{:S(2)}) copy-start(bf16[8,48,1920]{2,1,0:T(8,128)(2,1)S(1)} %collective-permute-done.15.rest_1_) | copy-start | bytes 4423684
  87.6 74.2 %collective-permute-start.17 = (bf16[8,48,1920]{2,1,0:T(8,128)(2,1)S(1)}, bf16[8,48,1920]{2,1,0:T(8,128)(2,1)}, u32[]{:S(2)}, u32[]{:S(2)}) collective-permute-start(bf16[8,48,1920]{2,1,0:T(8,128)(2,1)S(1)} %collective-permute-done.15.rest_1_), channel_id=1, source_target_pairs={{0,1},{1,0},{2,3},{3,2},{4,5},{5,4},{6,7},{7,6},{8,9},{9,8},{10,11... | collective-permute-start | bytes 4423688 | tf_op jit(solution)/shard_map/ppermute | solution.py:558
  125.4 43.4 %collective-permute-start.23 = (bf16[8,48,1536]{2,1,0:T(8,128)(2,1)}, bf16[8,48,1536]{2,1,0:T(8,128)(2,1)}, u32[]{:S(2)}, u32[]{:S(2)}) collective-permute-start(bf16[8,48,1536]{2,1,0:T(8,128)(2,1)} %constant_dynamic-update-slice_fusion.7.rest_4_), channel_id=1, source_target_pairs={{0,1},{1,0},{2,3},{3,2},{4,5},{5,4},{6,7},{7,6},{8,9},{9,8},{10,11... | collective-permute-start | bytes 3538952 | tf_op jit(solution)/shard_map/ppermute | solution.py:558
  125.7 43.2 %collective-permute-start.24 = (bf16[8,48,1536]{2,1,0:T(8,128)(2,1)}, bf16[8,48,1536]{2,1,0:T(8,128)(2,1)}, u32[]{:S(2)}, u32[]{:S(2)}) collective-permute-start(bf16[8,48,1536]{2,1,0:T(8,128)(2,1)} %collective-permute-done.22.rest_5_), channel_id=1, source_target_pairs={{0,1},{1,0},{2,3},{3,2},{4,5},{5,4},{6,7},{7,6},{8,9},{9,8},{10,11... | collective-permute-start | bytes 3538952 | tf_op jit(solution)/shard_map/ppermute | solution.py:558
  259.0 20.4 %copy-start.6 = (bf16[16,48,384]{2,1,0:T(8,128)(2,1)S(1)}, bf16[16,48,384]{2,1,0:T(8,128)(2,1)}, u32[]{:S(2)}) copy-start(bf16[16,48,384]{2,1,0:T(8,128)(2,1)} %get-tuple-element.72) | copy-start | bytes 1769476
  268.0 11.7 %collective-permute-start.25 = (bf16[16,48,1152]{2,1,0:T(8,128)(2,1)}, bf16[16,48,1152]{2,1,0:T(8,128)(2,1)}, u32[]{:S(2)}, u32[]{:S(2)}) collective-permute-start(bf16[16,48,1152]{2,1,0:T(8,128)(2,1)} %get-tuple-element.67), channel_id=1, source_target_pairs={{0,1},{1,0},{2,3},{3,2},{4,5},{5,4},{6,7},{7,6},{8,9},{9,8},{10,11... | collective-permute-start | bytes 5308424 | tf_op jit(solution)/shard_map/ppermute | solution.py:558
  268.2 13.6 %collective-permute-start.32 = (bf16[16,48,1536]{2,1,0:T(8,128)(2,1)}, bf16[16,48,1536]{2,1,0:T(8,128)(2,1)}, u32[]{:S(2)}, u32[]{:S(2)}) collective-permute-start(bf16[16,48,1536]{2,1,0:T(8,128)(2,1)} %get-tuple-element.69), channel_id=1, source_target_pairs={{0,1},{1,0},{2,3},{3,2},{4,5},{5,4},{6,7},{7,6},{8,9},{9,8},{10,11... | collective-permute-start | bytes 7077896 | tf_op jit(solution)/shard_map/ppermute | solution.py:558
  268.5 15.9 %collective-permute-start.33 = (bf16[16,48,1536]{2,1,0:T(8,128)(2,1)}, bf16[16,48,1536]{2,1,0:T(8,128)(2,1)S(1)}, u32[]{:S(2)}, u32[]{:S(2)}) collective-permute-start(bf16[16,48,1536]{2,1,0:T(8,128)(2,1)} %get-tuple-element.71), channel_id=1, source_target_pairs={{0,1},{1,0},{2,3},{3,2},{4,5},{5,4},{6,7},{7,6},{8,9},{9,8},{10,11... | collective-permute-start | bytes 7077896 | tf_op jit(solution)/shard_map/ppermute | solution.py:558
  268.7 10.8 %collective-permute-start.34 = (bf16[16,48,384]{2,1,0:T(8,128)(2,1)}, bf16[16,48,384]{2,1,0:T(8,128)(2,1)S(1)}, u32[]{:S(2)}, u32[]{:S(2)}) collective-permute-start(bf16[16,48,384]{2,1,0:T(8,128)(2,1)} %get-tuple-element.73), channel_id=1, source_target_pairs={{0,1},{1,0},{2,3},{3,2},{4,5},{5,4},{6,7},{7,6},{8,9},{9,8},{10,11... | collective-permute-start | bytes 1769480 | tf_op jit(solution)/shard_map/ppermute | solution.py:558
  269.0 10.6 %copy-start.4 = (bf16[16,48,1152]{2,1,0:T(8,128)(2,1)S(1)}, bf16[16,48,1152]{2,1,0:T(8,128)(2,1)}, u32[]{:S(2)}) copy-start(bf16[16,48,1152]{2,1,0:T(8,128)(2,1)} %get-tuple-element.66) | copy-start | bytes 5308420
  279.6 2.2 copy-start.2
  281.8 2.5 copy-start.1
  289.9 50.3 %collective-permute-start.35 = (bf16[4,2,48,3456]{3,2,0,1:T(8,128)(2,1)}, bf16[4,2,48,3456]{3,2,0,1:T(8,128)(2,1)}, u32[]{:S(2)}, u32[]{:S(2)}) collective-permute-start(bf16[4,2,48,3456]{3,2,0,1:T(8,128)(2,1)} %bitcast_select_fusion), channel_id=1, source_target_pairs={{0,4},{1,3},{2,6},{3,1},{4,0},{5,7},{6,2},{7,5},{8,12},{9,11},{10,... | collective-permute-start | bytes 7962632 | tf_op jit(solution)/shard_map/ppermute | solution.py:558
  290.1 3.6 copy-start.7
  292.2 45.2 %collective-permute-start.26 = (bf16[4,2,48,1152]{3,2,0,1:T(8,128)(2,1)}, bf16[4,2,48,1152]{3,2,0,1:T(8,128)(2,1)}, u32[]{:S(2)}, u32[]{:S(2)}) collective-permute-start(bf16[4,2,48,1152]{3,2,0,1:T(8,128)(2,1)} %bitcast_select_fusion.2), channel_id=1, source_target_pairs={{0,4},{1,3},{2,6},{3,1},{4,0},{5,7},{6,2},{7,5},{8,12},{9,11},{10,... | collective-permute-start | bytes 2654216 | tf_op jit(solution)/shard_map/ppermute | solution.py:558
  320.7 15.8 %all-to-all-start = ((f32[32,1,288]{2,1,0:T(1,128)}), f32[32,1,288]{2,1,0:T(1,128)}, u32[]{:S(2)}, u32[]{:S(2)}) async-start(f32[32,1,288]{2,1,0:T(1,128)} %all_to_all.6), calls=%async_computation | async-start | bytes 98304 | tf_op jit(solution)/shard_map/all_to_all | solution.py:651
  337.4 2.9 copy-start
  339.4 7.5 %collective-permute-start.27 = (bf16[4,48,1152]{2,1,0:T(8,128)(2,1)S(1)}, bf16[4,48,1152]{2,1,0:T(8,128)(2,1)S(1)}, u32[]{:S(2)}, u32[]{:S(2)}) collective-permute-start(bf16[4,48,1152]{2,1,0:T(8,128)(2,1)S(1)} %dynamic-slice_bitcast_fusion.1), channel_id=1, source_target_pairs={{0,2},{1,5},{2,0},{3,7},{4,6},{5,1},{6,4},{7,3},{8,10},{9,13},{10,... | collective-permute-start | bytes 1327112 | tf_op jit(solution)/shard_map/ppermute | solution.py:558
  343.2 18.5 %collective-permute-start.36 = (bf16[4,48,3456]{2,1,0:T(8,128)(2,1)S(1)}, bf16[4,48,3456]{2,1,0:T(8,128)(2,1)S(1)}, u32[]{:S(2)}, u32[]{:S(2)}) collective-permute-start(bf16[4,48,3456]{2,1,0:T(8,128)(2,1)S(1)} %dynamic-slice_bitcast_fusion), channel_id=1, source_target_pairs={{0,2},{1,5},{2,0},{3,7},{4,6},{5,1},{6,4},{7,3},{8,10},{9,13},{10,... | collective-permute-start | bytes 3981320 | tf_op jit(solution)/shard_map/ppermute | solution.py:558
  347.1 5.9 %collective-permute-start.28 = (bf16[48,1152]{1,0:T(8,128)(2,1)S(1)}, bf16[48,1152]{1,0:T(8,128)(2,1)S(1)}, u32[]{:S(2)}, u32[]{:S(2)}) collective-permute-start(bf16[48,1152]{1,0:T(8,128)(2,1)S(1)} %get-tuple-element.98), channel_id=1, source_target_pairs={{0,8},{1,9},{2,10},{3,11},{4,12},{5,13},{6,14},{7,15},{8,16},{9,17... | collective-permute-start | bytes 331784 | tf_op jit(solution)/shard_map/ppermute | solution.py:558
  347.5 10.6 %collective-permute-start.29 = (bf16[48,1152]{1,0:T(8,128)(2,1)S(1)}, bf16[48,1152]{1,0:T(8,128)(2,1)S(1)}, u32[]{:S(2)}, u32[]{:S(2)}) collective-permute-start(bf16[48,1152]{1,0:T(8,128)(2,1)S(1)} %get-tuple-element.100), channel_id=1, source_target_pairs={{0,16},{1,17},{2,18},{3,19},{4,20},{5,21},{6,22},{7,23},{8,24},{9,... | collective-permute-start | bytes 331784 | tf_op jit(solution)/shard_map/ppermute | solution.py:558
  351.2 9.0 %collective-permute-start.30 = (bf16[48,1152]{1,0:T(8,128)(2,1)S(1)}, bf16[48,1152]{1,0:T(8,128)(2,1)S(1)}, u32[]{:S(2)}, u32[]{:S(2)}) collective-permute-start(bf16[48,1152]{1,0:T(8,128)(2,1)S(1)} %get-tuple-element.99), channel_id=1, source_target_pairs={{0,24},{1,25},{2,26},{3,27},{4,28},{5,29},{6,30},{7,31},{8,0},{9,1... | collective-permute-start | bytes 331784 | tf_op jit(solution)/shard_map/ppermute | solution.py:558
  360.3 5.5 %collective-permute-start.31 = (f32[24,1152]{1,0:T(8,128)S(1)}, f32[24,1152]{1,0:T(8,128)S(1)}, u32[]{:S(2)}, u32[]{:S(2)}) collective-permute-start(f32[24,1152]{1,0:T(8,128)S(1)} %get-tuple-element.106), channel_id=1, source_target_pairs={{0,1},{1,0},{2,3},{3,2},{4,5},{5,4},{6,7},{7,6},{8,9},{9,8},{10,11... | collective-permute-start | bytes 331784 | tf_op jit(solution)/shard_map/ppermute | solution.py:558
  362.2 8.1 %collective-permute-start.37 = (bf16[48,3456]{1,0:T(8,128)(2,1)S(1)}, bf16[48,3456]{1,0:T(8,128)(2,1)S(1)}, u32[]{:S(2)}, u32[]{:S(2)}) collective-permute-start(bf16[48,3456]{1,0:T(8,128)(2,1)S(1)} %get-tuple-element.90), channel_id=1, source_target_pairs={{0,8},{1,9},{2,10},{3,11},{4,12},{5,13},{6,14},{7,15},{8,16},{9,17... | collective-permute-start | bytes 995336 | tf_op jit(solution)/shard_map/ppermute | solution.py:558
  362.3 26.9 %collective-permute-start.38 = (bf16[48,3456]{1,0:T(8,128)(2,1)S(1)}, bf16[48,3456]{1,0:T(8,128)(2,1)S(1)}, u32[]{:S(2)}, u32[]{:S(2)}) collective-permute-start(bf16[48,3456]{1,0:T(8,128)(2,1)S(1)} %get-tuple-element.92), channel_id=1, source_target_pairs={{0,16},{1,17},{2,18},{3,19},{4,20},{5,21},{6,22},{7,23},{8,24},{9,... | collective-permute-start | bytes 995336 | tf_op jit(solution)/shard_map/ppermute | solution.py:558
  365.8 27.9 %collective-permute-start.39 = (bf16[48,3456]{1,0:T(8,128)(2,1)S(1)}, bf16[48,3456]{1,0:T(8,128)(2,1)S(1)}, u32[]{:S(2)}, u32[]{:S(2)}) collective-permute-start(bf16[48,3456]{1,0:T(8,128)(2,1)S(1)} %get-tuple-element.91), channel_id=1, source_target_pairs={{0,24},{1,25},{2,26},{3,27},{4,28},{5,29},{6,30},{7,31},{8,0},{9,1... | collective-permute-start | bytes 995336 | tf_op jit(solution)/shard_map/ppermute | solution.py:558
  394.0 3.3 collective-permute-start.42
  395.5 1.2 collective-permute-start.40
  395.6 2.5 collective-permute-start.41

commit v2 on v1

--- a/solution.py
+++ b/solution.py
@@ -133,16 +133,17 @@
     g_ref[1] = dk_s[...].astype(BF)
     g_ref[2] = dv_s[...].astype(BF)
 
-def attend_grad(qkv, grad, out_t, stat, qb=256):
-    slot, width = qkv.shape[1], qkv.shape[2]
-    pairs = width // 128
+def attend_grad(qkv, grad, out_t, stat, first, qb=256):
+    slot = qkv.shape[1]
+    pairs = out_t.shape[0] // 128
+    width = pairs * 128
     return pl.pallas_call(
         functools.partial(attend_grad_kernel, qb),
         name="attend_grad",
         grid=(pairs,),
         in_specs=[
-            pl.BlockSpec((3, slot, 128), lambda j: (0, 0, j)),
-            pl.BlockSpec((slot, 128), lambda j: (0, j)),
+            pl.BlockSpec((3, slot, 128), lambda j: (0, 0, j + first)),
+            pl.BlockSpec((slot, 128), lambda j: (0, j + first)),
             pl.BlockSpec((128, slot), lambda j: (j, 0)),
             pl.BlockSpec((1, 2, slot), lambda j: (j, 0, 0)),
         ],
@@ -158,7 +159,7 @@
             pltpu.VMEM((slot, 128), F32),
         ],
         compiler_params=params(),
-        cost_estimate=cost(pairs * 5 * slot * slot * 256, 16e6, pairs * 2 * slot * slot),
+        cost_estimate=cost(pairs * 5 * slot * slot * 256, 16e6 * pairs / 6, pairs * 2 * slot * slot),
     )(qkv, grad, out_t, stat)
 branch_scale = 1.0 / math.sqrt(48.0)
 norm_epsilon = 1e-05
@@ -248,19 +249,19 @@
         cost_estimate=cost(2 * t * d * 3 * d, 18e6),
     )(place, x, gain, shift, bias, *sources)
 
-def mix_kernel(n_src, place, attn_ref, x_ref, bias_ref, gain_ref, shift_ref, *rest):
-    sources, (mid_ref, low_ref, w_ref) = rest[:n_src], rest[n_src:]
+def mix_kernel(n_src, place, x_ref, bias_ref, gain_ref, shift_ref, *rest):
+    sources, parts, (mid_ref, low_ref, w_ref) = rest[:n_src], rest[n_src:-3], rest[-3:]
     @pl.when(pl.program_id(0) == 0)
     def _():
         assemble(place, sources, w_ref)
     d = x_ref.shape[1]
     w = w_ref[...].reshape(d, d)
-    mid = x_ref[...].astype(F32) + branch_scale * (mm(attn_ref[...], w) + bias_ref[...])
+    mid = x_ref[...].astype(F32) + branch_scale * (mm(jnp.concatenate([p[...] for p in parts], 1), w) + bias_ref[...])
     mid_ref[...] = mid
     n, _ = normalised(mid)
     low_ref[...] = (n * gain_ref[...] + shift_ref[...]).astype(BF)
 
-def mix(place, attn, x, bias, gain, shift, sources, blocks, column, rows=256):
+def mix(place, parts, x, bias, gain, shift, sources, blocks, column, rows=256):
     t, d = x.shape
     r, np_ = d // blocks, sources[0].shape[0]
     return pl.pallas_call(
@@ -271,9 +272,9 @@
             grid=(t // rows,),
             in_specs=[
                 pl.BlockSpec((rows, d), lambda i, p: (i, 0)),
-                pl.BlockSpec((rows, d), lambda i, p: (i, 0)),
                 whole((1, d)), whole((1, d)), whole((1, d)),
                 *[whole((np_, r, d // 2), (0, 0, column)) for s in sources],
+                *[pl.BlockSpec((rows, p.shape[1]), lambda i, p: (i, 0)) for p in parts],
             ],
             out_specs=[
                 pl.BlockSpec((rows, d), lambda i, p: (i, 0)),
@@ -288,7 +289,7 @@
         ],
         compiler_params=params(),
         cost_estimate=cost(2 * t * d * d, 9e6),
-    )(place, attn, x, bias, gain, shift, *sources)
+    )(place, x, bias, gain, shift, *sources, *parts)
 
 def mlp_kernel(n_src, blocks, rb, core, place, lens, mid_ref, low_ref, cot_ref, fb_ref, pb_ref, gain_ref, *rest):
     fcs, projs, rest = rest[:n_src], rest[n_src : 2 * n_src], rest[2 * n_src :]
@@ -428,12 +429,13 @@
         cost_estimate=cost(12 * t * d * 4 * d, 40e6, t * 4 * d),
     )(core, place, lens, mid, low, cot, fb, pb, gain, *[a for a, _ in fcs], *[a for a, _ in projs])
 
-def unmix_kernel(blocks, core, lens, gbr_ref, attn_ref, w_ref, ga_ref, send_ref, keep_ref):
+def unmix_kernel(core, lens, gbr_ref, w_ref, *rest):
+    parts, (ga_ref, send_ref, keep_ref) = rest[:-3], rest[-3:]
     t, d = gbr_ref.shape
     w = w_ref[...].reshape(d, d)
     seen = lax.broadcasted_iota(jnp.int32, (t, 1), 0) < lens[0]
     ga_ref[...] = jnp.where(seen, mm_nt(gbr_ref[...], w), 0.0).astype(BF)
-    dw = mm_tn(attn_ref[...], gbr_ref[...]).astype(BF)
+    dw = jnp.concatenate([mm_tn(p[...], gbr_ref[...]).astype(BF) for p in parts], 0)
     h = d // 2
     for half in range(2):
         @pl.when(core[0] == half)
@@ -441,32 +443,29 @@
             keep_ref[...] = dw[:, half * h : (half + 1) * h].reshape(keep_ref.shape)
             send_ref[...] = dw[:, (1 - half) * h : (2 - half) * h].reshape(send_ref.shape)
 
-def unmix(core, lens, gbr, attn, w, blocks):
+def unmix(core, lens, gbr, parts, w, blocks):
     t, d = gbr.shape
     smem = pl.BlockSpec(memory_space=pltpu.SMEM)
     piece = jax.ShapeDtypeStruct((blocks, d // blocks, d // 2), BF)
     return pl.pallas_call(
-        functools.partial(unmix_kernel, blocks),
+        unmix_kernel,
         name="unmix",
-        in_specs=[smem, smem] + [pl.BlockSpec(memory_space=pltpu.VMEM)] * 3,
+        in_specs=[smem, smem] + [pl.BlockSpec(memory_space=pltpu.VMEM)] * (2 + len(parts)),
         out_shape=[jax.ShapeDtypeStruct((t, d), BF), piece, piece],
         compiler_params=params(0),
         cost_estimate=cost(4 * t * d * d, 9e6),
-    )(core, lens, gbr, attn, w)
+    )(core, lens, gbr, w, *parts)
 
 def unproject_kernel(blocks, core, low_ref, g_ref, send_ref, keep_ref, sums_ref):
-    d = low_ref.shape[1]
-    r = d // blocks
+    d, w = low_ref.shape[1], g_ref.shape[2]
+    r, h = d // blocks, w // 2
     low_t = low_ref[...].T
-    q = mm(low_t, g_ref[0]).astype(BF).reshape(blocks, r, d)
-    v = mm(low_t, g_ref[2]).astype(BF).reshape(blocks, r, d)
-    k = mm(low_t, g_ref[1]).astype(BF).reshape(blocks, r, d)
-    h = d // 2
+    q, k, v = [mm(low_t, g_ref[part]).astype(BF).reshape(blocks, r, w) for part in range(3)]
     for half, refs in ((0, (keep_ref, send_ref)), (1, (send_ref, keep_ref))):
         @pl.when(core[0] == half)
         def _():
-            refs[0][:, :, :d] = q
-            refs[0][:, :, d:] = k[:, :, :h]
+            refs[0][:, :, :w] = q
+            refs[0][:, :, w:] = k[:, :, :h]
             refs[1][:, :, :h] = k[:, :, h:]
             refs[1][:, :, h:] = v
     for part in range(3):
@@ -474,20 +473,27 @@
 
 def unproject(core, low, g, blocks):
     t, d = low.shape
-    piece = jax.ShapeDtypeStruct((blocks, d // blocks, d // 2 * 3), BF)
+    w = g.shape[2]
+    piece = jax.ShapeDtypeStruct((blocks, d // blocks, w // 2 * 3), BF)
     return pl.pallas_call(
         functools.partial(unproject_kernel, blocks),
         name="unproject",
         in_specs=[pl.BlockSpec(memory_space=pltpu.SMEM)] + [pl.BlockSpec(memory_space=pltpu.VMEM)] * 2,
-        out_shape=[piece, piece, jax.ShapeDtypeStruct((3, d), F32)],
+        out_shape=[piece, piece, jax.ShapeDtypeStruct((3, w), F32)],
         compiler_params=params(0),
-        cost_estimate=cost(6 * t * d * d, 10e6),
+        cost_estimate=cost(6 * t * d * w, 10e6 * w / d),
     )(core, low, g)
 
-def final_kernel(x_ref, g_ref, w_ref, gmid_ref, gain_ref, out_ref, vec_ref):
+def final_kernel(x_ref, w_ref, gmid_ref, gain_ref, *rest):
+    parts, (out_ref, vec_ref) = rest[:-2], rest[-2:]
     d = x_ref.shape[1]
     w = w_ref[...].reshape(d, 3 * d)
-    gh = mm_nt(g_ref[0], w[:, :d]) + mm_nt(g_ref[1], w[:, d : 2 * d]) + mm_nt(g_ref[2], w[:, 2 * d :])
+    gh = jnp.zeros(x_ref.shape, F32)
+    at = 0
+    for g in parts:
+        for i in range(3):
+            gh = gh + mm_nt(g[i], w[:, i * d + at : i * d + at + g.shape[2]])
+        at += g.shape[2]
     n, scale = normalised(x_ref[...].astype(F32))
     out_ref[...] = (gmid_ref[...] + norm_pull(n, scale, gain_ref[...], gh)).astype(BF)
     @pl.when(pl.program_id(0) == 0)
@@ -496,7 +502,7 @@
     vec_ref[0:1] += jnp.sum(gh * n, axis=0, keepdims=True)
     vec_ref[1:2] += jnp.sum(gh, axis=0, keepdims=True)
 
-def final(x, g, w, gmid, gain, rows=256):
+def final(x, parts, w, gmid, gain, rows=256):
     t, d = x.shape
     return pl.pallas_call(
         final_kernel,
@@ -504,16 +510,16 @@
         grid=(t // rows,),
         in_specs=[
             pl.BlockSpec((rows, d), lambda i: (i, 0)),
-            pl.BlockSpec((3, rows, d), lambda i: (0, i, 0)),
             whole(w.shape),
             pl.BlockSpec((rows, d), lambda i: (i, 0)),
             whole((1, d)),
+            *[pl.BlockSpec((3, rows, g.shape[2]), lambda i: (0, i, 0)) for g in parts],
         ],
         out_specs=[pl.BlockSpec((rows, d), lambda i: (i, 0)), whole((2, d))],
         out_shape=[jax.ShapeDtypeStruct((t, d), BF), jax.ShapeDtypeStruct((2, d), F32)],
         compiler_params=params(),
         cost_estimate=cost(6 * t * d * d, 15e6),
-    )(x, g, w, gmid, gain)
+    )(x, w, gmid, gain, *parts)
 
 
 class Grid:
@@ -544,13 +550,12 @@
         for z0, x0, y0, c0 in self.places():
             mine = []
             for half in (c0, 1 - c0):
-                for kb in range(2):
-                    line = [half]
-                    for ka in range(2):
-                        for kz in range(self.z):
-                            kx, ky = (ka, kb) if half == 0 else (kb, ka)
-                            line.append((((z0 - kz) % self.z) * 2 + (x0 ^ kx)) * 2 + (y0 ^ ky))
-                    mine.append(line)
+                for ka, kb in ((0, 0), (1, 0), (0, 1), (1, 1)):
+                    kx, ky = (ka, kb) if half == 0 else (kb, ka)
+                    blocks = [
+                        (((z0 - kz) % self.z) * 2 + (x0 ^ kx)) * 2 + (y0 ^ ky) for kz in range(self.z)
+                    ]
+                    mine.append([half] + blocks)
             rows.append(mine)
         return np.array(rows, np.int32)
 
@@ -587,10 +592,12 @@
     return jnp.stack([pair] + [grid.up(pair, k) for k in range(1, grid.z)])
 
 
-def spread_rest(grid, stack):
-    two = jnp.concatenate([stack, grid.along(stack, 0)], 0)
-    far = grid.along(two, 1)
-    return [two, far, grid.other_core(two), grid.other_core(far)]
+def with_other(grid, sources):
+    return sources + [grid.other_core(s) for s in sources]
+
+
+def stage(*values):
+    return lax.optimization_barrier(values)
 
 
 def after(value, *earlier):
@@ -601,22 +608,49 @@
     return (a.astype(F32) + b.astype(F32)).astype(BF)
 
 
-def collect(grid, sends, keeps):
-    z, x, y, c = grid.here()
-    got = [grid.other_core(s) for s in sends]
-    own = jnp.concatenate([add(k, g) for k, g in zip(keeps, got)], 2)
-    blocks, r, w = own.shape
-    own = own.reshape(grid.z, 2, 2, r, w)
-    pick = lambda v, at, axis: lax.dynamic_index_in_dim(v, at, axis, keepdims=False)
-    away = jnp.where(c == 0, pick(own, 1 - x, 1), pick(own, 1 - y, 2))
-    stay = jnp.where(c == 0, pick(own, x, 1), pick(own, y, 2))
-    own = add(stay, grid.along(away, 0))
-    left = jnp.where(c == 0, y, x)
-    own = add(pick(own, left, 1), grid.along(pick(own, 1 - left, 1), 1))
-    total = pick(own, z, 0).astype(F32)
-    for k in range(1, grid.z):
-        total = total + grid.up(pick(own, (z + k) % grid.z, 0), k).astype(F32)
-    return total
+def pick(v, at, axis):
+    return lax.dynamic_index_in_dim(v, at, axis, keepdims=False)
+
+
+class Sum:
+    def __init__(self, grid, sends, keeps):
+        self.grid, self.keeps = grid, keeps
+        self.got = [grid.other_core(s) for s in sends]
+
+    def core(self):
+        grid = self.grid
+        z, x, y, c = grid.here()
+        own = jnp.concatenate([add(k, g) for k, g in zip(self.keeps, self.got)], 2)
+        own = own.reshape(grid.z, 2, 2, *own.shape[1:])
+        self.away = jnp.where(c == 0, pick(own, 1 - x, 1), pick(own, 1 - y, 2))
+        self.stay = jnp.where(c == 0, pick(own, x, 1), pick(own, y, 2))
+        return self.away
+
+    def near(self, *earlier):
+        self.got = self.grid.along(after(self.away, *earlier), 0)
+
+    def middle(self):
+        z, x, y, c = self.grid.here()
+        own = add(self.stay, self.got)
+        left = jnp.where(c == 0, y, x)
+        self.away, self.stay = pick(own, 1 - left, 1), pick(own, left, 1)
+        return self.away
+
+    def far(self, *earlier):
+        self.got = self.grid.along(after(self.away, *earlier), 1)
+
+    def last(self):
+        self.own = add(self.stay, self.got)
+        return self.own
+
+    def rows(self, *earlier):
+        grid = self.grid
+        z = grid.here()[0]
+        own = after(self.own, *earlier)
+        total = pick(own, z, 0).astype(F32)
+        for k in range(1, grid.z):
+            total = total + grid.up(pick(own, (z + k) % grid.z, 0), k).astype(F32)
+        return total
 
 
 def own_rows(grid, total):
@@ -636,9 +670,14 @@
     return jnp.concatenate([total[:, j * w : (j + 1) * w] for j in range(4)], 0)
 
 
-def gather_small(vectors):
+def gather_small(count, vectors):
     flat = jnp.concatenate([v.astype(F32) for v in vectors]).astype(BF)
-    full = lax.all_gather(flat, AXES, axis=0, tiled=False).astype(F32)
+    full = jnp.broadcast_to(flat, (count, flat.shape[0]))
+    return lax.all_to_all(full, AXES, 0, 0, tiled=True)
+
+
+def split_small(full, vectors):
+    full = full.astype(F32)
     out, at = [], 0
     for v in vectors:
         out.append(full[:, at : at + v.shape[0]].reshape(-1))
@@ -683,38 +722,56 @@
     d = tokens.shape[1]
     grid = Grid(mesh, out_weight.shape[0])
     blocks = grid.blocks
+    vectors = [norm1_gain, norm1_bias, qkv_bias, out_bias, norm2_gain, norm2_bias, fc_bias, proj_bias]
+    little_all = gather_small(grid.count, vectors)
     if grid.paired:
         place = jnp.asarray(grid.table())[lax.axis_index(AXES)]
         core = grid.here()[3].reshape(1).astype(jnp.int32)
-        stack_qkv = spread_z(grid, pair_rows(grid, qkv_weight))
+        pair_qkv = pair_rows(grid, qkv_weight)
         first = jnp.concatenate([pair_rows(grid, fc_weight), pair_rows(grid, out_weight)], 1)
         second = to_chunks(pair_rows(grid, proj_weight))
-        stack_qkv, first, second = lax.optimization_barrier((stack_qkv, first, second))
+        stack_qkv = spread_z(grid, pair_qkv)
+        stack_qkv, first, second = stage(stack_qkv, first, second)
+        near_qkv, far_qkv = grid.along(stack_qkv, 0), grid.along(stack_qkv, 1)
         stack_first = spread_z(grid, first)
-        qkv_sources = spread_rest(grid, stack_qkv)
-        first_sources = spread_rest(grid, stack_first)
-        second_sources = spread_rest(grid, spread_z(grid, after(second, stack_first)))
-        fcs, outs = [(s, 0) for s in first_sources], first_sources
-        out_at = 4
-        projs = [(s, 0) for s in second_sources]
+        near_qkv, little_all = stage(near_qkv, little_all)
+        last_qkv = grid.along(near_qkv, 1)
+        last_qkv, stack_first, second, far_qkv = stage(last_qkv, stack_first, second, far_qkv)
+        near_first, far_first = grid.along(stack_first, 0), grid.along(stack_first, 1)
+        stack_second = spread_z(grid, second)
+        qkv_sources = with_other(grid, [stack_qkv, near_qkv, far_qkv, last_qkv])
     else:
         place = jnp.asarray(np.array([[0, 0], [1, 0]], np.int32))
         core = jnp.zeros((1,), jnp.int32)
         full = lambda v: lax.all_gather(v, AXES, axis=0, tiled=True)
         qkv_sources = halves_of(full(qkv_weight))
-        fcs = [(s, 0) for s in halves_of(full(fc_weight))]
-        outs, out_at = halves_of(full(out_weight)), 0
-        wide = full(proj_weight)
-        projs = [(to_chunks(s[0])[None], 0) for s in halves_of(wide)]
-    gain_one, shift_one, bias_qv, bias_out, gain_two, shift_two, bias_fc, bias_proj = gather_small(
-        [norm1_gain, norm1_bias, qkv_bias, out_bias, norm2_gain, norm2_bias, fc_bias, proj_bias]
+    gain_one, shift_one, bias_qv, bias_out, gain_two, shift_two, bias_fc, bias_proj = split_small(
+        little_all, vectors
     )
     row = lambda v: v.reshape(1, d)
     bias_qkv = jnp.stack([bias_qv[:d], jnp.zeros((d,), F32), bias_qv[d:]])
     qkv, low_one, qkv_full = project(
         place, tokens, row(gain_one), row(shift_one), bias_qkv, qkv_sources, blocks
     )
-    mixed_t, mixed, stats = attend(seq_lengths, qkv, d // 128, 0, 512)
+    if grid.paired:
+        qkv, near_first, far_first, stack_second = stage(qkv, near_first, far_first, stack_second)
+        last_first = grid.along(near_first, 1)
+        near_second, far_second = grid.along(stack_second, 0), grid.along(stack_second, 1)
+    attended = [attend(seq_lengths, qkv, 4, 0, 512)]
+    if grid.paired:
+        qkv, near_second, far_second, last_first, _ = stage(
+            qkv, near_second, far_second, last_first, attended[0][2]
+        )
+        last_second = grid.along(near_second, 1)
+        outs = with_other(grid, [stack_first, near_first, far_first, last_first])
+        seconds = with_other(grid, [stack_second, near_second, far_second, last_second])
+        fcs, out_at, projs = [(s, 0) for s in outs], 4, [(s, 0) for s in seconds]
+    else:
+        fcs = [(s, 0) for s in halves_of(full(fc_weight))]
+        outs, out_at = halves_of(full(out_weight)), 0
+        projs = [(to_chunks(s[0])[None], 0) for s in halves_of(full(proj_weight))]
+    attended.append(attend(seq_lengths, qkv, 2, 4, 512))
+    mixed = [a[1] for a in attended]
     middle, low_two, out_full = mix(
         place, mixed, tokens, row(bias_out), row(gain_two), row(shift_two), outs, blocks, out_at
     )
@@ -723,47 +780,74 @@
         row(gain_two), fcs, projs, blocks,
     )
     grad_mixed, out_send, out_keep = unmix(core, seq_lengths, grad_branch, mixed, out_full, blocks)
-    grad_qkv = attend_grad(qkv, grad_mixed, mixed_t, stats)
-    qkv_send, qkv_keep, qkv_sums = unproject(core, low_one, grad_qkv, blocks)
-    input_grad, first_sums = final(tokens, grad_qkv, qkv_full, grad_middle, row(gain_one))
+    grads, dense, small_sums = [], [], []
     if grid.paired:
-        total = collect(grid, [fc_send, proj_send, out_send], [fc_keep, proj_keep, out_keep])
+        block_sum = Sum(grid, [fc_send, proj_send, out_send], [fc_keep, proj_keep, out_keep])
+        grad_mixed = after(grad_mixed, block_sum.core())
+        block_sum.near()
+    grads.append(attend_grad(qkv, grad_mixed, attended[0][0], attended[0][2], 0))
+    dense.append(unproject(core, low_one, grads[0], blocks))
+    if grid.paired:
+        large = Sum(grid, [dense[0][0]], [dense[0][1]])
+        grad_mixed = after(grad_mixed, block_sum.middle(), dense[0][2])
+        block_sum.far()
+    grads.append(attend_grad(qkv, grad_mixed, attended[1][0], attended[1][2], 4))
+    dense.append(unproject(core, low_one, grads[1], blocks))
+    if grid.paired:
+        small = Sum(grid, [dense[1][0]], [dense[1][1]])
+        large.core()
+        large.near(block_sum.last())
+        small.core()
+        small.near(large.away)
+        grad_middle = after(grad_middle, small.away, large.away)
+    input_grad, first_sums = final(tokens, grads, qkv_full, grad_middle, row(gain_one))
+    if grid.paired:
+        total = block_sum.rows()
+        large.middle()
+        large.far()
+        small.middle()
+        small.far()
+        large.last()
+        small.last()
         fc_wide, out_wide = fc_keep.shape[2], out_keep.shape[2]
         fc_weight_grad = own_rows(grid, total[:, :fc_wide])
         proj_weight_grad = own_rows(grid, from_chunks(total[:, fc_wide : 2 * fc_wide]))
         out_weight_grad = own_rows(grid, total[:, 2 * fc_wide :])
-        qkv_weight_grad = own_rows(grid, collect(grid, [qkv_send], [qkv_keep]))
+        ends = [own_rows(grid, large.rows()), own_rows(grid, small.rows())]
     else:
         reduce = lambda v: lax.psum_scatter(v.astype(F32), AXES, scatter_dimension=0, tiled=True)
         side = lambda k, s: jnp.concatenate([k[0], s[0]], 1)
         fc_weight_grad = reduce(side(fc_keep, fc_send))
         out_weight_grad = reduce(side(out_keep, out_send))
-        qkv_weight_grad = reduce(side(qkv_keep, qkv_send))
+        ends = [reduce(side(u[1], u[0])) for u in dense]
         proj_weight_grad = reduce(
             jnp.concatenate([from_chunks(proj_keep[0]), from_chunks(proj_send[0])], 1)
         )
-    small = scatter_small(
+    split = lambda e, i: e[:, i * e.shape[1] // 3 : (i + 1) * e.shape[1] // 3]
+    qkv_weight_grad = jnp.concatenate([split(e, i) for i in range(3) for e in ends], 1)
+    qkv_bias_term = jnp.concatenate([dense[p][2][i] for i in (0, 2) for p in range(2)])
+    little = scatter_small(
         grid.count,
         [
-            first_sums[0], first_sums[1], jnp.concatenate([qkv_sums[0], qkv_sums[2]]), sums[3],
+            first_sums[0], first_sums[1], qkv_bias_term, sums[3],
             sums[1], sums[2], fc_bias_term.reshape(-1), sums[0],
         ],
     )
     return (
         layer_out,
         input_grad,
-        small[0],
-        small[1],
+        little[0],
+        little[1],
         qkv_weight_grad,
-        small[2],
+        little[2],
         out_weight_grad,
-        small[3],
-        small[4],
-        small[5],
+        little[3],
+        little[4],
+        little[5],
         fc_weight_grad,
-        small[6],
+        little[6],
         proj_weight_grad,
-        small[7],
+        little[7],
     )
 
 

time: 407 us -> 384 us (0.943)
  blocking collectives: 37.5 us -> 0 us
  starting transfers between devices: 48 us -> 63.6 us
  waiting for transfers between devices: 110 us -> 95.2 us
  Pallas kernels: 144 us -> 151 us
  other arithmetic: 20.6 us -> 26.2 us
    all_gather x1 -> x0, blocking collectives: 37.5 us -> none  [gather_small(): full = lax.all_gather(flat, AXES, axis=0, tiled=False).astype(F32)]
    ppermute x43 -> x59, waiting for transfers between devices: 104 us -> 87.3 us  [send(): return lax.ppermute(value, AXES, self.perm(target))]
    ppermute x43 -> x59, starting transfers between devices: 37.9 us -> 52.5 us  [send(): return lax.ppermute(value, AXES, self.perm(target))]
    all_to_all x0 -> x1, waiting for transfers between devices: none -> 7.57 us  [gather_small(): return lax.all_to_all(full, AXES, 0, 0, tiled=True)]
    all_to_all x1, waiting for transfers between devices: 5.6 us -> 0.34 us  [scatter_small(): got = lax.all_to_all(jnp.concatenate(parts, 1), AXES, 0, 0, tiled=True)]
    all_to_all x0 -> x1, starting transfers between devices: none -> 5.14 us  [gather_small(): return lax.all_to_all(full, AXES, 0, 0, tiled=True)]
    convert_element_type x8 -> x11, other arithmetic: 10.7 us -> 15.4 us  [add(): return (a.astype(F32) + b.astype(F32)).astype(BF)]
    all_to_all x1, starting transfers between devices: 10.1 us -> 5.97 us  [scatter_small(): got = lax.all_to_all(jnp.concatenate(parts, 1), AXES, 0, 0, tiled=True)]
  transfers between devices with their start and end apart: 44 -> 61, of which waited for: 20 -> 24; matrix products, arithmetic and copies ran while one was open for 12% -> 13% of each run, Pallas kernels for 11% -> 24%
where the time goes in v2:
time: 384 us; the launch traced here: 379 us
  Pallas kernels  151 us (39%)
  waiting for transfers between devices  95.2 us (25%)
  starting transfers between devices  63.6 us (17%)
  local copies, waits for them, and re-layouts  40.3 us (10%)
  other arithmetic  26.2 us (7%)
    ppermute x59, waiting for transfers between devices, send(): return lax.ppermute(value, AXES, self.perm(target))  87.3 us
    pallas_call x1, Pallas kernels, mlp(): pl.pallas_call(functools.partial(mlp_kernel, len(fcs), blocks, rb), name=...  59 us
    ppermute x59, starting transfers between devices, send(): return lax.ppermute(value, AXES, self.perm(target))  52.5 us
    pallas_call x2, Pallas kernels, attend_grad(): pl.pallas_call(functools.partial(attend_grad_kernel, qb), name='attend_gr...  27.2 us
    pallas_call x2, Pallas kernels, attend(): pl.pallas_call(functools.partial(attend_kernel, qb), name='attend', grid=...  19.1 us
    convert_element_type x11, other arithmetic, add(): return (a.astype(F32) + b.astype(F32)).astype(BF)  15.4 us
    pallas_call x2, Pallas kernels, unproject(): pl.pallas_call(functools.partial(unproject_kernel, blocks), name='unproje...  11.4 us
    pallas_call x1, Pallas kernels, project(): pl.pallas_call(functools.partial(project_kernel, len(sources)), name='pro...  10.9 us
  transfers between devices with their start and end apart: 61, of which 24 were waited for; matrix products, arithmetic and copies ran while one was open for 13% of the time, Pallas kernels for 24%

profile of v2, /device:TPU:9, one launch (start us, length us, event | category | flops | bytes accessed | tf_op | source)
XLA Modules:
  0.0 378.6 jit_solution(16815207054242758097)
XLA Ops:
  5.7 1.3 collective-permute-start.1
  8.2 1.4 collective-permute-start.3
  9.9 6.2 %collective-permute-done.2 = bf16[48,1152]{1,0:T(8,128)(2,1)S(1)} collective-permute-done((bf16[48,1152]{1,0:T(8,128)(2,1)S(1)}, bf16[48,1152]{1,0:T(8,128)(2,1)S(1)}, u32[]{:S(2)}, u32[]{:S(2)}) %collective-permute-start.2) | collective-permute-done | bytes 110624 | tf_op jit(solution)/shard_map/ppermute | solution.py:563
  16.1 2.6 collective-permute-done.3
  18.8 1.3 collective-permute-start.7
  20.1 1.5 collective-permute-start.9
  21.6 2.3 collective-permute-start.10
  26.1 5.1 %all-to-all-start = ((bf16[32,2,144]{2,1,0:T(2,128)(2,1)}), bf16[32,2,144]{2,1,0:T(2,128)(2,1)S(1)}, u32[]{:S(2)}, u32[]{:S(2)}) async-start(bf16[32,2,144]{2,1,0:T(2,128)(2,1)} %reshape.139), calls=%async_computation | async-start | bytes 65536 | tf_op jit(solution)/shard_map/all_to_all | solution.py:676
  31.2 1.3 fusion.9.place
  32.6 7.6 %all-to-all-done = bf16[32,2,144]{2,1,0:T(2,128)(2,1)S(1)} async-done(((bf16[32,2,144]{2,1,0:T(2,128)(2,1)}), bf16[32,2,144]{2,1,0:T(2,128)(2,1)S(1)}, u32[]{:S(2)}, u32[]{:S(2)}) %all-to-all-start) | async-done | bytes 18464 | tf_op jit(solution)/shard_map/all_to_all | solution.py:676
  40.6 1.5 collective-permute-start.13
  43.3 4.5 %collective-permute-done.12.rest_2_ = bf16[4,48,1152]{2,1,0:T(8,128)(2,1)S(1)} collective-permute-done((bf16[4,48,1152]{2,1,0:T(8,128)(2,1)S(1)}, bf16[4,48,1152]{2,1,0:T(8,128)(2,1)S(1)}, u32[]{:S(2)}, u32[]{:S(2)}) %collective-permute-start.12) | collective-permute-done | bytes 442400 | tf_op jit(solution)/shard_map/ppermute | solution.py:563
  48.6 4.1 %collective-permute-done.8.rest_3_ = bf16[4,48,1152]{2,1,0:T(8,128)(2,1)} collective-permute-done((bf16[4,48,1152]{2,1,0:T(8,128)(2,1)}, bf16[4,48,1152]{2,1,0:T(8,128)(2,1)}, u32[]{:S(2)}, u32[]{:S(2)}) %collective-permute-start.8) | collective-permute-done | bytes 442400 | tf_op jit(solution)/shard_map/ppermute | solution.py:563
  52.6 1.4 collective-permute-start.19
  54.1 1.8 collective-permute-start.20
  59.8 6.1 %collective-permute-done.20 = bf16[48,1536]{1,0:T(8,128)(2,1)S(1)} collective-permute-done((bf16[48,1536]{1,0:T(8,128)(2,1)S(1)}, bf16[48,1536]{1,0:T(8,128)(2,1)S(1)}, u32[]{:S(2)}, u32[]{:S(2)}) %collective-permute-start.20) | collective-permute-done | bytes 147488 | tf_op jit(solution)/shard_map/ppermute | solution.py:563
  65.9 1.9 collective-permute-start.15
  72.7 10.9 %project.1 = (bf16[3,1024,768]{2,1,0:T(8,128)(2,1)}, bf16[1024,768]{1,0:T(8,128)(2,1)}, bf16[16,48,2304]{2,1,0:T(8,128)(2,1)}) custom-call(s32[8,5]{1,0:T(8,128)} %fusion.9.place, bf16[1024,768]{1,0:T(8,128)(2,1)} %x_ref.5, f32[1,768]{1,0:T(1,128)} %reshape_reshape.29.gain_ref, f32[1,768]{1,0:T(1,128)} %reshape_reshape.30.shift_ref, ...), custom_call_target="tpu_custom_call" | custom-call | flops 3623878656 | bytes 18000000 | tf_op jit(solution)/shard_map/project/pallas_call | solution.py:226
  87.6 11.0 %collective-permute-done.22.rest_9_ = bf16[4,48,1536]{2,1,0:T(8,128)(2,1)} collective-permute-done((bf16[4,48,1536]{2,1,0:T(8,128)(2,1)}, bf16[4,48,1536]{2,1,0:T(8,128)(2,1)}, u32[]{:S(2)}, u32[]{:S(2)}) %collective-permute-start.22) | collective-permute-done | bytes 589856 | tf_op jit(solution)/shard_map/ppermute | solution.py:563
  98.6 1.3 collective-permute-start.27
  99.9 12.1 %attend.2 = (f32[512,1024]{1,0:T(8,128)}, bf16[1024,512]{1,0:T(8,128)(2,1)}, f32[4,2,1024]{2,1,0:T(2,128)}) custom-call(s32[1]{0:T(128)S(6)} %copy.98.len_ref.lens, bf16[3,1024,768]{2,1,0:T(8,128)(2,1)} %get-tuple-element.85.qkv_ref), custom_call_target="tpu_custom_call" | custom-call | flops 2147483648 | bytes 5333333 | tf_op jit(solution)/shard_map/attend/pallas_call | solution.py:67
  112.3 1.5 collective-permute-start.28
  114.4 7.0 %collective-permute-done.29.rest_11_ = bf16[4,48,1536]{2,1,0:T(8,128)(2,1)} collective-permute-done((bf16[4,48,1536]{2,1,0:T(8,128)(2,1)}, bf16[4,48,1536]{2,1,0:T(8,128)(2,1)}, u32[]{:S(2)}, u32[]{:S(2)}) %collective-permute-start.29) | collective-permute-done | bytes 589856 | tf_op jit(solution)/shard_map/ppermute | solution.py:563
  125.7 7.0 %attend.3 = (f32[256,1024]{1,0:T(8,128)}, bf16[1024,256]{1,0:T(8,128)(2,1)}, f32[2,2,1024]{2,1,0:T(2,128)}) custom-call(s32[1]{0:T(128)S(6)} %copy.98.len_ref.lens, bf16[3,1024,768]{2,1,0:T(8,128)(2,1)} %get-tuple-element.85.qkv_ref), custom_call_target="tpu_custom_call" | custom-call | flops 1073741824 | bytes 2666666 | tf_op jit(solution)/shard_map/attend/pallas_call | solution.py:67
  132.7 7.0 %mix.1 = (f32[1024,768]{1,0:T(8,128)}, bf16[1024,768]{1,0:T(8,128)(2,1)}, bf16[16,48,768]{2,1,0:T(8,128)(2,1)}) custom-call(s32[8,5]{1,0:T(8,128)} %fusion.9.place, bf16[1024,768]{1,0:T(8,128)(2,1)} %x_ref.5, f32[1,768]{1,0:T(1,128)} %reshape_reshape.26.bias_ref, f32[1,768]{1,0:T(1,128)} %reshape_reshape.27.gain_ref, f32[1,768]{1,0:T(1,128)} %reshape_reshape.28.shift_ref, ...), custom_call_target="tpu_custom_call" | custom-call | flops 1207959552 | bytes 9000000 | tf_op jit(solution)/shard_map/mix/pallas_call | solution.py:267
  140.9 59.0 %mlp.1 = (bf16[1024,768]{1,0:T(8,128)(2,1)}, f32[1024,768]{1,0:T(8,128)}, bf16[1024,768]{1,0:T(8,128)(2,1)}, bf16[16,48,1536]{2,1,0:T(8,128)(2,1)}, bf16[16,48,1...) custom-call(s32[1]{0:T(128)} %bitcast.core, ...), custom_call_target="tpu_custom_call" | custom-call | flops 28991029248 | bytes 40000000 | tf_op jit(solution)/shard_map/mlp/pallas_call | solution.py:394
  200.5 6.6 %unmix.1 = (bf16[1024,768]{1,0:T(8,128)(2,1)}, bf16[16,48,384]{2,1,0:T(8,128)(2,1)}, bf16[16,48,384]{2,1,0:T(8,128)(2,1)}) custom-call(s32[1]{0:T(128)} %bitcast.core, s32[1]{0:T(128)S(6)} %copy.98.len_ref.lens, bf16[1024,768]{1,0:T(8,128)(2,1)} %get-tuple-element.95.gbr_ref, bf16[16,48,768]{2,1,0:T(8,128)(2,1)} %get-tuple-element.96.w_ref, ...), custom_call_target="tpu_custom_call" | custom-call | flops 2415919104 | bytes 9000000 | tf_op jit(solution)/shard_map/unmix/pallas_call | solution.py:450
  207.3 2.1 collective-permute-done.36
  210.6 2.5 add_convert_fusion.2
  213.2 2.4 add_convert_fusion.1
  216.2 1.9 constant_dynamic-slice_fusion.19
  218.1 1.9 constant_dynamic-slice_fusion.18
  220.0 1.9 bitcast_select_fusion.1
  221.9 1.4 collective-permute-start.37
  226.1 17.1 %attend_grad.2.g_ref.rest_0_ = bf16[3,1024,512]{2,1,0:T(8,128)(2,1)} custom-call(bf16[3,1024,768]{2,1,0:T(8,128)(2,1)} %get-tuple-element.85.qkv_ref, bf16[1024,768]{1,0:T(8,128)(2,1)} %get-tuple-element.107.grad_ref, f32[512,1024]{1,0:T(8,128)} %get-tuple-element.105.out_t_ref, f32[4,2,1024]{2,1,0:T(2,128)} %get-tuple-element.82.stat_ref), custom_call_target="tpu_custom_call" | custom-call | flops 5368709120 | bytes 10666666 | tf_op jit(solution)/shard_map/attend_grad/pallas_call | solution.py:140
  243.3 6.8 %unproject.2 = (bf16[16,48,768]{2,1,0:T(8,128)(2,1)}, bf16[16,48,768]{2,1,0:T(8,128)(2,1)}, f32[3,512]{1,0:T(4,128)}) custom-call(s32[1]{0:T(128)} %bitcast.core, bf16[1024,768]{1,0:T(8,128)(2,1)} %get-tuple-element.94.low_ref, bf16[3,1024,512]{2,1,0:T(8,128)(2,1)} %attend_grad.2.g_ref.rest_0_), custom_call_target="tpu_custom_call" | custom-call | flops 2415919104 | bytes 6666666 | tf_op jit(solution)/shard_map/unproject/pallas_call | solution.py:478
  250.9 2.4 collective-permute-done.37
  253.2 1.6 copy-done.2
  254.8 3.5 add_convert_fusion
  259.5 10.0 %attend_grad.3.g_ref.rest_1_ = bf16[3,1024,256]{2,1,0:T(8,128)(2,1)} custom-call(bf16[3,1024,768]{2,1,0:T(8,128)(2,1)} %get-tuple-element.85.qkv_ref, bf16[1024,768]{1,0:T(8,128)(2,1)} %get-tuple-element.107.grad_ref, f32[256,1024]{1,0:T(8,128)} %get-tuple-element.108.out_t_ref, f32[2,2,1024]{2,1,0:T(2,128)} %get-tuple-element.109.stat_ref), custom_call_target="tpu_custom_call" | custom-call | flops 2684354560 | bytes 5333333 | tf_op jit(solution)/shard_map/attend_grad/pallas_call | solution.py:140
  269.5 4.6 %unproject.3 = (bf16[16,48,384]{2,1,0:T(8,128)(2,1)}, bf16[16,48,384]{2,1,0:T(8,128)(2,1)}, f32[3,256]{1,0:T(4,128)}) custom-call(s32[1]{0:T(128)} %bitcast.core, bf16[1024,768]{1,0:T(8,128)(2,1)} %get-tuple-element.94.low_ref, bf16[3,1024,256]{2,1,0:T(8,128)(2,1)} %attend_grad.3.g_ref.rest_1_), custom_call_target="tpu_custom_call" | custom-call | flops 1207959552 | bytes 3333333 | tf_op jit(solution)/shard_map/unproject/pallas_call | solution.py:478
  275.1 1.6 add_convert_fusion.3
  280.6 1.5 collective-permute-start.47
  282.7 1.4 reshape.125
  284.1 5.8 %collective-permute-done.47 = bf16[4,2,48,384]{3,2,0,1:T(8,128)(2,1)} collective-permute-done((bf16[4,2,48,384]{3,2,0,1:T(8,128)(2,1)S(1)}, bf16[4,2,48,384]{3,2,0,1:T(8,128)(2,1)}, u32[]{:S(2)}, u32[]{:S(2)}) %collective-permute-start.47) | collective-permute-done | bytes 294944 | tf_op jit(solution)/shard_map/ppermute | solution.py:563
  289.9 1.3 add_convert_fusion.7
  293.0 9.6 %final.1 = (bf16[1024,768]{1,0:T(8,128)(2,1)}, f32[2,768]{1,0:T(2,128)}) custom-call(bf16[1024,768]{1,0:T(8,128)(2,1)} %x_ref.5, bf16[16,48,2304]{2,1,0:T(8,128)(2,1)} %get-tuple-element.92.w_ref, f32[1024,768]{1,0:T(8,128)} %get-tuple-element.114.gmid_ref, f32[1,768]{1,0:T(1,128)} %reshape_reshape.29.gain_ref, ...), custom_call_target="tpu_custom_call" | custom-call | flops 3623878656 | bytes 15000000 | tf_op jit(solution)/shard_map/final/pallas_call | solution.py:507
  302.7 1.4 slice_reduce_fusion.4
  304.0 1.4 reshape_squeeze.18
  305.4 1.4 reshape_squeeze.19
  306.8 1.5 concatenate.118
  308.3 1.5 all_to_all.14
  309.8 6.0 %all-to-all-start.1 = ((f32[32,1,288]{2,1,0:T(1,128)}), f32[32,1,288]{2,1,0:T(1,128)}, u32[]{:S(2)}, u32[]{:S(2)}) async-start(f32[32,1,288]{2,1,0:T(1,128)} %all_to_all.14), calls=%async_computation.1 | async-start | bytes 98304 | tf_op jit(solution)/shard_map/all_to_all | solution.py:690
  319.7 1.4 collective-permute-start.51
  325.5 1.6 fusion
  328.4 2.3 collective-permute-start.54
  333.7 1.3 collective-permute-start.41
  334.9 1.8 collective-permute-done.53
  336.7 20.2 %collective-permute-done.54 = bf16[48,3456]{1,0:T(8,128)(2,1)S(1)} collective-permute-done((bf16[48,3456]{1,0:T(8,128)(2,1)S(1)}, bf16[48,3456]{1,0:T(8,128)(2,1)S(1)}, u32[]{:S(2)}, u32[]{:S(2)}) %collective-permute-start.54) | collective-permute-done | bytes 331808 | tf_op jit(solution)/shard_map/ppermute | solution.py:563
  356.9 3.3 collective-permute-done.55
  364.2 3.2 collective-permute-done.42
  367.8 1.4 collective-permute-start.45
  371.9 2.6 collective-permute-done.45
  374.6 2.0 collective-permute-start.46
  (246 shorter events, 65.4 us)
Async XLA Ops:
  1.7 7.9 %collective-permute-start.6 = (bf16[96,384]{1,0:T(8,128)(2,1)S(1)}, bf16[96,384]{1,0:T(8,128)(2,1)S(1)}, u32[]{:S(2)}, u32[]{:S(2)}) collective-permute-start(bf16[96,384]{1,0:T(8,128)(2,1)S(1)} %get-tuple-element.165), channel_id=1, source_target_pairs={{0,1},{1,0},{2,3},{3,2},{4,5},{5,4},{6,7},{7,6},{8,9},{9,8},{10,11... | collective-permute-start | bytes 221192 | tf_op jit(solution)/shard_map/ppermute | solution.py:563
  3.3 2.4 collective-permute-start
  4.2 1.5 collective-permute-start.5
  5.6 4.1 %collective-permute-start.4 = (bf16[24,1536]{1,0:T(8,128)(2,1)S(1)}, bf16[24,1536]{1,0:T(8,128)(2,1)S(1)}, u32[]{:S(2)}, u32[]{:S(2)}) collective-permute-start(bf16[24,1536]{1,0:T(8,128)(2,1)S(1)} %get-tuple-element.167), channel_id=1, source_target_pairs={{0,1},{1,0},{2,3},{3,2},{4,5},{5,4},{6,7},{7,6},{8,9},{9,8},{10,11... | collective-permute-start | bytes 221192 | tf_op jit(solution)/shard_map/ppermute | solution.py:563
  5.7 4.2 %collective-permute-start.1 = (bf16[48,1152]{1,0:T(8,128)(2,1)S(1)}, bf16[48,1152]{1,0:T(8,128)(2,1)S(1)}, u32[]{:S(2)}, u32[]{:S(2)}) collective-permute-start(bf16[48,1152]{1,0:T(8,128)(2,1)S(1)} %maximum_select_fusion.6), channel_id=1, source_target_pairs={{0,8},{1,9},{2,10},{3,11},{4,12},{5,13},{6,14},{7,15},{8,16},{9,17... | collective-permute-start | bytes 331784 | tf_op jit(solution)/shard_map/ppermute | solution.py:563
  7.1 9.1 %collective-permute-start.2 = (bf16[48,1152]{1,0:T(8,128)(2,1)S(1)}, bf16[48,1152]{1,0:T(8,128)(2,1)S(1)}, u32[]{:S(2)}, u32[]{:S(2)}) collective-permute-start(bf16[48,1152]{1,0:T(8,128)(2,1)S(1)} %maximum_select_fusion.6), channel_id=1, source_target_pairs={{0,16},{1,17},{2,18},{3,19},{4,20},{5,21},{6,22},{7,23},{8,24},{9,... | collective-permute-start | bytes 331784 | tf_op jit(solution)/shard_map/ppermute | solution.py:563
  8.2 10.6 %collective-permute-start.3 = (bf16[48,1152]{1,0:T(8,128)(2,1)S(1)}, bf16[48,1152]{1,0:T(8,128)(2,1)S(1)}, u32[]{:S(2)}, u32[]{:S(2)}) collective-permute-start(bf16[48,1152]{1,0:T(8,128)(2,1)S(1)} %maximum_select_fusion.6), channel_id=1, source_target_pairs={{0,24},{1,25},{2,26},{3,27},{4,28},{5,29},{6,30},{7,31},{8,0},{9,1... | collective-permute-start | bytes 331784 | tf_op jit(solution)/shard_map/ppermute | solution.py:563
  18.8 52.4 %copy-start.16 = (bf16[4,48,1152]{2,1,0:T(8,128)(2,1)}, bf16[4,48,1152]{2,1,0:T(8,128)(2,1)S(1)}, u32[]{:S(2)}) copy-start(bf16[4,48,1152]{2,1,0:T(8,128)(2,1)S(1)} %pad_maximum_fusion.3.rest_0_) | copy-start | bytes 1327108
  18.8 21.8 %collective-permute-start.7 = (bf16[4,48,1152]{2,1,0:T(8,128)(2,1)S(1)}, bf16[4,48,1152]{2,1,0:T(8,128)(2,1)}, u32[]{:S(2)}, u32[]{:S(2)}) collective-permute-start(bf16[4,48,1152]{2,1,0:T(8,128)(2,1)S(1)} %pad_maximum_fusion.3.rest_0_), channel_id=1, source_target_pairs={{0,4},{1,3},{2,6},{3,1},{4,0},{5,7},{6,2},{7,5},{8,12},{9,11},{10,... | collective-permute-start | bytes 1327112 | tf_op jit(solution)/shard_map/ppermute | solution.py:563
  20.1 22.1 %collective-permute-start.11 = (bf16[48,1920]{1,0:T(8,128)(2,1)S(1)}, bf16[48,1920]{1,0:T(8,128)(2,1)S(1)}, u32[]{:S(2)}, u32[]{:S(2)}) collective-permute-start(bf16[48,1920]{1,0:T(8,128)(2,1)S(1)} %pad_maximum_fusion.5), channel_id=1, source_target_pairs={{0,24},{1,25},{2,26},{3,27},{4,28},{5,29},{6,30},{7,31},{8,0},{9,1... | collective-permute-start | bytes 552968 | tf_op jit(solution)/shard_map/ppermute | solution.py:563
  20.1 22.4 %collective-permute-start.9 = (bf16[48,1920]{1,0:T(8,128)(2,1)S(1)}, bf16[48,1920]{1,0:T(8,128)(2,1)S(1)}, u32[]{:S(2)}, u32[]{:S(2)}) collective-permute-start(bf16[48,1920]{1,0:T(8,128)(2,1)S(1)} %pad_maximum_fusion.5), channel_id=1, source_target_pairs={{0,8},{1,9},{2,10},{3,11},{4,12},{5,13},{6,14},{7,15},{8,16},{9,17... | collective-permute-start | bytes 552968 | tf_op jit(solution)/shard_map/ppermute | solution.py:563
  21.6 21.0 %collective-permute-start.10 = (bf16[48,1920]{1,0:T(8,128)(2,1)S(1)}, bf16[48,1920]{1,0:T(8,128)(2,1)S(1)}, u32[]{:S(2)}, u32[]{:S(2)}) collective-permute-start(bf16[48,1920]{1,0:T(8,128)(2,1)S(1)} %pad_maximum_fusion.5), channel_id=1, source_target_pairs={{0,16},{1,17},{2,18},{3,19},{4,20},{5,21},{6,22},{7,23},{8,24},{9,... | collective-permute-start | bytes 552968 | tf_op jit(solution)/shard_map/ppermute | solution.py:563
  26.1 14.1 %all-to-all-start = ((bf16[32,2,144]{2,1,0:T(2,128)(2,1)}), bf16[32,2,144]{2,1,0:T(2,128)(2,1)S(1)}, u32[]{:S(2)}, u32[]{:S(2)}) async-start(bf16[32,2,144]{2,1,0:T(2,128)(2,1)} %reshape.139), calls=%async_computation | async-start | bytes 65536 | tf_op jit(solution)/shard_map/all_to_all | solution.py:676
  40.3 7.5 %collective-permute-start.12 = (bf16[4,48,1152]{2,1,0:T(8,128)(2,1)S(1)}, bf16[4,48,1152]{2,1,0:T(8,128)(2,1)S(1)}, u32[]{:S(2)}, u32[]{:S(2)}) collective-permute-start(bf16[4,48,1152]{2,1,0:T(8,128)(2,1)S(1)} %pad_maximum_fusion.3.rest_0_), channel_id=1, source_target_pairs={{0,2},{1,5},{2,0},{3,7},{4,6},{5,1},{6,4},{7,3},{8,10},{9,13},{10,... | collective-permute-start | bytes 1327112 | tf_op jit(solution)/shard_map/ppermute | solution.py:563
  40.6 17.7 %collective-permute-start.13 = (bf16[4,48,1152]{2,1,0:T(8,128)(2,1)S(1)}, bf16[4,48,1152]{2,1,0:T(8,128)(2,1)S(1)}, u32[]{:S(2)}, u32[]{:S(2)}) collective-permute-start(bf16[4,48,1152]{2,1,0:T(8,128)(2,1)S(1)} %pad_maximum_fusion.3.rest_0_), channel_id=1, source_target_pairs={{0,1},{1,0},{2,3},{3,2},{4,5},{5,4},{6,7},{7,6},{8,9},{9,8},{10,11... | collective-permute-start | bytes 1327112 | tf_op jit(solution)/shard_map/ppermute | solution.py:563
  42.2 10.5 %collective-permute-start.8 = (bf16[4,48,1152]{2,1,0:T(8,128)(2,1)}, bf16[4,48,1152]{2,1,0:T(8,128)(2,1)}, u32[]{:S(2)}, u32[]{:S(2)}) collective-permute-start(bf16[4,48,1152]{2,1,0:T(8,128)(2,1)} %collective-permute-done.7.rest_1_), channel_id=1, source_target_pairs={{0,2},{1,5},{2,0},{3,7},{4,6},{5,1},{6,4},{7,3},{8,10},{9,13},{10,... | collective-permute-start | bytes 1327112 | tf_op jit(solution)/shard_map/ppermute | solution.py:563
  42.7 44.3 %copy-start.1 = (bf16[4,48,1920]{2,1,0:T(8,128)(2,1)}, bf16[4,48,1920]{2,1,0:T(8,128)(2,1)S(1)}, u32[]{:S(2)}) copy-start(bf16[4,48,1920]{2,1,0:T(8,128)(2,1)S(1)} %pad_maximum_fusion.1.rest_0_) | copy-start | bytes 2211844
  42.7 28.5 %collective-permute-start.14 = (bf16[4,48,1152]{2,1,0:T(8,128)(2,1)}, bf16[4,48,1152]{2,1,0:T(8,128)(2,1)}, u32[]{:S(2)}, u32[]{:S(2)}) collective-permute-start(bf16[4,48,1152]{2,1,0:T(8,128)(2,1)} %collective-permute-done.7.rest_1_), channel_id=1, source_target_pairs={{0,1},{1,0},{2,3},{3,2},{4,5},{5,4},{6,7},{7,6},{8,9},{9,8},{10,11... | collective-permute-start | bytes 1327112 | tf_op jit(solution)/shard_map/ppermute | solution.py:563
  52.6 6.9 %collective-permute-start.19 = (bf16[48,1536]{1,0:T(8,128)(2,1)S(1)}, bf16[48,1536]{1,0:T(8,128)(2,1)S(1)}, u32[]{:S(2)}, u32[]{:S(2)}) collective-permute-start(bf16[48,1536]{1,0:T(8,128)(2,1)S(1)} %pad_maximum_fusion.6), channel_id=1, source_target_pairs={{0,8},{1,9},{2,10},{3,11},{4,12},{5,13},{6,14},{7,15},{8,16},{9,17... | collective-permute-start | bytes 442376 | tf_op jit(solution)/shard_map/ppermute | solution.py:563
  54.1 11.8 %collective-permute-start.20 = (bf16[48,1536]{1,0:T(8,128)(2,1)S(1)}, bf16[48,1536]{1,0:T(8,128)(2,1)S(1)}, u32[]{:S(2)}, u32[]{:S(2)}) collective-permute-start(bf16[48,1536]{1,0:T(8,128)(2,1)S(1)} %pad_maximum_fusion.6), channel_id=1, source_target_pairs={{0,16},{1,17},{2,18},{3,19},{4,20},{5,21},{6,22},{7,23},{8,24},{9,... | collective-permute-start | bytes 442376 | tf_op jit(solution)/shard_map/ppermute | solution.py:563
  55.9 12.5 %collective-permute-start.21 = (bf16[48,1536]{1,0:T(8,128)(2,1)S(1)}, bf16[48,1536]{1,0:T(8,128)(2,1)S(1)}, u32[]{:S(2)}, u32[]{:S(2)}) collective-permute-start(bf16[48,1536]{1,0:T(8,128)(2,1)S(1)} %pad_maximum_fusion.6), channel_id=1, source_target_pairs={{0,24},{1,25},{2,26},{3,27},{4,28},{5,29},{6,30},{7,31},{8,0},{9,1... | collective-permute-start | bytes 442376 | tf_op jit(solution)/shard_map/ppermute | solution.py:563
  58.3 25.3 %collective-permute-start.17 = (bf16[4,48,1920]{2,1,0:T(8,128)(2,1)S(1)}, bf16[4,48,1920]{2,1,0:T(8,128)(2,1)S(1)}, u32[]{:S(2)}, u32[]{:S(2)}) collective-permute-start(bf16[4,48,1920]{2,1,0:T(8,128)(2,1)S(1)} %pad_maximum_fusion.1.rest_0_), channel_id=1, source_target_pairs={{0,4},{1,3},{2,6},{3,1},{4,0},{5,7},{6,2},{7,5},{8,12},{9,11},{10,... | collective-permute-start | bytes 2211848 | tf_op jit(solution)/shard_map/ppermute | solution.py:563
  59.5 24.2 %collective-permute-start.18 = (bf16[4,48,1920]{2,1,0:T(8,128)(2,1)S(1)}, bf16[4,48,1920]{2,1,0:T(8,128)(2,1)S(1)}, u32[]{:S(2)}, u32[]{:S(2)}) collective-permute-start(bf16[4,48,1920]{2,1,0:T(8,128)(2,1)S(1)} %pad_maximum_fusion.1.rest_0_), channel_id=1, source_target_pairs={{0,2},{1,5},{2,0},{3,7},{4,6},{5,1},{6,4},{7,3},{8,10},{9,13},{10,... | collective-permute-start | bytes 2211848 | tf_op jit(solution)/shard_map/ppermute | solution.py:563
  65.9 5.3 %collective-permute-start.15 = (bf16[4,48,1152]{2,1,0:T(8,128)(2,1)}, bf16[4,48,1152]{2,1,0:T(8,128)(2,1)S(1)}, u32[]{:S(2)}, u32[]{:S(2)}) collective-permute-start(bf16[4,48,1152]{2,1,0:T(8,128)(2,1)} %copy-done.32), channel_id=1, source_target_pairs={{0,1},{1,0},{2,3},{3,2},{4,5},{5,4},{6,7},{7,6},{8,9},{9,8},{10,11... | collective-permute-start | bytes 1327112 | tf_op jit(solution)/shard_map/ppermute | solution.py:563
  68.4 2.8 collective-permute-start.16
  83.7 28.3 %copy-start.7 = (bf16[4,48,1920]{2,1,0:T(8,128)(2,1)}, bf16[4,48,1920]{2,1,0:T(8,128)(2,1)S(1)}, u32[]{:S(2)}) copy-start(bf16[4,48,1920]{2,1,0:T(8,128)(2,1)S(1)} %collective-permute-done.17.rest_1_) | copy-start | bytes 2211844
  83.7 15.0 %collective-permute-start.22 = (bf16[4,48,1536]{2,1,0:T(8,128)(2,1)}, bf16[4,48,1536]{2,1,0:T(8,128)(2,1)}, u32[]{:S(2)}, u32[]{:S(2)}) collective-permute-start(bf16[4,48,1536]{2,1,0:T(8,128)(2,1)} %pad_maximum_fusion.2.rest_8_), channel_id=1, source_target_pairs={{0,4},{1,3},{2,6},{3,1},{4,0},{5,7},{6,2},{7,5},{8,12},{9,11},{10,... | collective-permute-start | bytes 1769480 | tf_op jit(solution)/shard_map/ppermute | solution.py:563
  84.9 27.1 %collective-permute-start.24 = (bf16[4,48,1920]{2,1,0:T(8,128)(2,1)S(1)}, bf16[4,48,1920]{2,1,0:T(8,128)(2,1)S(1)}, u32[]{:S(2)}, u32[]{:S(2)}) collective-permute-start(bf16[4,48,1920]{2,1,0:T(8,128)(2,1)S(1)} %collective-permute-done.17.rest_1_), channel_id=1, source_target_pairs={{0,2},{1,5},{2,0},{3,7},{4,6},{5,1},{6,4},{7,3},{8,10},{9,13},{10,... | collective-permute-start | bytes 2211848 | tf_op jit(solution)/shard_map/ppermute | solution.py:563
  85.2 26.8 %collective-permute-start.23 = (bf16[4,48,1536]{2,1,0:T(8,128)(2,1)}, bf16[4,48,1536]{2,1,0:T(8,128)(2,1)}, u32[]{:S(2)}, u32[]{:S(2)}) collective-permute-start(bf16[4,48,1536]{2,1,0:T(8,128)(2,1)} %pad_maximum_fusion.2.rest_8_), channel_id=1, source_target_pairs={{0,2},{1,5},{2,0},{3,7},{4,6},{5,1},{6,4},{7,3},{8,10},{9,13},{10,... | collective-permute-start | bytes 1769480 | tf_op jit(solution)/shard_map/ppermute | solution.py:563
  87.0 26.8 %collective-permute-start.25 = (bf16[4,48,1920]{2,1,0:T(8,128)(2,1)S(1)}, bf16[4,48,1920]{2,1,0:T(8,128)(2,1)S(1)}, u32[]{:S(2)}, u32[]{:S(2)}) collective-permute-start(bf16[4,48,1920]{2,1,0:T(8,128)(2,1)S(1)} %pad_maximum_fusion.1.rest_0_), channel_id=1, source_target_pairs={{0,1},{1,0},{2,3},{3,2},{4,5},{5,4},{6,7},{7,6},{8,9},{9,8},{10,11... | collective-permute-start | bytes 2211848 | tf_op jit(solution)/shard_map/ppermute | solution.py:563
  87.1 26.8 %collective-permute-start.26 = (bf16[4,48,1920]{2,1,0:T(8,128)(2,1)S(1)}, bf16[4,48,1920]{2,1,0:T(8,128)(2,1)S(1)}, u32[]{:S(2)}, u32[]{:S(2)}) collective-permute-start(bf16[4,48,1920]{2,1,0:T(8,128)(2,1)S(1)} %collective-permute-done.17.rest_1_), channel_id=1, source_target_pairs={{0,1},{1,0},{2,3},{3,2},{4,5},{5,4},{6,7},{7,6},{8,9},{9,8},{10,11... | collective-permute-start | bytes 2211848 | tf_op jit(solution)/shard_map/ppermute | solution.py:563
  98.6 15.7 %collective-permute-start.27 = (bf16[4,48,1920]{2,1,0:T(8,128)(2,1)S(1)}, bf16[4,48,1920]{2,1,0:T(8,128)(2,1)S(1)}, u32[]{:S(2)}, u32[]{:S(2)}) collective-permute-start(bf16[4,48,1920]{2,1,0:T(8,128)(2,1)S(1)} %collective-permute-done.18.rest_2_), channel_id=1, source_target_pairs={{0,1},{1,0},{2,3},{3,2},{4,5},{5,4},{6,7},{7,6},{8,9},{9,8},{10,11... | collective-permute-start | bytes 2211848 | tf_op jit(solution)/shard_map/ppermute | solution.py:563
  112.0 9.4 %collective-permute-start.29 = (bf16[4,48,1536]{2,1,0:T(8,128)(2,1)}, bf16[4,48,1536]{2,1,0:T(8,128)(2,1)}, u32[]{:S(2)}, u32[]{:S(2)}) collective-permute-start(bf16[4,48,1536]{2,1,0:T(8,128)(2,1)} %collective-permute-done.22.rest_9_), channel_id=1, source_target_pairs={{0,2},{1,5},{2,0},{3,7},{4,6},{5,1},{6,4},{7,3},{8,10},{9,13},{10,... | collective-permute-start | bytes 1769480 | tf_op jit(solution)/shard_map/ppermute | solution.py:563
  112.3 20.4 %collective-permute-start.28 = (bf16[4,48,1920]{2,1,0:T(8,128)(2,1)S(1)}, bf16[4,48,1920]{2,1,0:T(8,128)(2,1)}, u32[]{:S(2)}, u32[]{:S(2)}) collective-permute-start(bf16[4,48,1920]{2,1,0:T(8,128)(2,1)S(1)} %collective-permute-done.24.rest_3_), channel_id=1, source_target_pairs={{0,1},{1,0},{2,3},{3,2},{4,5},{5,4},{6,7},{7,6},{8,9},{9,8},{10,11... | collective-permute-start | bytes 2211848 | tf_op jit(solution)/shard_map/ppermute | solution.py:563
  113.8 26.0 %collective-permute-start.30 = (bf16[4,48,1536]{2,1,0:T(8,128)(2,1)}, bf16[4,48,1536]{2,1,0:T(8,128)(2,1)S(1)}, u32[]{:S(2)}, u32[]{:S(2)}) collective-permute-start(bf16[4,48,1536]{2,1,0:T(8,128)(2,1)} %pad_maximum_fusion.2.rest_8_), channel_id=1, source_target_pairs={{0,1},{1,0},{2,3},{3,2},{4,5},{5,4},{6,7},{7,6},{8,9},{9,8},{10,11... | collective-permute-start | bytes 1769480 | tf_op jit(solution)/shard_map/ppermute | solution.py:563
  113.9 25.9 %collective-permute-start.31 = (bf16[4,48,1536]{2,1,0:T(8,128)(2,1)}, bf16[4,48,1536]{2,1,0:T(8,128)(2,1)S(1)}, u32[]{:S(2)}, u32[]{:S(2)}) collective-permute-start(bf16[4,48,1536]{2,1,0:T(8,128)(2,1)} %collective-permute-done.22.rest_9_), channel_id=1, source_target_pairs={{0,1},{1,0},{2,3},{3,2},{4,5},{5,4},{6,7},{7,6},{8,9},{9,8},{10,11... | collective-permute-start | bytes 1769480 | tf_op jit(solution)/shard_map/ppermute | solution.py:563
  114.3 25.5 %collective-permute-start.32 = (bf16[4,48,1536]{2,1,0:T(8,128)(2,1)}, bf16[4,48,1536]{2,1,0:T(8,128)(2,1)S(1)}, u32[]{:S(2)}, u32[]{:S(2)}) collective-permute-start(bf16[4,48,1536]{2,1,0:T(8,128)(2,1)} %collective-permute-done.23.rest_10_), channel_id=1, source_target_pairs={{0,1},{1,0},{2,3},{3,2},{4,5},{5,4},{6,7},{7,6},{8,9},{9,8},{10,11... | collective-permute-start | bytes 1769480 | tf_op jit(solution)/shard_map/ppermute | solution.py:563
  121.4 18.4 %collective-permute-start.33 = (bf16[4,48,1536]{2,1,0:T(8,128)(2,1)}, bf16[4,48,1536]{2,1,0:T(8,128)(2,1)}, u32[]{:S(2)}, u32[]{:S(2)}) collective-permute-start(bf16[4,48,1536]{2,1,0:T(8,128)(2,1)} %collective-permute-done.29.rest_11_), channel_id=1, source_target_pairs={{0,1},{1,0},{2,3},{3,2},{4,5},{5,4},{6,7},{7,6},{8,9},{9,8},{10,11... | collective-permute-start | bytes 1769480 | tf_op jit(solution)/shard_map/ppermute | solution.py:563
  200.0 10.6 %collective-permute-start.34 = (bf16[16,48,1536]{2,1,0:T(8,128)(2,1)}, bf16[16,48,1536]{2,1,0:T(8,128)(2,1)}, u32[]{:S(2)}, u32[]{:S(2)}) collective-permute-start(bf16[16,48,1536]{2,1,0:T(8,128)(2,1)} %get-tuple-element.99), channel_id=1, source_target_pairs={{0,1},{1,0},{2,3},{3,2},{4,5},{5,4},{6,7},{7,6},{8,9},{9,8},{10,11... | collective-permute-start | bytes 7077896 | tf_op jit(solution)/shard_map/ppermute | solution.py:563
  200.1 13.1 %collective-permute-start.35 = (bf16[16,48,1536]{2,1,0:T(8,128)(2,1)}, bf16[16,48,1536]{2,1,0:T(8,128)(2,1)}, u32[]{:S(2)}, u32[]{:S(2)}) collective-permute-start(bf16[16,48,1536]{2,1,0:T(8,128)(2,1)} %get-tuple-element.101), channel_id=1, source_target_pairs={{0,1},{1,0},{2,3},{3,2},{4,5},{5,4},{6,7},{7,6},{8,9},{9,8},{10,11... | collective-permute-start | bytes 7077896 | tf_op jit(solution)/shard_map/ppermute | solution.py:563
  207.2 2.2 collective-permute-start.36
  221.9 31.4 %collective-permute-start.37 = (bf16[4,2,48,3456]{3,2,0,1:T(8,128)(2,1)}, bf16[4,2,48,3456]{3,2,0,1:T(8,128)(2,1)S(1)}, u32[]{:S(2)}, u32[]{:S(2)}) collective-permute-start(bf16[4,2,48,3456]{3,2,0,1:T(8,128)(2,1)} %bitcast_select_fusion.1), channel_id=1, source_target_pairs={{0,4},{1,3},{2,6},{3,1},{4,0},{5,7},{6,2},{7,5},{8,12},{9,11},{10,... | collective-permute-start | bytes 7962632 | tf_op jit(solution)/shard_map/ppermute | solution.py:563
  250.1 25.0 %collective-permute-start.39 = (bf16[16,48,768]{2,1,0:T(8,128)(2,1)}, bf16[16,48,768]{2,1,0:T(8,128)(2,1)}, u32[]{:S(2)}, u32[]{:S(2)}) collective-permute-start(bf16[16,48,768]{2,1,0:T(8,128)(2,1)} %get-tuple-element.113), channel_id=1, source_target_pairs={{0,1},{1,0},{2,3},{3,2},{4,5},{5,4},{6,7},{7,6},{8,9},{9,8},{10,11... | collective-permute-start | bytes 3538952 | tf_op jit(solution)/shard_map/ppermute | solution.py:563
  274.1 4.8 %collective-permute-start.38 = (bf16[16,48,384]{2,1,0:T(8,128)(2,1)}, bf16[16,48,384]{2,1,0:T(8,128)(2,1)S(1)}, u32[]{:S(2)}, u32[]{:S(2)}) collective-permute-start(bf16[16,48,384]{2,1,0:T(8,128)(2,1)} %get-tuple-element.111), channel_id=1, source_target_pairs={{0,1},{1,0},{2,3},{3,2},{4,5},{5,4},{6,7},{7,6},{8,9},{9,8},{10,11... | collective-permute-start | bytes 1769480 | tf_op jit(solution)/shard_map/ppermute | solution.py:563
  278.6 46.9 %collective-permute-start.40 = (bf16[4,48,3456]{2,1,0:T(8,128)(2,1)}, bf16[4,48,3456]{2,1,0:T(8,128)(2,1)}, u32[]{:S(2)}, u32[]{:S(2)}) collective-permute-start(bf16[4,48,3456]{2,1,0:T(8,128)(2,1)} %dynamic-slice_bitcast_fusion), channel_id=1, source_target_pairs={{0,2},{1,5},{2,0},{3,7},{4,6},{5,1},{6,4},{7,3},{8,10},{9,13},{10,... | collective-permute-start | bytes 3981320 | tf_op jit(solution)/shard_map/ppermute | solution.py:563
  280.6 9.3 %collective-permute-start.47 = (bf16[4,2,48,384]{3,2,0,1:T(8,128)(2,1)S(1)}, bf16[4,2,48,384]{3,2,0,1:T(8,128)(2,1)}, u32[]{:S(2)}, u32[]{:S(2)}) collective-permute-start(bf16[4,2,48,384]{3,2,0,1:T(8,128)(2,1)S(1)} %bitcast_select_fusion.5), channel_id=1, source_target_pairs={{0,4},{1,3},{2,6},{3,1},{4,0},{5,7},{6,2},{7,5},{8,12},{9,11},{10,... | collective-permute-start | bytes 884744 | tf_op jit(solution)/shard_map/ppermute | solution.py:563
  291.8 24.0 %collective-permute-start.48 = (bf16[4,48,384]{2,1,0:T(8,128)(2,1)}, bf16[4,48,384]{2,1,0:T(8,128)(2,1)}, u32[]{:S(2)}, u32[]{:S(2)}) collective-permute-start(bf16[4,48,384]{2,1,0:T(8,128)(2,1)} %dynamic-slice_bitcast_fusion.5), channel_id=1, source_target_pairs={{0,2},{1,5},{2,0},{3,7},{4,6},{5,1},{6,4},{7,3},{8,10},{9,13},{10,... | collective-permute-start | bytes 442376 | tf_op jit(solution)/shard_map/ppermute | solution.py:563
  309.8 11.6 %all-to-all-start.1 = ((f32[32,1,288]{2,1,0:T(1,128)}), f32[32,1,288]{2,1,0:T(1,128)}, u32[]{:S(2)}, u32[]{:S(2)}) async-start(f32[32,1,288]{2,1,0:T(1,128)} %all_to_all.14), calls=%async_computation.1 | async-start | bytes 98304 | tf_op jit(solution)/shard_map/all_to_all | solution.py:690
  317.4 4.8 %collective-permute-start.49 = (bf16[48,384]{1,0:T(8,128)(2,1)S(1)}, bf16[48,384]{1,0:T(8,128)(2,1)S(1)}, u32[]{:S(2)}, u32[]{:S(2)}) collective-permute-start(bf16[48,384]{1,0:T(8,128)(2,1)S(1)} %get-tuple-element.155), channel_id=1, source_target_pairs={{0,8},{1,9},{2,10},{3,11},{4,12},{5,13},{6,14},{7,15},{8,16},{9,17... | collective-permute-start | bytes 110600 | tf_op jit(solution)/shard_map/ppermute | solution.py:563
  318.6 3.7 collective-permute-start.50
  319.7 3.8 collective-permute-start.51
  324.3 9.4 %collective-permute-start.52 = (f32[24,384]{1,0:T(8,128)S(1)}, f32[24,384]{1,0:T(8,128)S(1)}, u32[]{:S(2)}, u32[]{:S(2)}) collective-permute-start(f32[24,384]{1,0:T(8,128)S(1)} %get-tuple-element.173), channel_id=1, source_target_pairs={{0,1},{1,0},{2,3},{3,2},{4,5},{5,4},{6,7},{7,6},{8,9},{9,8},{10,11... | collective-permute-start | bytes 110600 | tf_op jit(solution)/shard_map/ppermute | solution.py:563
  327.3 9.4 %collective-permute-start.53 = (bf16[48,3456]{1,0:T(8,128)(2,1)S(1)}, bf16[48,3456]{1,0:T(8,128)(2,1)S(1)}, u32[]{:S(2)}, u32[]{:S(2)}) collective-permute-start(bf16[48,3456]{1,0:T(8,128)(2,1)S(1)} %get-tuple-element.132), channel_id=1, source_target_pairs={{0,8},{1,9},{2,10},{3,11},{4,12},{5,13},{6,14},{7,15},{8,16},{9,17... | collective-permute-start | bytes 995336 | tf_op jit(solution)/shard_map/ppermute | solution.py:563
  328.4 28.5 %collective-permute-start.54 = (bf16[48,3456]{1,0:T(8,128)(2,1)S(1)}, bf16[48,3456]{1,0:T(8,128)(2,1)S(1)}, u32[]{:S(2)}, u32[]{:S(2)}) collective-permute-start(bf16[48,3456]{1,0:T(8,128)(2,1)S(1)} %get-tuple-element.134), channel_id=1, source_target_pairs={{0,16},{1,17},{2,18},{3,19},{4,20},{5,21},{6,22},{7,23},{8,24},{9,... | collective-permute-start | bytes 995336 | tf_op jit(solution)/shard_map/ppermute | solution.py:563
  330.7 29.5 %collective-permute-start.55 = (bf16[48,3456]{1,0:T(8,128)(2,1)S(1)}, bf16[48,3456]{1,0:T(8,128)(2,1)S(1)}, u32[]{:S(2)}, u32[]{:S(2)}) collective-permute-start(bf16[48,3456]{1,0:T(8,128)(2,1)S(1)} %get-tuple-element.133), channel_id=1, source_target_pairs={{0,24},{1,25},{2,26},{3,27},{4,28},{5,29},{6,30},{7,31},{8,0},{9,1... | collective-permute-start | bytes 995336 | tf_op jit(solution)/shard_map/ppermute | solution.py:563
  333.7 27.6 %collective-permute-start.41 = (bf16[4,2,48,768]{3,2,0,1:T(8,128)(2,1)S(1)}, bf16[4,2,48,768]{3,2,0,1:T(8,128)(2,1)S(1)}, u32[]{:S(2)}, u32[]{:S(2)}) collective-permute-start(bf16[4,2,48,768]{3,2,0,1:T(8,128)(2,1)S(1)} %copy-done.15), channel_id=1, source_target_pairs={{0,4},{1,3},{2,6},{3,1},{4,0},{5,7},{6,2},{7,5},{8,12},{9,11},{10,... | collective-permute-start | bytes 1769480 | tf_op jit(solution)/shard_map/ppermute | solution.py:563
  360.6 16.0 %collective-permute-start.58 = (f32[96,384]{1,0:T(8,128)S(1)}, f32[96,384]{1,0:T(8,128)S(1)}, u32[]{:S(2)}, u32[]{:S(2)}) collective-permute-start(f32[96,384]{1,0:T(8,128)S(1)} %get-tuple-element.149), channel_id=1, source_target_pairs={{0,1},{1,0},{2,3},{3,2},{4,5},{5,4},{6,7},{7,6},{8,9},{9,8},{10,11... | collective-permute-start | bytes 442376 | tf_op jit(solution)/shard_map/ppermute | solution.py:563
  361.2 2.4 collective-permute-start.56
  361.5 5.9 %collective-permute-start.42 = (bf16[4,48,768]{2,1,0:T(8,128)(2,1)S(1)}, bf16[4,48,768]{2,1,0:T(8,128)(2,1)S(1)}, u32[]{:S(2)}, u32[]{:S(2)}) collective-permute-start(bf16[4,48,768]{2,1,0:T(8,128)(2,1)S(1)} %dynamic-slice_bitcast_fusion.4), channel_id=1, source_target_pairs={{0,2},{1,5},{2,0},{3,7},{4,6},{5,1},{6,4},{7,3},{8,10},{9,13},{10,... | collective-permute-start | bytes 884744 | tf_op jit(solution)/shard_map/ppermute | solution.py:563
  362.8 6.4 %collective-permute-start.57 = (f32[24,1536]{1,0:T(8,128)S(1)}, f32[24,1536]{1,0:T(8,128)S(1)}, u32[]{:S(2)}, u32[]{:S(2)}) collective-permute-start(f32[24,1536]{1,0:T(8,128)S(1)} %get-tuple-element.151), channel_id=1, source_target_pairs={{0,1},{1,0},{2,3},{3,2},{4,5},{5,4},{6,7},{7,6},{8,9},{9,8},{10,11... | collective-permute-start | bytes 442376 | tf_op jit(solution)/shard_map/ppermute | solution.py:563
  367.6 3.3 collective-permute-start.43
  367.7 4.2 %collective-permute-start.44 = (bf16[48,768]{1,0:T(8,128)(2,1)S(1)}, bf16[48,768]{1,0:T(8,128)(2,1)S(1)}, u32[]{:S(2)}, u32[]{:S(2)}) collective-permute-start(bf16[48,768]{1,0:T(8,128)(2,1)S(1)} %get-tuple-element.154), channel_id=1, source_target_pairs={{0,16},{1,17},{2,18},{3,19},{4,20},{5,21},{6,22},{7,23},{8,24},{9,... | collective-permute-start | bytes 221192 | tf_op jit(solution)/shard_map/ppermute | solution.py:563
  367.8 6.7 %collective-permute-start.45 = (bf16[48,768]{1,0:T(8,128)(2,1)S(1)}, bf16[48,768]{1,0:T(8,128)(2,1)S(1)}, u32[]{:S(2)}, u32[]{:S(2)}) collective-permute-start(bf16[48,768]{1,0:T(8,128)(2,1)S(1)} %get-tuple-element.153), channel_id=1, source_target_pairs={{0,24},{1,25},{2,26},{3,27},{4,28},{5,29},{6,30},{7,31},{8,0},{9,1... | collective-permute-start | bytes 221192 | tf_op jit(solution)/shard_map/ppermute | solution.py:563
  374.6 2.9 collective-permute-start.46
  (33 other events, 350.2 us)

commit v3 on v2

--- a/solution.py
+++ b/solution.py
@@ -456,33 +456,81 @@
         cost_estimate=cost(4 * t * d * d, 9e6),
     )(core, lens, gbr, w, *parts)
 
-def unproject_kernel(blocks, core, low_ref, g_ref, send_ref, keep_ref, sums_ref):
-    d, w = low_ref.shape[1], g_ref.shape[2]
-    r, h = d // blocks, w // 2
+def unproject_kernel(blocks, core, low_ref, *rest):
+    parts, (send_ref, keep_ref, sums_ref) = rest[:-3], rest[-3:]
+    d = low_ref.shape[1]
+    r, h = d // blocks, d // 2
     low_t = low_ref[...].T
-    q, k, v = [mm(low_t, g_ref[part]).astype(BF).reshape(blocks, r, w) for part in range(3)]
-    for half, refs in ((0, (keep_ref, send_ref)), (1, (send_ref, keep_ref))):
-        @pl.when(core[0] == half)
-        def _():
-            refs[0][:, :, :w] = q
-            refs[0][:, :, w:] = k[:, :, :h]
-            refs[1][:, :, :h] = k[:, :, h:]
-            refs[1][:, :, h:] = v
-    for part in range(3):
-        sums_ref[part : part + 1] = jnp.sum(g_ref[part].astype(F32), axis=0, keepdims=True)
-
-def unproject(core, low, g, blocks):
+    first, second = (keep_ref, send_ref), (send_ref, keep_ref)
+    at = 0
+    for g in parts:
+        w = g.shape[2]
+        for part in range(3):
+            grad = mm(low_t, g[part]).astype(BF).reshape(blocks, r, w)
+            sums_ref[part : part + 1, at : at + w] = jnp.sum(g[part].astype(F32), axis=0, keepdims=True)
+            for half, refs in ((0, first), (1, second)):
+                @pl.when(core[0] == half)
+                def _():
+                    for lo in range(0, w, 128):
+                        to = part * d + at + lo
+                        side, to = to // (d + h), to % (d + h)
+                        refs[side][:, :, to : to + 128] = grad[:, :, lo : lo + 128]
+        at += w
+
+def unproject(core, low, parts, blocks):
     t, d = low.shape
-    w = g.shape[2]
-    piece = jax.ShapeDtypeStruct((blocks, d // blocks, w // 2 * 3), BF)
+    piece = jax.ShapeDtypeStruct((blocks, d // blocks, d // 2 * 3), BF)
     return pl.pallas_call(
         functools.partial(unproject_kernel, blocks),
         name="unproject",
-        in_specs=[pl.BlockSpec(memory_space=pltpu.SMEM)] + [pl.BlockSpec(memory_space=pltpu.VMEM)] * 2,
-        out_shape=[piece, piece, jax.ShapeDtypeStruct((3, w), F32)],
+        in_specs=[pl.BlockSpec(memory_space=pltpu.SMEM)] + [pl.BlockSpec(memory_space=pltpu.VMEM)] * (1 + len(parts)),
+        out_shape=[piece, piece, jax.ShapeDtypeStruct((3, d), F32)],
         compiler_params=params(0),
-        cost_estimate=cost(6 * t * d * w, 10e6 * w / d),
-    )(core, low, g)
+        cost_estimate=cost(6 * t * d * d, 10e6),
+    )(core, low, *parts)
+
+def route_kernel(count, steps, table, *refs):
+    keeps, gots, (away_ref, stay_ref) = refs[:count], refs[count : 2 * count], refs[2 * count :]
+    def write(ref):
+        at = 0
+        for k, g in zip(keeps, gots):
+            w = k.shape[-1]
+            total = (k[...].astype(F32) + g[...].astype(F32)).astype(BF)
+            ref[..., at : at + w] = total.reshape(ref.shape[:-1] + (w,))
+            at += w
+    @pl.when(pl.program_id(0) < steps)
+    def _():
+        write(away_ref)
+    @pl.when(pl.program_id(0) >= steps)
+    def _():
+        write(stay_ref)
+
+def route(table, keeps, gots):
+    shape = keeps[0].shape
+    z, r = (shape[0], shape[3]) if len(shape) == 5 else (shape[1], shape[2])
+    steps = 2 if len(shape) == 5 else 1
+    wide = sum(k.shape[-1] for k in keeps)
+    def spec(w):
+        if len(shape) == 5:
+            return pl.BlockSpec((z, 1, 1, r, w), lambda i, t: (0, t[i, 0], t[i, 1], 0, 0))
+        return pl.BlockSpec((1, z, r, w), lambda i, t: (t[i, 0], 0, 0, 0))
+    out = jax.ShapeDtypeStruct((steps, z, r, wide), BF)
+    return pl.pallas_call(
+        functools.partial(route_kernel, len(keeps), steps),
+        name="route",
+        grid_spec=pltpu.PrefetchScalarGridSpec(
+            num_scalar_prefetch=1,
+            grid=(2 * steps,),
+            in_specs=[spec(k.shape[-1]) for k in keeps] * 2,
+            out_specs=[
+                pl.BlockSpec((1, z, r, wide), lambda i, t: (jnp.minimum(i, steps - 1), 0, 0, 0)),
+                pl.BlockSpec((1, z, r, wide), lambda i, t: (jnp.maximum(i - steps, 0), 0, 0, 0)),
+            ],
+        ),
+        out_shape=[out, out],
+        compiler_params=params(1, 24 << 20),
+        cost_estimate=cost(1e6, steps * 2 * z * r * wide * 6),
+    )(table, *keeps, *gots)
 
 def final_kernel(x_ref, w_ref, gmid_ref, gain_ref, *rest):
     parts, (out_ref, vec_ref) = rest[:-2], rest[-2:]
@@ -520,6 +568,75 @@
         compiler_params=params(),
         cost_estimate=cost(6 * t * d * d, 15e6),
     )(x, w, gmid, gain, *parts)
+def spread_matrix(size, width):
+    row = lax.broadcasted_iota(jnp.int32, (128, width), 0).astype(F32)
+    col = lax.broadcasted_iota(jnp.int32, (128, width), 1).astype(F32)
+    inside = col - jnp.floor((col + 0.5) / size) * size
+    return jnp.where(inside == row, 1.0, 0.0)
+
+def own_columns(count, size, per, width):
+    at = lax.broadcasted_iota(jnp.int32, (count, width), 0).astype(F32)
+    at = at - jnp.floor((at + 0.5) / per) * per
+    col = lax.broadcasted_iota(jnp.int32, (count, width), 1).astype(F32)
+    return jnp.logical_and(col >= at * size, col < (at + 1) * size)
+
+SMALL_ROWS = (1, 1, 1, 1, 1, 1, 2, 4)
+
+def unfold_kernel(x_ref, *out_refs):
+    count, d = x_ref.shape[1], out_refs[0].shape[1]
+    for rows, slots in ((1, range(6)), (2, (6,)), (4, (7,))):
+        size, per = d * rows // count, count // rows
+        spread = spread_matrix(size, d).astype(BF)
+        mine = own_columns(count, size, per, d)
+        for s in slots:
+            got = jnp.where(mine, mm(x_ref[s], spread), 0.0)
+            for r in range(rows):
+                to = 2 * r if rows == 2 else r
+                out_refs[s][to : to + 1] = jnp.sum(got[r * per : (r + 1) * per], axis=0, keepdims=True)
+    out_refs[6][1:2] = jnp.zeros((1, d), F32)
+
+def unfold(x, d):
+    return pl.pallas_call(
+        unfold_kernel,
+        name="unfold",
+        in_specs=[pl.BlockSpec(memory_space=pltpu.VMEM)],
+        out_shape=[jax.ShapeDtypeStruct((r if r != 2 else 3, d), F32) for r in SMALL_ROWS],
+        compiler_params=params(0, 16 << 20),
+        cost_estimate=cost(1e8, 1e6),
+    )(x)
+
+def fold_kernel(first_ref, sums_ref, qkv_ref, fc_ref, out_ref):
+    count, d = out_ref.shape[1], first_ref.shape[1]
+    singles = [
+        first_ref[0:1], first_ref[1:2], sums_ref[3:4], sums_ref[1:2], sums_ref[2:3], sums_ref[0:1],
+    ]
+    pairs = [[v] for v in singles] + [[qkv_ref[0:1], qkv_ref[2:3]], [fc_ref[r : r + 1] for r in range(4)]]
+    for rows, slots in ((1, range(6)), (2, (6,)), (4, (7,))):
+        size, per = d * rows // count, count // rows
+        spread = spread_matrix(size, d)
+        mine = own_columns(count, size, per, d)
+        full = jnp.concatenate(
+            [
+                jnp.where(mine, jnp.concatenate([jnp.broadcast_to(v, (per, d)) for v in pairs[s]], 0), 0.0)
+                for s in slots
+            ],
+            0,
+        )
+        got = lax.dot_general(
+            full, spread, (((1,), (1,)), ((), ())), precision=lax.Precision.HIGHEST, preferred_element_type=F32
+        )
+        for i, s in enumerate(slots):
+            out_ref[s] = got[i * count : (i + 1) * count]
+
+def fold(first, sums, qkv, fc, count):
+    return pl.pallas_call(
+        fold_kernel,
+        name="fold",
+        in_specs=[pl.BlockSpec(memory_space=pltpu.VMEM)] * 4,
+        out_shape=jax.ShapeDtypeStruct((8, count, 128), F32),
+        compiler_params=params(0, 32 << 20),
+        cost_estimate=cost(1e8, 1e6),
+    )(first, sums, qkv, fc)
 
 
 class Grid:
@@ -559,6 +676,17 @@
             rows.append(mine)
         return np.array(rows, np.int32)
 
+    def routes(self):
+        near, far = [], []
+        for z0, x0, y0, c0 in self.places():
+            if c0 == 0:
+                near.append([[1 - x0, 0], [1 - x0, 1], [x0, 0], [x0, 1]])
+                far.append([[1 - y0], [y0]])
+            else:
+                near.append([[0, 1 - y0], [1, 1 - y0], [0, y0], [1, y0]])
+                far.append([[1 - x0], [x0]])
+        return np.array(near, np.int32), np.array(far, np.int32)
+
     def send(self, value, target):
         return lax.ppermute(value, AXES, self.perm(target))
 
@@ -614,42 +742,44 @@
 
 class Sum:
     def __init__(self, grid, sends, keeps):
-        self.grid, self.keeps = grid, keeps
+        self.grid = grid
+        at = lax.axis_index(AXES)
+        self.tables = [jnp.asarray(t)[at] for t in grid.routes()]
+        self.shape = (grid.z, 2, 2)
+        self.keeps = keeps
         self.got = [grid.other_core(s) for s in sends]
 
     def core(self):
-        grid = self.grid
-        z, x, y, c = grid.here()
-        own = jnp.concatenate([add(k, g) for k, g in zip(self.keeps, self.got)], 2)
-        own = own.reshape(grid.z, 2, 2, *own.shape[1:])
-        self.away = jnp.where(c == 0, pick(own, 1 - x, 1), pick(own, 1 - y, 2))
-        self.stay = jnp.where(c == 0, pick(own, x, 1), pick(own, y, 2))
+        block = lambda v: v.reshape(*self.shape, *v.shape[1:])
+        self.away, self.stay = route(
+            self.tables[0], [block(k) for k in self.keeps], [block(g) for g in self.got]
+        )
         return self.away
 
-    def near(self, *earlier):
-        self.got = self.grid.along(after(self.away, *earlier), 0)
+    def near(self):
+        self.got = self.grid.along(self.away, 0)
 
     def middle(self):
-        z, x, y, c = self.grid.here()
-        own = add(self.stay, self.got)
-        left = jnp.where(c == 0, y, x)
-        self.away, self.stay = pick(own, 1 - left, 1), pick(own, left, 1)
+        self.away, self.stay = route(self.tables[1], [self.stay], [self.got])
         return self.away
 
-    def far(self, *earlier):
-        self.got = self.grid.along(after(self.away, *earlier), 1)
+    def far(self):
+        self.got = self.grid.along(self.away, 1)
 
     def last(self):
-        self.own = add(self.stay, self.got)
+        self.own = add(self.stay, self.got)[0]
         return self.own
 
-    def rows(self, *earlier):
-        grid = self.grid
-        z = grid.here()[0]
-        own = after(self.own, *earlier)
-        total = pick(own, z, 0).astype(F32)
-        for k in range(1, grid.z):
-            total = total + grid.up(pick(own, (z + k) % grid.z, 0), k).astype(F32)
+    def up(self):
+        grid, z = self.grid, self.grid.here()[0]
+        self.got = [
+            grid.up(pick(self.own, (z + k) % grid.z, 0), k) for k in range(1, grid.z)
+        ]
+
+    def rows(self):
+        total = pick(self.own, self.grid.here()[0], 0).astype(F32)
+        for g in self.got:
+            total = total + g.astype(F32)
         return total
 
 
@@ -670,30 +800,14 @@
     return jnp.concatenate([total[:, j * w : (j + 1) * w] for j in range(4)], 0)
 
 
-def gather_small(count, vectors):
-    flat = jnp.concatenate([v.astype(F32) for v in vectors]).astype(BF)
-    full = jnp.broadcast_to(flat, (count, flat.shape[0]))
-    return lax.all_to_all(full, AXES, 0, 0, tiled=True)
-
-
-def split_small(full, vectors):
-    full = full.astype(F32)
-    out, at = [], 0
-    for v in vectors:
-        out.append(full[:, at : at + v.shape[0]].reshape(-1))
-        at += v.shape[0]
-    return out
-
-
-def scatter_small(count, vectors):
-    parts = [v.reshape(count, -1) for v in vectors]
-    got = lax.all_to_all(jnp.concatenate(parts, 1), AXES, 0, 0, tiled=True)
-    total = jnp.sum(got, axis=0)
-    out, at = [], 0
-    for p in parts:
-        out.append(total[at : at + p.shape[1]])
-        at += p.shape[1]
-    return out
+def gather_small(count, vectors, first):
+    rows = [jnp.pad(v, (0, 128 - v.shape[0])) for v in vectors]
+    flat, _ = stage(jnp.stack(rows), first)
+    return lax.all_to_all(jnp.broadcast_to(flat[:, None], (8, count, 128)), AXES, 1, 1, tiled=True)
+
+
+def scatter_small(cut):
+    return jnp.sum(lax.all_to_all(cut, AXES, 1, 1, tiled=True), axis=1)
 
 
 def halves_of(weight):
@@ -722,36 +836,35 @@
     d = tokens.shape[1]
     grid = Grid(mesh, out_weight.shape[0])
     blocks = grid.blocks
-    vectors = [norm1_gain, norm1_bias, qkv_bias, out_bias, norm2_gain, norm2_bias, fc_bias, proj_bias]
-    little_all = gather_small(grid.count, vectors)
+    vectors = [norm1_gain, norm1_bias, out_bias, norm2_gain, norm2_bias, proj_bias, qkv_bias, fc_bias]
     if grid.paired:
         place = jnp.asarray(grid.table())[lax.axis_index(AXES)]
         core = grid.here()[3].reshape(1).astype(jnp.int32)
         pair_qkv = pair_rows(grid, qkv_weight)
-        first = jnp.concatenate([pair_rows(grid, fc_weight), pair_rows(grid, out_weight)], 1)
-        second = to_chunks(pair_rows(grid, proj_weight))
+        fc_shard, out_shard, proj_shard, pair_qkv = stage(fc_weight, out_weight, proj_weight, pair_qkv)
         stack_qkv = spread_z(grid, pair_qkv)
+        first = jnp.concatenate([pair_rows(grid, fc_shard), pair_rows(grid, out_shard)], 1)
+        second = to_chunks(pair_rows(grid, proj_shard))
+        little_all = gather_small(grid.count, vectors, pair_qkv)
         stack_qkv, first, second = stage(stack_qkv, first, second)
         near_qkv, far_qkv = grid.along(stack_qkv, 0), grid.along(stack_qkv, 1)
+        near_qkv, far_qkv, first, little_all = stage(near_qkv, far_qkv, first, little_all)
+        last_qkv = grid.along(near_qkv, 1)
         stack_first = spread_z(grid, first)
-        near_qkv, little_all = stage(near_qkv, little_all)
-        last_qkv = grid.along(near_qkv, 1)
-        last_qkv, stack_first, second, far_qkv = stage(last_qkv, stack_first, second, far_qkv)
+        last_qkv, stack_first = stage(last_qkv, stack_first)
+        qkv_sources = with_other(grid, [stack_qkv, near_qkv, far_qkv, last_qkv])
         near_first, far_first = grid.along(stack_first, 0), grid.along(stack_first, 1)
+        *qkv_sources, second = stage(*qkv_sources, second)
         stack_second = spread_z(grid, second)
-        qkv_sources = with_other(grid, [stack_qkv, near_qkv, far_qkv, last_qkv])
     else:
         place = jnp.asarray(np.array([[0, 0], [1, 0]], np.int32))
         core = jnp.zeros((1,), jnp.int32)
         full = lambda v: lax.all_gather(v, AXES, axis=0, tiled=True)
         qkv_sources = halves_of(full(qkv_weight))
-    gain_one, shift_one, bias_qv, bias_out, gain_two, shift_two, bias_fc, bias_proj = split_small(
-        little_all, vectors
-    )
-    row = lambda v: v.reshape(1, d)
-    bias_qkv = jnp.stack([bias_qv[:d], jnp.zeros((d,), F32), bias_qv[d:]])
+        little_all = gather_small(grid.count, vectors, tokens)
+    gain_one, shift_one, bias_out, gain_two, shift_two, bias_proj, bias_qkv, bias_fc = unfold(little_all, d)
     qkv, low_one, qkv_full = project(
-        place, tokens, row(gain_one), row(shift_one), bias_qkv, qkv_sources, blocks
+        place, tokens, gain_one, shift_one, bias_qkv, qkv_sources, blocks
     )
     if grid.paired:
         qkv, near_first, far_first, stack_second = stage(qkv, near_first, far_first, stack_second)
@@ -773,81 +886,86 @@
     attended.append(attend(seq_lengths, qkv, 2, 4, 512))
     mixed = [a[1] for a in attended]
     middle, low_two, out_full = mix(
-        place, mixed, tokens, row(bias_out), row(gain_two), row(shift_two), outs, blocks, out_at
+        place, mixed, tokens, bias_out, gain_two, shift_two, outs, blocks, out_at
     )
     (layer_out, grad_middle, grad_branch, fc_send, fc_keep, proj_send, proj_keep, fc_bias_term, sums) = mlp(
-        core, place, seq_lengths, middle, low_two, out_cotangent, bias_fc.reshape(4, d), row(bias_proj),
-        row(gain_two), fcs, projs, blocks,
+        core, place, seq_lengths, middle, low_two, out_cotangent, bias_fc, bias_proj,
+        gain_two, fcs, projs, blocks,
     )
     grad_mixed, out_send, out_keep = unmix(core, seq_lengths, grad_branch, mixed, out_full, blocks)
-    grads, dense, small_sums = [], [], []
     if grid.paired:
-        block_sum = Sum(grid, [fc_send, proj_send, out_send], [fc_keep, proj_keep, out_keep])
-        grad_mixed = after(grad_mixed, block_sum.core())
-        block_sum.near()
-    grads.append(attend_grad(qkv, grad_mixed, attended[0][0], attended[0][2], 0))
-    dense.append(unproject(core, low_one, grads[0], blocks))
+        fc_sum = Sum(grid, [fc_send], [fc_keep])
+        proj_sum = Sum(grid, [proj_send, out_send], [proj_keep, out_keep])
+        grad_mixed, fc_sum.away, fc_sum.stay = stage(grad_mixed, fc_sum.core(), fc_sum.stay)
+        fc_sum.near()
+    grad_one = attend_grad(qkv, grad_mixed, attended[0][0], attended[0][2], 0)
     if grid.paired:
-        large = Sum(grid, [dense[0][0]], [dense[0][1]])
-        grad_mixed = after(grad_mixed, block_sum.middle(), dense[0][2])
-        block_sum.far()
-    grads.append(attend_grad(qkv, grad_mixed, attended[1][0], attended[1][2], 4))
-    dense.append(unproject(core, low_one, grads[1], blocks))
+        fc_sum.got, grad_one, grad_mixed = stage(fc_sum.got, grad_one, grad_mixed)
+        fc_sum.middle()
+        proj_sum.core()
+        grad_mixed, fc_sum.away, fc_sum.stay, proj_sum.away, proj_sum.stay = stage(
+            grad_mixed, fc_sum.away, fc_sum.stay, proj_sum.away, proj_sum.stay
+        )
+        fc_sum.far()
+        proj_sum.near()
+    grad_two = attend_grad(qkv, grad_mixed, attended[1][0], attended[1][2], 4)
     if grid.paired:
-        small = Sum(grid, [dense[1][0]], [dense[1][1]])
-        large.core()
-        large.near(block_sum.last())
-        small.core()
-        small.near(large.away)
-        grad_middle = after(grad_middle, small.away, large.away)
-    input_grad, first_sums = final(tokens, grads, qkv_full, grad_middle, row(gain_one))
+        fc_sum.got, grad_two = stage(fc_sum.got, grad_two)
+        fc_sum.own, grad_two = stage(fc_sum.last(), grad_two)
+        fc_sum.up()
+    grads = [grad_one, grad_two]
+    qkv_send, qkv_keep, qkv_sums = unproject(core, low_one, grads, blocks)
     if grid.paired:
-        total = block_sum.rows()
-        large.middle()
-        large.far()
-        small.middle()
-        small.far()
-        large.last()
-        small.last()
-        fc_wide, out_wide = fc_keep.shape[2], out_keep.shape[2]
-        fc_weight_grad = own_rows(grid, total[:, :fc_wide])
-        proj_weight_grad = own_rows(grid, from_chunks(total[:, fc_wide : 2 * fc_wide]))
-        out_weight_grad = own_rows(grid, total[:, 2 * fc_wide :])
-        ends = [own_rows(grid, large.rows()), own_rows(grid, small.rows())]
+        qkv_send, proj_sum.got = stage(qkv_send, proj_sum.got)
+        qkv_sum = Sum(grid, [qkv_send], [qkv_keep])
+        proj_sum.away, proj_sum.stay, *qkv_sum.got = stage(proj_sum.middle(), proj_sum.stay, *qkv_sum.got)
+        proj_sum.far()
+        grad_middle, qkv_sum.away, qkv_sum.stay = stage(grad_middle, qkv_sum.core(), qkv_sum.stay)
+        qkv_sum.near()
+    input_grad, first_sums = final(tokens, grads, qkv_full, grad_middle, gain_one)
+    cut = fold(first_sums, sums, qkv_sums, fc_bias_term, grid.count)
+    if grid.paired:
+        first_sums, proj_sum.got, fc_sum.got = stage(first_sums, proj_sum.got, fc_sum.got)
+        first_sums, proj_sum.own, qkv_sum.got = stage(first_sums, proj_sum.last(), qkv_sum.got)
+        proj_sum.up()
+        cut, qkv_sum.away, qkv_sum.stay = stage(cut, qkv_sum.middle(), qkv_sum.stay)
+        qkv_sum.far()
+    little = scatter_small(cut)
+    if grid.paired:
+        little, qkv_sum.got = stage(little, qkv_sum.got)
+        proj_sum.own = after(proj_sum.own, qkv_sum.last())
+        qkv_sum.up()
+        fc_weight_grad = own_rows(grid, fc_sum.rows())
+        total = proj_sum.rows()
+        proj_wide = proj_keep.shape[2]
+        proj_weight_grad = own_rows(grid, from_chunks(total[:, :proj_wide]))
+        out_weight_grad = own_rows(grid, total[:, proj_wide:])
+        qkv_weight_grad = own_rows(grid, qkv_sum.rows())
     else:
         reduce = lambda v: lax.psum_scatter(v.astype(F32), AXES, scatter_dimension=0, tiled=True)
         side = lambda k, s: jnp.concatenate([k[0], s[0]], 1)
         fc_weight_grad = reduce(side(fc_keep, fc_send))
         out_weight_grad = reduce(side(out_keep, out_send))
-        ends = [reduce(side(u[1], u[0])) for u in dense]
+        qkv_weight_grad = reduce(side(qkv_keep, qkv_send))
         proj_weight_grad = reduce(
             jnp.concatenate([from_chunks(proj_keep[0]), from_chunks(proj_send[0])], 1)
         )
-    split = lambda e, i: e[:, i * e.shape[1] // 3 : (i + 1) * e.shape[1] // 3]
-    qkv_weight_grad = jnp.concatenate([split(e, i) for i in range(3) for e in ends], 1)
-    qkv_bias_term = jnp.concatenate([dense[p][2][i] for i in (0, 2) for p in range(2)])
-    little = scatter_small(
-        grid.count,
-        [
-            first_sums[0], first_sums[1], qkv_bias_term, sums[3],
-            sums[1], sums[2], fc_bias_term.reshape(-1), sums[0],
-        ],
-    )
+    shard = lambda s: little[s, : vectors[s].shape[0]]
     return (
         layer_out,
         input_grad,
-        little[0],
-        little[1],
+        shard(0),
+        shard(1),
         qkv_weight_grad,
-        little[2],
+        shard(6),
         out_weight_grad,
-        little[3],
-        little[4],
-        little[5],
+        shard(2),
+        shard(3),
+        shard(4),
         fc_weight_grad,
-        little[6],
+        shard(7),
         proj_weight_grad,
-        little[7],
+        shard(5),
     )
 
 

time: 384 us -> 333 us (0.87)
  waiting for transfers between devices: 95.2 us -> 55.7 us
  other arithmetic: 26.2 us -> 7.98 us
  Pallas kernels: 151 us -> 166 us
  local copies, waits for them, and re-layouts: 40.3 us -> 27.6 us
  blocking collectives: 0 us -> 11.3 us
  starting transfers between devices: 63.6 us -> 57.8 us
    ppermute x59 -> x57, waiting for transfers between devices: 87.3 us -> 55.7 us  [send(): return lax.ppermute(value, AXES, self.perm(target))]
    pallas_call x0 -> x8, Pallas kernels: none -> 15.5 us  [the longest x6 13.8 us: route(): pl.pallas_call(functools.partial(route_kernel, len(keeps), steps), name='...]
    convert_element_type x11 -> x1, other arithmetic: 15.4 us -> 0.11 us  [add(): return (a.astype(F32) + b.astype(F32)).astype(BF)]
    all_to_all x0 -> x1, blocking collectives: none -> 11.3 us  [gather_small(): lax.all_to_all(jnp.broadcast_to(flat[:, None], (8, count, 128)), AXES, 1,...]
    another operation x17 -> x5, local copies, waits for them, and re-layouts: 10.5 us -> 0.73 us  [gather_small(): flat, _ = stage(jnp.stack(rows), first)]
    unnamed x80 -> x88, local copies, waits for them, and re-layouts: 7.29 us -> 15.6 us
    all_to_all x2 -> x1, waiting for transfers between devices: 7.91 us -> 0.01 us  [scatter_small(): return jnp.sum(lax.all_to_all(cut, AXES, 1, 1, tiled=True), axis=1)]
    all_to_all x2 -> x1, starting transfers between devices: 11.1 us -> 4.59 us  [scatter_small(): return jnp.sum(lax.all_to_all(cut, AXES, 1, 1, tiled=True), axis=1)]
  transfers between devices with their start and end apart: 61 -> 58, of which waited for: 24 -> 20; matrix products, arithmetic and copies ran while one was open for 13% -> 5% of each run, Pallas kernels for 24% -> 32%
where the time goes in v3:
time: 333 us; the launch traced here: 329 us
  Pallas kernels  166 us (50%)
  starting transfers between devices  57.8 us (17%)
  waiting for transfers between devices  55.7 us (17%)
  local copies, waits for them, and re-layouts  27.6 us (8%)
  blocking collectives  11.3 us (3%)
  other arithmetic  7.98 us (2%)
    pallas_call x1, Pallas kernels, mlp(): pl.pallas_call(functools.partial(mlp_kernel, len(fcs), blocks, rb), name=...  59 us
    ppermute x57, waiting for transfers between devices, send(): return lax.ppermute(value, AXES, self.perm(target))  55.7 us
    ppermute x57, starting transfers between devices, send(): return lax.ppermute(value, AXES, self.perm(target))  53.2 us
    pallas_call x2, Pallas kernels, attend_grad(): pl.pallas_call(functools.partial(attend_grad_kernel, qb), name='attend_gr...  27 us
    pallas_call x2, Pallas kernels, attend(): pl.pallas_call(functools.partial(attend_kernel, qb), name='attend', grid=...  19.1 us
    unnamed x88, local copies, waits for them, and re-layouts  15.6 us
    pallas_call x6, Pallas kernels, route(): pl.pallas_call(functools.partial(route_kernel, len(keeps), steps), name='...  13.8 us
    pallas_call x1, Pallas kernels, unproject(): pl.pallas_call(functools.partial(unproject_kernel, blocks), name='unproje...  11.6 us
  transfers between devices with their start and end apart: 58, of which 20 were waited for; matrix products, arithmetic and copies ran while one was open for 5% of the time, Pallas kernels for 32%

profile of v3, /device:TPU:9, one launch (start us, length us, event | category | flops | bytes accessed | tf_op | source)
XLA Modules:
  0.0 329.1 jit_solution(13796099987778872463)
XLA Ops:
  3.3 1.3 collective-permute-start.1
  4.6 1.1 collective-permute-start.2
  5.7 1.4 collective-permute-start.3
  8.0 1.3 collective-permute-start.6
  12.6 1.2 collective-permute-done.2
  13.8 2.4 collective-permute-done.3
  16.3 1.3 collective-permute-start.7
  17.6 1.2 collective-permute-start.8
  19.0 11.3 %all_to_all.10 = bf16[8,32,128]{2,0,1:T(8,128)(2,1)S(1)} all-to-all(bf16[8,32,128]{2,0,1:T(8,128)(2,1)S(1)} %broadcast_in_dim.2), channel_id=1, replica_groups=mesh['wide'=8,'narrow'=4] {'wide','narrow'}, dimensions={1} | all-to-all | bytes 131072 | tf_op jit(solution)/shard_map/all_to_all | solution.py:806
  30.3 1.5 collective-permute-start.9
  32.6 1.3 collective-permute-start.12
  33.9 1.5 collective-permute-start.13
  35.4 2.3 collective-permute-done.10
  37.6 2.0 collective-permute-start.14
  39.6 7.9 %collective-permute-done.11 = bf16[48,1920]{1,0:T(8,128)(2,1)S(1)} collective-permute-done((bf16[48,1920]{1,0:T(8,128)(2,1)S(1)}, bf16[48,1920]{1,0:T(8,128)(2,1)S(1)}, u32[]{:S(2)}, u32[]{:S(2)}) %collective-permute-start.11) | collective-permute-done | bytes 184352 | tf_op jit(solution)/shard_map/ppermute | solution.py:691
  48.4 1.1 collective-permute-done.12
  51.5 1.3 fusion.8.place
  58.0 1.5 collective-permute-start.20
  59.6 1.9 collective-permute-start.21
  61.5 11.0 %project.1 = (bf16[3,1024,768]{2,1,0:T(8,128)(2,1)}, bf16[1024,768]{1,0:T(8,128)(2,1)}, bf16[16,48,2304]{2,1,0:T(8,128)(2,1)}) custom-call(s32[8,5]{1,0:T(8,128)} %fusion.8.place, bf16[1024,768]{1,0:T(8,128)(2,1)} %x_ref.5, f32[1,768]{1,0:T(1,128)} %copy-done.21, f32[1,768]{1,0:T(1,128)} %copy-done.23, f32[3,768]{1,0:T(4,128)} %copy-done.20, ...), custom_call_target="tpu_custom_call" | custom-call | flops 3623878656 | bytes 18000000 | tf_op jit(solution)/shard_map/project/pallas_call | solution.py:226
  73.9 1.4 collective-permute-start.24
  76.0 2.4 collective-permute-start.25
  78.5 7.7 %collective-permute-done.22.rest_9_ = bf16[4,48,1536]{2,1,0:T(8,128)(2,1)} collective-permute-done((bf16[4,48,1536]{2,1,0:T(8,128)(2,1)S(1)}, bf16[4,48,1536]{2,1,0:T(8,128)(2,1)}, u32[]{:S(2)}, u32[]{:S(2)}) %collective-permute-start.22) | collective-permute-done | bytes 589856 | tf_op jit(solution)/shard_map/ppermute | solution.py:691
  86.2 4.6 %collective-permute-start.27 = (bf16[4,48,1920]{2,1,0:T(8,128)(2,1)S(1)}, bf16[4,48,1920]{2,1,0:T(8,128)(2,1)S(1)}, u32[]{:S(2)}, u32[]{:S(2)}) collective-permute-start(bf16[4,48,1920]{2,1,0:T(8,128)(2,1)S(1)} %collective-permute-done.18.rest_2_), channel_id=1, source_target_pairs={{0,1},{1,0},{2,3},{3,2},{4,5},{5,4},{6,7},{7,6},{8,9},{9,8},{10,11... | collective-permute-start | bytes 2211848 | tf_op jit(solution)/shard_map/ppermute | solution.py:691
  90.8 12.1 %attend.2 = (f32[512,1024]{1,0:T(8,128)}, bf16[1024,512]{1,0:T(8,128)(2,1)}, f32[4,2,1024]{2,1,0:T(2,128)}) custom-call(s32[1]{0:T(128)S(6)} %copy.50.len_ref.lens, bf16[3,1024,768]{2,1,0:T(8,128)(2,1)} %get-tuple-element.165.qkv_ref), custom_call_target="tpu_custom_call" | custom-call | flops 2147483648 | bytes 5333333 | tf_op jit(solution)/shard_map/attend/pallas_call | solution.py:67
  104.9 7.4 %collective-permute-done.29.rest_11_ = bf16[4,48,1536]{2,1,0:T(8,128)(2,1)} collective-permute-done((bf16[4,48,1536]{2,1,0:T(8,128)(2,1)}, bf16[4,48,1536]{2,1,0:T(8,128)(2,1)}, u32[]{:S(2)}, u32[]{:S(2)}) %collective-permute-start.29) | collective-permute-done | bytes 589856 | tf_op jit(solution)/shard_map/ppermute | solution.py:691
  113.2 7.0 %attend.3 = (f32[256,1024]{1,0:T(8,128)}, bf16[1024,256]{1,0:T(8,128)(2,1)}, f32[2,2,1024]{2,1,0:T(2,128)}) custom-call(s32[1]{0:T(128)S(6)} %copy.50.len_ref.lens, bf16[3,1024,768]{2,1,0:T(8,128)(2,1)} %get-tuple-element.165.qkv_ref), custom_call_target="tpu_custom_call" | custom-call | flops 1073741824 | bytes 2666666 | tf_op jit(solution)/shard_map/attend/pallas_call | solution.py:67
  120.3 7.0 %mix.1 = (f32[1024,768]{1,0:T(8,128)}, bf16[1024,768]{1,0:T(8,128)(2,1)}, bf16[16,48,768]{2,1,0:T(8,128)(2,1)}) custom-call(s32[8,5]{1,0:T(8,128)} %fusion.8.place, bf16[1024,768]{1,0:T(8,128)(2,1)} %x_ref.5, f32[1,768]{1,0:T(1,128)} %copy-done.11, f32[1,768]{1,0:T(1,128)} %copy-done.10, f32[1,768]{1,0:T(1,128)} %copy-done.12, ...), custom_call_target="tpu_custom_call" | custom-call | flops 1207959552 | bytes 9000000 | tf_op jit(solution)/shard_map/mix/pallas_call | solution.py:267
  128.7 59.0 %mlp.1 = (bf16[1024,768]{1,0:T(8,128)(2,1)}, f32[1024,768]{1,0:T(8,128)}, bf16[1024,768]{1,0:T(8,128)(2,1)}, bf16[16,48,1536]{2,1,0:T(8,128)(2,1)}, bf16[16,48,1...) custom-call(s32[1]{0:T(128)} %bitcast.core, ...), custom_call_target="tpu_custom_call" | custom-call | flops 28991029248 | bytes 40000000 | tf_op jit(solution)/shard_map/mlp/pallas_call | solution.py:394
  189.0 6.7 %unmix.1 = (bf16[1024,768]{1,0:T(8,128)(2,1)}, bf16[16,48,384]{2,1,0:T(8,128)(2,1)}, bf16[16,48,384]{2,1,0:T(8,128)(2,1)}) custom-call(s32[1]{0:T(128)} %bitcast.core, s32[1]{0:T(128)S(6)} %copy.50.len_ref.lens, bf16[1024,768]{1,0:T(8,128)(2,1)} %get-tuple-element.177.gbr_ref, bf16[16,48,768]{2,1,0:T(8,128)(2,1)} %get-tuple-element.178.w_ref, ...), custom_call_target="tpu_custom_call" | custom-call | flops 2415919104 | bytes 9000000 | tf_op jit(solution)/shard_map/unmix/pallas_call | solution.py:450
  195.7 1.5 copy-done.2
  197.2 1.7 copy-done.3
  198.8 3.2 route.6
  204.0 1.2 collective-permute-done.37
  205.2 1.1 copy-done.9
  206.3 3.7 %route.8 = (bf16[2,4,48,1920]{3,2,1,0:T(8,128)(2,1)S(1)}, bf16[2,4,48,1920]{3,2,1,0:T(8,128)(2,1)S(1)}) custom-call(s32[4,2]{1,0:T(4,128)S(1)} %copy.47.table, bf16[4,2,2,48,1536]{4,3,2,1,0:T(8,128)(2,1)S(1)} %bitcast.90, bf16[4,2,2,48,384]{4,3,2,1,0:T(8,128)(2,1)S(1)} %bitcast.95, bf16[4,2,2,48,1536]{4,3,2,1,0:T(8,128)(2,1)} %bitcast.28.refs_2_, ...), custom_call_target="tpu_custom_call" | custom-call | flops 1000000 | bytes 8847360 | tf_op jit(solution)/shard_map/route/pallas_call | solution.py:518
  210.0 1.1 copy-done.13
  211.1 17.2 %attend_grad.2.rest_0_ = bf16[3,1024,512]{2,1,0:T(8,128)(2,1)} custom-call(bf16[3,1024,768]{2,1,0:T(8,128)(2,1)} %get-tuple-element.165.qkv_ref, bf16[1024,768]{1,0:T(8,128)(2,1)} %get-tuple-element.201.grad_ref, f32[512,1024]{1,0:T(8,128)} %get-tuple-element.186.out_t_ref, f32[4,2,1024]{2,1,0:T(2,128)} %get-tuple-element.162.stat_ref), custom_call_target="tpu_custom_call" | custom-call | flops 5368709120 | bytes 10666666 | tf_op jit(solution)/shard_map/attend_grad/pallas_call | solution.py:140
  228.3 2.8 route.7
  232.6 9.8 %attend_grad.3.rest_1_ = bf16[3,1024,256]{2,1,0:T(8,128)(2,1)} custom-call(bf16[3,1024,768]{2,1,0:T(8,128)(2,1)} %get-tuple-element.165.qkv_ref, bf16[1024,768]{1,0:T(8,128)(2,1)} %get-tuple-element.201.grad_ref, f32[256,1024]{1,0:T(8,128)} %get-tuple-element.202.out_t_ref, f32[2,2,1024]{2,1,0:T(2,128)} %get-tuple-element.203.stat_ref), custom_call_target="tpu_custom_call" | custom-call | flops 2684354560 | bytes 5333333 | tf_op jit(solution)/shard_map/attend_grad/pallas_call | solution.py:140
  242.4 5.2 %collective-permute-done.38 = bf16[1,4,48,1536]{3,2,1,0:T(8,128)(2,1)S(1)} collective-permute-done((bf16[1,4,48,1536]{3,2,1,0:T(8,128)(2,1)}, bf16[1,4,48,1536]{3,2,1,0:T(8,128)(2,1)S(1)}, u32[]{:S(2)}, u32[]{:S(2)}) %collective-permute-start.38) | collective-permute-done | bytes 589856 | tf_op jit(solution)/shard_map/ppermute | solution.py:691
  248.5 11.6 %unproject.1 = (bf16[16,48,1152]{2,1,0:T(8,128)(2,1)}, bf16[16,48,1152]{2,1,0:T(8,128)(2,1)}, f32[3,768]{1,0:T(4,128)}) custom-call(s32[1]{0:T(128)} %bitcast.core, bf16[1024,768]{1,0:T(8,128)(2,1)} %get-tuple-element.176.low_ref, bf16[3,1024,512]{2,1,0:T(8,128)(2,1)} %attend_grad.2.rest_0_, bf16[3,1024,256]{2,1,0:T(8,128)(2,1)} %attend_grad.3.rest_1_), custom_call_target="tpu_custom_call" | custom-call | flops 3623878656 | bytes 10000000 | tf_op jit(solution)/shard_map/unproject/pallas_call | solution.py:483
  260.1 1.1 copy-done.5
  261.2 1.4 collective-permute-start.40
  262.6 1.4 copy-done.6
  264.0 1.8 route.9
  267.5 1.8 dynamic-slice_bitcast_fusion.3
  269.3 2.5 collective-permute-start.43
  271.8 1.5 route.10
  273.8 9.7 %final.1 = (bf16[1024,768]{1,0:T(8,128)(2,1)}, f32[2,768]{1,0:T(2,128)}) custom-call(bf16[1024,768]{1,0:T(8,128)(2,1)} %x_ref.5, bf16[16,48,2304]{2,1,0:T(8,128)(2,1)} %get-tuple-element.174.w_ref, f32[1024,768]{1,0:T(8,128)} %get-tuple-element.218.gmid_ref, f32[1,768]{1,0:T(1,128)} %copy-done.21, bf16[3,1024,512]{2,1,0:T(8,128)(2,1)} %attend_grad.2.rest_0_, ...), custom_call_target="tpu_custom_call" | custom-call | flops 3623878656 | bytes 15000000 | tf_op jit(solution)/shard_map/final/pallas_call | solution.py:555
  284.3 1.3 fold.1
  286.0 1.2 fusion.5
  287.2 1.3 fusion
  288.6 1.2 collective-permute-start.51
  289.7 2.1 collective-permute-start.52
  292.5 2.0 collective-permute-start.55
  296.9 4.6 %all-to-all-start.1 = ((f32[8,32,128]{2,0,1:T(8,128)}), f32[8,32,128]{2,0,1:T(8,128)S(1)}, u32[]{:S(2)}, u32[]{:S(2)}) async-start(f32[8,32,128]{2,0,1:T(8,128)} %copy.49), calls=%async_computation.1 | async-start | bytes 262144 | tf_op jit(solution)/shard_map/all_to_all | solution.py:810
  301.5 4.1 %collective-permute-done.52 = bf16[48,1920]{1,0:T(8,128)(2,1)S(1)} collective-permute-done((bf16[48,1920]{1,0:T(8,128)(2,1)S(1)}, bf16[48,1920]{1,0:T(8,128)(2,1)S(1)}, u32[]{:S(2)}, u32[]{:S(2)}) %collective-permute-start.52) | collective-permute-done | bytes 184352 | tf_op jit(solution)/shard_map/ppermute | solution.py:691
  305.6 3.4 %collective-permute-done.53 = bf16[48,1920]{1,0:T(8,128)(2,1)S(1)} collective-permute-done((bf16[48,1920]{1,0:T(8,128)(2,1)S(1)}, bf16[48,1920]{1,0:T(8,128)(2,1)S(1)}, u32[]{:S(2)}, u32[]{:S(2)}) %collective-permute-start.53) | collective-permute-done | bytes 184352 | tf_op jit(solution)/shard_map/ppermute | solution.py:691
  309.2 1.9 collective-permute-start.56
  311.3 1.7 maximum_select_fusion
  314.6 1.2 collective-permute-start.48
  318.8 5.1 %collective-permute-done.48 = bf16[48,1152]{1,0:T(8,128)(2,1)S(1)} collective-permute-done((bf16[48,1152]{1,0:T(8,128)(2,1)S(1)}, bf16[48,1152]{1,0:T(8,128)(2,1)S(1)}, u32[]{:S(2)}, u32[]{:S(2)}) %collective-permute-start.48) | collective-permute-done | bytes 110624 | tf_op jit(solution)/shard_map/ppermute | solution.py:691
  323.9 2.5 collective-permute-done.49
  (209 shorter events, 41.0 us)
Async XLA Ops:
  1.5 1.6 collective-permute-start
  3.3 9.3 %collective-permute-start.1 = (bf16[48,1152]{1,0:T(8,128)(2,1)S(1)}, bf16[48,1152]{1,0:T(8,128)(2,1)S(1)}, u32[]{:S(2)}, u32[]{:S(2)}) collective-permute-start(bf16[48,1152]{1,0:T(8,128)(2,1)S(1)} %maximum_select_fusion.5), channel_id=1, source_target_pairs={{0,8},{1,9},{2,10},{3,11},{4,12},{5,13},{6,14},{7,15},{8,16},{9,17... | collective-permute-start | bytes 331784 | tf_op jit(solution)/shard_map/ppermute | solution.py:691
  4.6 9.2 %collective-permute-start.2 = (bf16[48,1152]{1,0:T(8,128)(2,1)S(1)}, bf16[48,1152]{1,0:T(8,128)(2,1)S(1)}, u32[]{:S(2)}, u32[]{:S(2)}) collective-permute-start(bf16[48,1152]{1,0:T(8,128)(2,1)S(1)} %maximum_select_fusion.5), channel_id=1, source_target_pairs={{0,16},{1,17},{2,18},{3,19},{4,20},{5,21},{6,22},{7,23},{8,24},{9,... | collective-permute-start | bytes 331784 | tf_op jit(solution)/shard_map/ppermute | solution.py:691
  5.7 10.6 %collective-permute-start.3 = (bf16[48,1152]{1,0:T(8,128)(2,1)S(1)}, bf16[48,1152]{1,0:T(8,128)(2,1)S(1)}, u32[]{:S(2)}, u32[]{:S(2)}) collective-permute-start(bf16[48,1152]{1,0:T(8,128)(2,1)S(1)} %maximum_select_fusion.5), channel_id=1, source_target_pairs={{0,24},{1,25},{2,26},{3,27},{4,28},{5,29},{6,30},{7,31},{8,0},{9,1... | collective-permute-start | bytes 331784 | tf_op jit(solution)/shard_map/ppermute | solution.py:691
  8.0 3.5 %collective-permute-start.6 = (bf16[96,384]{1,0:T(8,128)(2,1)S(1)}, bf16[96,384]{1,0:T(8,128)(2,1)S(1)}, u32[]{:S(2)}, u32[]{:S(2)}) collective-permute-start(bf16[96,384]{1,0:T(8,128)(2,1)S(1)} %get-tuple-element.267), channel_id=1, source_target_pairs={{0,1},{1,0},{2,3},{3,2},{4,5},{5,4},{6,7},{7,6},{8,9},{9,8},{10,11... | collective-permute-start | bytes 221192 | tf_op jit(solution)/shard_map/ppermute | solution.py:691
  10.0 1.2 collective-permute-start.5
  11.2 1.3 collective-permute-start.4
  16.3 45.1 %copy-start.32 = (bf16[4,48,1152]{2,1,0:T(8,128)(2,1)}, bf16[4,48,1152]{2,1,0:T(8,128)(2,1)S(1)}, u32[]{:S(2)}) copy-start(bf16[4,48,1152]{2,1,0:T(8,128)(2,1)S(1)} %pad_maximum_fusion.2.rest_0_) | copy-start | bytes 1327108
  16.3 13.9 %collective-permute-start.7 = (bf16[4,48,1152]{2,1,0:T(8,128)(2,1)S(1)}, bf16[4,48,1152]{2,1,0:T(8,128)(2,1)S(1)}, u32[]{:S(2)}, u32[]{:S(2)}) collective-permute-start(bf16[4,48,1152]{2,1,0:T(8,128)(2,1)S(1)} %pad_maximum_fusion.2.rest_0_), channel_id=1, source_target_pairs={{0,4},{1,3},{2,6},{3,1},{4,0},{5,7},{6,2},{7,5},{8,12},{9,11},{10,... | collective-permute-start | bytes 1327112 | tf_op jit(solution)/shard_map/ppermute | solution.py:691
  17.6 12.6 %collective-permute-start.8 = (bf16[4,48,1152]{2,1,0:T(8,128)(2,1)S(1)}, bf16[4,48,1152]{2,1,0:T(8,128)(2,1)}, u32[]{:S(2)}, u32[]{:S(2)}) collective-permute-start(bf16[4,48,1152]{2,1,0:T(8,128)(2,1)S(1)} %pad_maximum_fusion.2.rest_0_), channel_id=1, source_target_pairs={{0,2},{1,5},{2,0},{3,7},{4,6},{5,1},{6,4},{7,3},{8,10},{9,13},{10,... | collective-permute-start | bytes 1327112 | tf_op jit(solution)/shard_map/ppermute | solution.py:691
  30.2 31.2 %copy-start.43 = (bf16[4,48,1152]{2,1,0:T(8,128)(2,1)}, bf16[4,48,1152]{2,1,0:T(8,128)(2,1)S(1)}, u32[]{:S(2)}) copy-start(bf16[4,48,1152]{2,1,0:T(8,128)(2,1)S(1)} %collective-permute-done.7.rest_1_) | copy-start | bytes 1327108
  30.3 19.4 %collective-permute-start.9 = (bf16[4,48,1152]{2,1,0:T(8,128)(2,1)S(1)}, bf16[4,48,1152]{2,1,0:T(8,128)(2,1)}, u32[]{:S(2)}, u32[]{:S(2)}) collective-permute-start(bf16[4,48,1152]{2,1,0:T(8,128)(2,1)S(1)} %collective-permute-done.7.rest_1_), channel_id=1, source_target_pairs={{0,2},{1,5},{2,0},{3,7},{4,6},{5,1},{6,4},{7,3},{8,10},{9,13},{10,... | collective-permute-start | bytes 1327112 | tf_op jit(solution)/shard_map/ppermute | solution.py:691
  31.7 5.9 %collective-permute-start.10 = (bf16[48,1920]{1,0:T(8,128)(2,1)S(1)}, bf16[48,1920]{1,0:T(8,128)(2,1)S(1)}, u32[]{:S(2)}, u32[]{:S(2)}) collective-permute-start(bf16[48,1920]{1,0:T(8,128)(2,1)S(1)} %pad_maximum_fusion.4), channel_id=1, source_target_pairs={{0,8},{1,9},{2,10},{3,11},{4,12},{5,13},{6,14},{7,15},{8,16},{9,17... | collective-permute-start | bytes 552968 | tf_op jit(solution)/shard_map/ppermute | solution.py:691
  31.7 15.8 %collective-permute-start.11 = (bf16[48,1920]{1,0:T(8,128)(2,1)S(1)}, bf16[48,1920]{1,0:T(8,128)(2,1)S(1)}, u32[]{:S(2)}, u32[]{:S(2)}) collective-permute-start(bf16[48,1920]{1,0:T(8,128)(2,1)S(1)} %pad_maximum_fusion.4), channel_id=1, source_target_pairs={{0,16},{1,17},{2,18},{3,19},{4,20},{5,21},{6,22},{7,23},{8,24},{9,... | collective-permute-start | bytes 552968 | tf_op jit(solution)/shard_map/ppermute | solution.py:691
  32.6 17.0 %collective-permute-start.12 = (bf16[48,1920]{1,0:T(8,128)(2,1)S(1)}, bf16[48,1920]{1,0:T(8,128)(2,1)S(1)}, u32[]{:S(2)}, u32[]{:S(2)}) collective-permute-start(bf16[48,1920]{1,0:T(8,128)(2,1)S(1)} %pad_maximum_fusion.4), channel_id=1, source_target_pairs={{0,24},{1,25},{2,26},{3,27},{4,28},{5,29},{6,30},{7,31},{8,0},{9,1... | collective-permute-start | bytes 552968 | tf_op jit(solution)/shard_map/ppermute | solution.py:691
  33.9 17.3 %collective-permute-start.13 = (bf16[4,48,1152]{2,1,0:T(8,128)(2,1)S(1)}, bf16[4,48,1152]{2,1,0:T(8,128)(2,1)}, u32[]{:S(2)}, u32[]{:S(2)}) collective-permute-start(bf16[4,48,1152]{2,1,0:T(8,128)(2,1)S(1)} %pad_maximum_fusion.2.rest_0_), channel_id=1, source_target_pairs={{0,1},{1,0},{2,3},{3,2},{4,5},{5,4},{6,7},{7,6},{8,9},{9,8},{10,11... | collective-permute-start | bytes 1327112 | tf_op jit(solution)/shard_map/ppermute | solution.py:691
  37.6 20.3 %collective-permute-start.14 = (bf16[4,48,1152]{2,1,0:T(8,128)(2,1)S(1)}, bf16[4,48,1152]{2,1,0:T(8,128)(2,1)}, u32[]{:S(2)}, u32[]{:S(2)}) collective-permute-start(bf16[4,48,1152]{2,1,0:T(8,128)(2,1)S(1)} %collective-permute-done.7.rest_1_), channel_id=1, source_target_pairs={{0,1},{1,0},{2,3},{3,2},{4,5},{5,4},{6,7},{7,6},{8,9},{9,8},{10,11... | collective-permute-start | bytes 1327112 | tf_op jit(solution)/shard_map/ppermute | solution.py:691
  47.5 10.4 %collective-permute-start.15 = (bf16[4,48,1152]{2,1,0:T(8,128)(2,1)}, bf16[4,48,1152]{2,1,0:T(8,128)(2,1)}, u32[]{:S(2)}, u32[]{:S(2)}) collective-permute-start(bf16[4,48,1152]{2,1,0:T(8,128)(2,1)} %collective-permute-done.8.rest_2_), channel_id=1, source_target_pairs={{0,1},{1,0},{2,3},{3,2},{4,5},{5,4},{6,7},{7,6},{8,9},{9,8},{10,11... | collective-permute-start | bytes 1327112 | tf_op jit(solution)/shard_map/ppermute | solution.py:691
  49.7 26.3 %copy-start.24 = (bf16[4,48,1920]{2,1,0:T(8,128)(2,1)}, bf16[4,48,1920]{2,1,0:T(8,128)(2,1)S(1)}, u32[]{:S(2)}) copy-start(bf16[4,48,1920]{2,1,0:T(8,128)(2,1)S(1)} %pad_maximum_fusion.rest_0_) | copy-start | bytes 2211844
  49.7 8.2 %collective-permute-start.16 = (bf16[4,48,1152]{2,1,0:T(8,128)(2,1)}, bf16[4,48,1152]{2,1,0:T(8,128)(2,1)}, u32[]{:S(2)}, u32[]{:S(2)}) collective-permute-start(bf16[4,48,1152]{2,1,0:T(8,128)(2,1)} %collective-permute-done.9.rest_3_), channel_id=1, source_target_pairs={{0,1},{1,0},{2,3},{3,2},{4,5},{5,4},{6,7},{7,6},{8,9},{9,8},{10,11... | collective-permute-start | bytes 1327112 | tf_op jit(solution)/shard_map/ppermute | solution.py:691
  50.3 23.1 %collective-permute-start.17 = (bf16[4,48,1920]{2,1,0:T(8,128)(2,1)S(1)}, bf16[4,48,1920]{2,1,0:T(8,128)(2,1)S(1)}, u32[]{:S(2)}, u32[]{:S(2)}) collective-permute-start(bf16[4,48,1920]{2,1,0:T(8,128)(2,1)S(1)} %pad_maximum_fusion.rest_0_), channel_id=1, source_target_pairs={{0,4},{1,3},{2,6},{3,1},{4,0},{5,7},{6,2},{7,5},{8,12},{9,11},{10,... | collective-permute-start | bytes 2211848 | tf_op jit(solution)/shard_map/ppermute | solution.py:691
  51.2 22.2 %collective-permute-start.18 = (bf16[4,48,1920]{2,1,0:T(8,128)(2,1)S(1)}, bf16[4,48,1920]{2,1,0:T(8,128)(2,1)S(1)}, u32[]{:S(2)}, u32[]{:S(2)}) collective-permute-start(bf16[4,48,1920]{2,1,0:T(8,128)(2,1)S(1)} %pad_maximum_fusion.rest_0_), channel_id=1, source_target_pairs={{0,2},{1,5},{2,0},{3,7},{4,6},{5,1},{6,4},{7,3},{8,10},{9,13},{10,... | collective-permute-start | bytes 2211848 | tf_op jit(solution)/shard_map/ppermute | solution.py:691
  58.0 14.5 %collective-permute-start.19 = (bf16[48,1536]{1,0:T(8,128)(2,1)S(1)}, bf16[48,1536]{1,0:T(8,128)(2,1)S(1)}, u32[]{:S(2)}, u32[]{:S(2)}) collective-permute-start(bf16[48,1536]{1,0:T(8,128)(2,1)S(1)} %pad_maximum_fusion.5), channel_id=1, source_target_pairs={{0,8},{1,9},{2,10},{3,11},{4,12},{5,13},{6,14},{7,15},{8,16},{9,17... | collective-permute-start | bytes 442376 | tf_op jit(solution)/shard_map/ppermute | solution.py:691
  58.0 14.4 %collective-permute-start.20 = (bf16[48,1536]{1,0:T(8,128)(2,1)S(1)}, bf16[48,1536]{1,0:T(8,128)(2,1)S(1)}, u32[]{:S(2)}, u32[]{:S(2)}) collective-permute-start(bf16[48,1536]{1,0:T(8,128)(2,1)S(1)} %pad_maximum_fusion.5), channel_id=1, source_target_pairs={{0,16},{1,17},{2,18},{3,19},{4,20},{5,21},{6,22},{7,23},{8,24},{9,... | collective-permute-start | bytes 442376 | tf_op jit(solution)/shard_map/ppermute | solution.py:691
  59.6 13.7 %collective-permute-start.21 = (bf16[48,1536]{1,0:T(8,128)(2,1)S(1)}, bf16[48,1536]{1,0:T(8,128)(2,1)S(1)}, u32[]{:S(2)}, u32[]{:S(2)}) collective-permute-start(bf16[48,1536]{1,0:T(8,128)(2,1)S(1)} %pad_maximum_fusion.5), channel_id=1, source_target_pairs={{0,24},{1,25},{2,26},{3,27},{4,28},{5,29},{6,30},{7,31},{8,0},{9,1... | collective-permute-start | bytes 442376 | tf_op jit(solution)/shard_map/ppermute | solution.py:691
  73.4 30.5 %copy-start.31 = (bf16[4,48,1536]{2,1,0:T(8,128)(2,1)}, bf16[4,48,1536]{2,1,0:T(8,128)(2,1)S(1)}, u32[]{:S(2)}) copy-start(bf16[4,48,1536]{2,1,0:T(8,128)(2,1)S(1)} %pad_maximum_fusion.1.rest_8_) | copy-start | bytes 1769476
  73.4 29.5 %copy-start.25 = (bf16[4,48,1920]{2,1,0:T(8,128)(2,1)}, bf16[4,48,1920]{2,1,0:T(8,128)(2,1)S(1)}, u32[]{:S(2)}) copy-start(bf16[4,48,1920]{2,1,0:T(8,128)(2,1)S(1)} %collective-permute-done.17.rest_1_) | copy-start | bytes 2211844
  73.4 29.5 %copy-start.26 = (bf16[4,48,1920]{2,1,0:T(8,128)(2,1)}, bf16[4,48,1920]{2,1,0:T(8,128)(2,1)S(1)}, u32[]{:S(2)}) copy-start(bf16[4,48,1920]{2,1,0:T(8,128)(2,1)S(1)} %collective-permute-done.18.rest_2_) | copy-start | bytes 2211844
  73.4 12.8 %collective-permute-start.22 = (bf16[4,48,1536]{2,1,0:T(8,128)(2,1)S(1)}, bf16[4,48,1536]{2,1,0:T(8,128)(2,1)}, u32[]{:S(2)}, u32[]{:S(2)}) collective-permute-start(bf16[4,48,1536]{2,1,0:T(8,128)(2,1)S(1)} %pad_maximum_fusion.1.rest_8_), channel_id=1, source_target_pairs={{0,4},{1,3},{2,6},{3,1},{4,0},{5,7},{6,2},{7,5},{8,12},{9,11},{10,... | collective-permute-start | bytes 1769480 | tf_op jit(solution)/shard_map/ppermute | solution.py:691
  73.9 29.0 %collective-permute-start.24 = (bf16[4,48,1920]{2,1,0:T(8,128)(2,1)S(1)}, bf16[4,48,1920]{2,1,0:T(8,128)(2,1)S(1)}, u32[]{:S(2)}, u32[]{:S(2)}) collective-permute-start(bf16[4,48,1920]{2,1,0:T(8,128)(2,1)S(1)} %collective-permute-done.17.rest_1_), channel_id=1, source_target_pairs={{0,2},{1,5},{2,0},{3,7},{4,6},{5,1},{6,4},{7,3},{8,10},{9,13},{10,... | collective-permute-start | bytes 2211848 | tf_op jit(solution)/shard_map/ppermute | solution.py:691
  75.2 27.6 %collective-permute-start.23 = (bf16[4,48,1536]{2,1,0:T(8,128)(2,1)S(1)}, bf16[4,48,1536]{2,1,0:T(8,128)(2,1)}, u32[]{:S(2)}, u32[]{:S(2)}) collective-permute-start(bf16[4,48,1536]{2,1,0:T(8,128)(2,1)S(1)} %pad_maximum_fusion.1.rest_8_), channel_id=1, source_target_pairs={{0,2},{1,5},{2,0},{3,7},{4,6},{5,1},{6,4},{7,3},{8,10},{9,13},{10,... | collective-permute-start | bytes 1769480 | tf_op jit(solution)/shard_map/ppermute | solution.py:691
  76.0 27.8 %collective-permute-start.25 = (bf16[4,48,1920]{2,1,0:T(8,128)(2,1)S(1)}, bf16[4,48,1920]{2,1,0:T(8,128)(2,1)S(1)}, u32[]{:S(2)}, u32[]{:S(2)}) collective-permute-start(bf16[4,48,1920]{2,1,0:T(8,128)(2,1)S(1)} %pad_maximum_fusion.rest_0_), channel_id=1, source_target_pairs={{0,1},{1,0},{2,3},{3,2},{4,5},{5,4},{6,7},{7,6},{8,9},{9,8},{10,11... | collective-permute-start | bytes 2211848 | tf_op jit(solution)/shard_map/ppermute | solution.py:691
  78.4 26.0 %collective-permute-start.26 = (bf16[4,48,1920]{2,1,0:T(8,128)(2,1)S(1)}, bf16[4,48,1920]{2,1,0:T(8,128)(2,1)S(1)}, u32[]{:S(2)}, u32[]{:S(2)}) collective-permute-start(bf16[4,48,1920]{2,1,0:T(8,128)(2,1)S(1)} %collective-permute-done.17.rest_1_), channel_id=1, source_target_pairs={{0,1},{1,0},{2,3},{3,2},{4,5},{5,4},{6,7},{7,6},{8,9},{9,8},{10,11... | collective-permute-start | bytes 2211848 | tf_op jit(solution)/shard_map/ppermute | solution.py:691
  86.2 18.3 %collective-permute-start.27 = (bf16[4,48,1920]{2,1,0:T(8,128)(2,1)S(1)}, bf16[4,48,1920]{2,1,0:T(8,128)(2,1)S(1)}, u32[]{:S(2)}, u32[]{:S(2)}) collective-permute-start(bf16[4,48,1920]{2,1,0:T(8,128)(2,1)S(1)} %collective-permute-done.18.rest_2_), channel_id=1, source_target_pairs={{0,1},{1,0},{2,3},{3,2},{4,5},{5,4},{6,7},{7,6},{8,9},{9,8},{10,11... | collective-permute-start | bytes 2211848 | tf_op jit(solution)/shard_map/ppermute | solution.py:691
  102.9 9.4 %collective-permute-start.29 = (bf16[4,48,1536]{2,1,0:T(8,128)(2,1)}, bf16[4,48,1536]{2,1,0:T(8,128)(2,1)}, u32[]{:S(2)}, u32[]{:S(2)}) collective-permute-start(bf16[4,48,1536]{2,1,0:T(8,128)(2,1)} %collective-permute-done.22.rest_9_), channel_id=1, source_target_pairs={{0,2},{1,5},{2,0},{3,7},{4,6},{5,1},{6,4},{7,3},{8,10},{9,13},{10,... | collective-permute-start | bytes 1769480 | tf_op jit(solution)/shard_map/ppermute | solution.py:691
  103.8 16.4 %collective-permute-start.28 = (bf16[4,48,1920]{2,1,0:T(8,128)(2,1)S(1)}, bf16[4,48,1920]{2,1,0:T(8,128)(2,1)}, u32[]{:S(2)}, u32[]{:S(2)}) collective-permute-start(bf16[4,48,1920]{2,1,0:T(8,128)(2,1)S(1)} %collective-permute-done.24.rest_3_), channel_id=1, source_target_pairs={{0,1},{1,0},{2,3},{3,2},{4,5},{5,4},{6,7},{7,6},{8,9},{9,8},{10,11... | collective-permute-start | bytes 2211848 | tf_op jit(solution)/shard_map/ppermute | solution.py:691
  103.9 23.4 %collective-permute-start.30 = (bf16[4,48,1536]{2,1,0:T(8,128)(2,1)S(1)}, bf16[4,48,1536]{2,1,0:T(8,128)(2,1)S(1)}, u32[]{:S(2)}, u32[]{:S(2)}) collective-permute-start(bf16[4,48,1536]{2,1,0:T(8,128)(2,1)S(1)} %pad_maximum_fusion.1.rest_8_), channel_id=1, source_target_pairs={{0,1},{1,0},{2,3},{3,2},{4,5},{5,4},{6,7},{7,6},{8,9},{9,8},{10,11... | collective-permute-start | bytes 1769480 | tf_op jit(solution)/shard_map/ppermute | solution.py:691
  104.4 22.8 %collective-permute-start.31 = (bf16[4,48,1536]{2,1,0:T(8,128)(2,1)}, bf16[4,48,1536]{2,1,0:T(8,128)(2,1)S(1)}, u32[]{:S(2)}, u32[]{:S(2)}) collective-permute-start(bf16[4,48,1536]{2,1,0:T(8,128)(2,1)} %collective-permute-done.22.rest_9_), channel_id=1, source_target_pairs={{0,1},{1,0},{2,3},{3,2},{4,5},{5,4},{6,7},{7,6},{8,9},{9,8},{10,11... | collective-permute-start | bytes 1769480 | tf_op jit(solution)/shard_map/ppermute | solution.py:691
  104.5 22.8 %collective-permute-start.32 = (bf16[4,48,1536]{2,1,0:T(8,128)(2,1)}, bf16[4,48,1536]{2,1,0:T(8,128)(2,1)S(1)}, u32[]{:S(2)}, u32[]{:S(2)}) collective-permute-start(bf16[4,48,1536]{2,1,0:T(8,128)(2,1)} %collective-permute-done.23.rest_10_), channel_id=1, source_target_pairs={{0,1},{1,0},{2,3},{3,2},{4,5},{5,4},{6,7},{7,6},{8,9},{9,8},{10,11... | collective-permute-start | bytes 1769480 | tf_op jit(solution)/shard_map/ppermute | solution.py:691
  112.3 15.0 %collective-permute-start.33 = (bf16[4,48,1536]{2,1,0:T(8,128)(2,1)}, bf16[4,48,1536]{2,1,0:T(8,128)(2,1)S(1)}, u32[]{:S(2)}, u32[]{:S(2)}) collective-permute-start(bf16[4,48,1536]{2,1,0:T(8,128)(2,1)} %collective-permute-done.29.rest_11_), channel_id=1, source_target_pairs={{0,1},{1,0},{2,3},{3,2},{4,5},{5,4},{6,7},{7,6},{8,9},{9,8},{10,11... | collective-permute-start | bytes 1769480 | tf_op jit(solution)/shard_map/ppermute | solution.py:691
  187.7 8.0 %collective-permute-start.34 = (bf16[16,48,1536]{2,1,0:T(8,128)(2,1)}, bf16[16,48,1536]{2,1,0:T(8,128)(2,1)S(1)}, u32[]{:S(2)}, u32[]{:S(2)}) collective-permute-start(bf16[16,48,1536]{2,1,0:T(8,128)(2,1)} %get-tuple-element.181), channel_id=1, source_target_pairs={{0,1},{1,0},{2,3},{3,2},{4,5},{5,4},{6,7},{7,6},{8,9},{9,8},{10,11... | collective-permute-start | bytes 7077896 | tf_op jit(solution)/shard_map/ppermute | solution.py:691
  187.8 17.5 %collective-permute-start.36 = (bf16[16,48,1536]{2,1,0:T(8,128)(2,1)}, bf16[16,48,1536]{2,1,0:T(8,128)(2,1)}, u32[]{:S(2)}, u32[]{:S(2)}) collective-permute-start(bf16[16,48,1536]{2,1,0:T(8,128)(2,1)} %get-tuple-element.195), channel_id=1, source_target_pairs={{0,1},{1,0},{2,3},{3,2},{4,5},{5,4},{6,7},{7,6},{8,9},{9,8},{10,11... | collective-permute-start | bytes 7077896 | tf_op jit(solution)/shard_map/ppermute | solution.py:691
  202.0 26.3 %collective-permute-start.35 = (bf16[2,4,48,1536]{3,2,1,0:T(8,128)(2,1)}, bf16[2,4,48,1536]{3,2,1,0:T(8,128)(2,1)}, u32[]{:S(2)}, u32[]{:S(2)}) collective-permute-start(bf16[2,4,48,1536]{3,2,1,0:T(8,128)(2,1)} %get-tuple-element.184), channel_id=1, source_target_pairs={{0,4},{1,3},{2,6},{3,1},{4,0},{5,7},{6,2},{7,5},{8,12},{9,11},{10,... | collective-permute-start | bytes 3538952 | tf_op jit(solution)/shard_map/ppermute | solution.py:691
  202.4 2.8 collective-permute-start.37
  231.1 29.0 %collective-permute-start.39 = (bf16[2,4,48,1920]{3,2,1,0:T(8,128)(2,1)S(1)}, bf16[2,4,48,1920]{3,2,1,0:T(8,128)(2,1)S(1)}, u32[]{:S(2)}, u32[]{:S(2)}) collective-permute-start(bf16[2,4,48,1920]{3,2,1,0:T(8,128)(2,1)S(1)} %copy-done.14), channel_id=1, source_target_pairs={{0,4},{1,3},{2,6},{3,1},{4,0},{5,7},{6,2},{7,5},{8,12},{9,11},{10,... | collective-permute-start | bytes 4423688 | tf_op jit(solution)/shard_map/ppermute | solution.py:691
  232.0 15.6 %collective-permute-start.38 = (bf16[1,4,48,1536]{3,2,1,0:T(8,128)(2,1)}, bf16[1,4,48,1536]{3,2,1,0:T(8,128)(2,1)S(1)}, u32[]{:S(2)}, u32[]{:S(2)}) collective-permute-start(bf16[1,4,48,1536]{3,2,1,0:T(8,128)(2,1)} %get-tuple-element.200), channel_id=1, source_target_pairs={{0,2},{1,5},{2,0},{3,7},{4,6},{5,1},{6,4},{7,3},{8,10},{9,13},{10,... | collective-permute-start | bytes 1769480 | tf_op jit(solution)/shard_map/ppermute | solution.py:691
  261.2 5.5 %collective-permute-start.40 = (bf16[16,48,1152]{2,1,0:T(8,128)(2,1)}, bf16[16,48,1152]{2,1,0:T(8,128)(2,1)S(1)}, u32[]{:S(2)}, u32[]{:S(2)}) collective-permute-start(bf16[16,48,1152]{2,1,0:T(8,128)(2,1)} %get-tuple-element.214), channel_id=1, source_target_pairs={{0,1},{1,0},{2,3},{3,2},{4,5},{5,4},{6,7},{7,6},{8,9},{9,8},{10,11... | collective-permute-start | bytes 5308424 | tf_op jit(solution)/shard_map/ppermute | solution.py:691
  266.7 19.3 %collective-permute-start.41 = (bf16[1,4,48,1920]{3,2,1,0:T(8,128)(2,1)}, bf16[1,4,48,1920]{3,2,1,0:T(8,128)(2,1)}, u32[]{:S(2)}, u32[]{:S(2)}) collective-permute-start(bf16[1,4,48,1920]{3,2,1,0:T(8,128)(2,1)} %get-tuple-element.226), channel_id=1, source_target_pairs={{0,2},{1,5},{2,0},{3,7},{4,6},{5,1},{6,4},{7,3},{8,10},{9,13},{10,... | collective-permute-start | bytes 2211848 | tf_op jit(solution)/shard_map/ppermute | solution.py:691
  269.3 16.2 %collective-permute-start.42 = (bf16[48,1536]{1,0:T(8,128)(2,1)}, bf16[48,1536]{1,0:T(8,128)(2,1)}, u32[]{:S(2)}, u32[]{:S(2)}) collective-permute-start(bf16[48,1536]{1,0:T(8,128)(2,1)} %get-tuple-element.247), channel_id=1, source_target_pairs={{0,8},{1,9},{2,10},{3,11},{4,12},{5,13},{6,14},{7,15},{8,16},{9,17... | collective-permute-start | bytes 442376 | tf_op jit(solution)/shard_map/ppermute | solution.py:691
  269.3 16.3 %collective-permute-start.43 = (bf16[48,1536]{1,0:T(8,128)(2,1)}, bf16[48,1536]{1,0:T(8,128)(2,1)}, u32[]{:S(2)}, u32[]{:S(2)}) collective-permute-start(bf16[48,1536]{1,0:T(8,128)(2,1)} %get-tuple-element.246), channel_id=1, source_target_pairs={{0,16},{1,17},{2,18},{3,19},{4,20},{5,21},{6,22},{7,23},{8,24},{9,... | collective-permute-start | bytes 442376 | tf_op jit(solution)/shard_map/ppermute | solution.py:691
  271.8 14.1 %collective-permute-start.44 = (bf16[48,1536]{1,0:T(8,128)(2,1)}, bf16[48,1536]{1,0:T(8,128)(2,1)}, u32[]{:S(2)}, u32[]{:S(2)}) collective-permute-start(bf16[48,1536]{1,0:T(8,128)(2,1)} %get-tuple-element.245), channel_id=1, source_target_pairs={{0,24},{1,25},{2,26},{3,27},{4,28},{5,29},{6,30},{7,31},{8,0},{9,1... | collective-permute-start | bytes 442376 | tf_op jit(solution)/shard_map/ppermute | solution.py:691
  273.3 15.2 %collective-permute-start.45 = (bf16[2,4,48,1152]{3,2,1,0:T(8,128)(2,1)S(1)}, bf16[2,4,48,1152]{3,2,1,0:T(8,128)(2,1)S(1)}, u32[]{:S(2)}, u32[]{:S(2)}) collective-permute-start(bf16[2,4,48,1152]{3,2,1,0:T(8,128)(2,1)S(1)} %get-tuple-element.229), channel_id=1, source_target_pairs={{0,4},{1,3},{2,6},{3,1},{4,0},{5,7},{6,2},{7,5},{8,12},{9,11},{10,... | collective-permute-start | bytes 2654216 | tf_op jit(solution)/shard_map/ppermute | solution.py:691
  288.6 12.9 %collective-permute-start.51 = (bf16[48,1920]{1,0:T(8,128)(2,1)S(1)}, bf16[48,1920]{1,0:T(8,128)(2,1)S(1)}, u32[]{:S(2)}, u32[]{:S(2)}) collective-permute-start(bf16[48,1920]{1,0:T(8,128)(2,1)S(1)} %get-tuple-element.242), channel_id=1, source_target_pairs={{0,8},{1,9},{2,10},{3,11},{4,12},{5,13},{6,14},{7,15},{8,16},{9,17... | collective-permute-start | bytes 552968 | tf_op jit(solution)/shard_map/ppermute | solution.py:691
  289.7 15.9 %collective-permute-start.52 = (bf16[48,1920]{1,0:T(8,128)(2,1)S(1)}, bf16[48,1920]{1,0:T(8,128)(2,1)S(1)}, u32[]{:S(2)}, u32[]{:S(2)}) collective-permute-start(bf16[48,1920]{1,0:T(8,128)(2,1)S(1)} %get-tuple-element.244), channel_id=1, source_target_pairs={{0,16},{1,17},{2,18},{3,19},{4,20},{5,21},{6,22},{7,23},{8,24},{9,... | collective-permute-start | bytes 552968 | tf_op jit(solution)/shard_map/ppermute | solution.py:691
  291.9 17.2 %collective-permute-start.53 = (bf16[48,1920]{1,0:T(8,128)(2,1)S(1)}, bf16[48,1920]{1,0:T(8,128)(2,1)S(1)}, u32[]{:S(2)}, u32[]{:S(2)}) collective-permute-start(bf16[48,1920]{1,0:T(8,128)(2,1)S(1)} %get-tuple-element.243), channel_id=1, source_target_pairs={{0,24},{1,25},{2,26},{3,27},{4,28},{5,29},{6,30},{7,31},{8,0},{9,1... | collective-permute-start | bytes 552968 | tf_op jit(solution)/shard_map/ppermute | solution.py:691
  292.5 18.7 %collective-permute-start.55 = (f32[24,1536]{1,0:T(8,128)}, f32[24,1536]{1,0:T(8,128)}, u32[]{:S(2)}, u32[]{:S(2)}) collective-permute-start(f32[24,1536]{1,0:T(8,128)} %get-tuple-element.259), channel_id=1, source_target_pairs={{0,1},{1,0},{2,3},{3,2},{4,5},{5,4},{6,7},{7,6},{8,9},{9,8},{10,11... | collective-permute-start | bytes 442376 | tf_op jit(solution)/shard_map/ppermute | solution.py:691
  295.4 19.0 %collective-permute-start.46 = (bf16[1,4,48,1152]{3,2,1,0:T(8,128)(2,1)S(1)}, bf16[1,4,48,1152]{3,2,1,0:T(8,128)(2,1)S(1)}, u32[]{:S(2)}, u32[]{:S(2)}) collective-permute-start(bf16[1,4,48,1152]{3,2,1,0:T(8,128)(2,1)S(1)} %get-tuple-element.234), channel_id=1, source_target_pairs={{0,2},{1,5},{2,0},{3,7},{4,6},{5,1},{6,4},{7,3},{8,10},{9,13},{10,... | collective-permute-start | bytes 1327112 | tf_op jit(solution)/shard_map/ppermute | solution.py:691
  296.9 16.8 %all-to-all-start.1 = ((f32[8,32,128]{2,0,1:T(8,128)}), f32[8,32,128]{2,0,1:T(8,128)S(1)}, u32[]{:S(2)}, u32[]{:S(2)}) async-start(f32[8,32,128]{2,0,1:T(8,128)} %copy.49), calls=%async_computation.1 | async-start | bytes 262144 | tf_op jit(solution)/shard_map/all_to_all | solution.py:810
  309.2 4.4 %collective-permute-start.56 = (f32[96,384]{1,0:T(8,128)S(1)}, f32[96,384]{1,0:T(8,128)S(1)}, u32[]{:S(2)}, u32[]{:S(2)}) collective-permute-start(f32[96,384]{1,0:T(8,128)S(1)} %get-tuple-element.257), channel_id=1, source_target_pairs={{0,1},{1,0},{2,3},{3,2},{4,5},{5,4},{6,7},{7,6},{8,9},{9,8},{10,11... | collective-permute-start | bytes 442376 | tf_op jit(solution)/shard_map/ppermute | solution.py:691
  311.2 1.8 collective-permute-start.54
  314.6 4.3 %collective-permute-start.47 = (bf16[48,1152]{1,0:T(8,128)(2,1)S(1)}, bf16[48,1152]{1,0:T(8,128)(2,1)S(1)}, u32[]{:S(2)}, u32[]{:S(2)}) collective-permute-start(bf16[48,1152]{1,0:T(8,128)(2,1)S(1)} %get-tuple-element.248), channel_id=1, source_target_pairs={{0,8},{1,9},{2,10},{3,11},{4,12},{5,13},{6,14},{7,15},{8,16},{9,17... | collective-permute-start | bytes 331784 | tf_op jit(solution)/shard_map/ppermute | solution.py:691
  314.6 9.3 %collective-permute-start.48 = (bf16[48,1152]{1,0:T(8,128)(2,1)S(1)}, bf16[48,1152]{1,0:T(8,128)(2,1)S(1)}, u32[]{:S(2)}, u32[]{:S(2)}) collective-permute-start(bf16[48,1152]{1,0:T(8,128)(2,1)S(1)} %get-tuple-element.250), channel_id=1, source_target_pairs={{0,16},{1,17},{2,18},{3,19},{4,20},{5,21},{6,22},{7,23},{8,24},{9,... | collective-permute-start | bytes 331784 | tf_op jit(solution)/shard_map/ppermute | solution.py:691
  315.8 10.6 %collective-permute-start.49 = (bf16[48,1152]{1,0:T(8,128)(2,1)S(1)}, bf16[48,1152]{1,0:T(8,128)(2,1)S(1)}, u32[]{:S(2)}, u32[]{:S(2)}) collective-permute-start(bf16[48,1152]{1,0:T(8,128)(2,1)S(1)} %get-tuple-element.249), channel_id=1, source_target_pairs={{0,24},{1,25},{2,26},{3,27},{4,28},{5,29},{6,30},{7,31},{8,0},{9,1... | collective-permute-start | bytes 331784 | tf_op jit(solution)/shard_map/ppermute | solution.py:691
  326.6 1.5 collective-permute-start.50
  (38 other events, 238.5 us)

commit v4 on v3

--- a/solution.py
+++ b/solution.py
@@ -12,7 +12,6 @@
 AXES = ("wide", "narrow")
 BF, F32 = jnp.bfloat16, jnp.float32
 VMEM_CAP = 58 << 20
-LOG2E = 1.4426950408889634
 
 def params(n=1, cap=VMEM_CAP):
     return pltpu.CompilerParams(dimension_semantics=("arbitrary",) * n, vmem_limit_bytes=cap)
@@ -456,38 +455,33 @@
         cost_estimate=cost(4 * t * d * d, 9e6),
     )(core, lens, gbr, w, *parts)
 
-def unproject_kernel(blocks, core, low_ref, *rest):
-    parts, (send_ref, keep_ref, sums_ref) = rest[:-3], rest[-3:]
-    d = low_ref.shape[1]
-    r, h = d // blocks, d // 2
+def unproject_kernel(blocks, core, low_ref, g_ref, send_ref, keep_ref, sums_ref):
+    d, w = low_ref.shape[1], g_ref.shape[2]
+    r, h = d // blocks, w // 2
     low_t = low_ref[...].T
-    first, second = (keep_ref, send_ref), (send_ref, keep_ref)
-    at = 0
-    for g in parts:
-        w = g.shape[2]
-        for part in range(3):
-            grad = mm(low_t, g[part]).astype(BF).reshape(blocks, r, w)
-            sums_ref[part : part + 1, at : at + w] = jnp.sum(g[part].astype(F32), axis=0, keepdims=True)
-            for half, refs in ((0, first), (1, second)):
-                @pl.when(core[0] == half)
-                def _():
-                    for lo in range(0, w, 128):
-                        to = part * d + at + lo
-                        side, to = to // (d + h), to % (d + h)
-                        refs[side][:, :, to : to + 128] = grad[:, :, lo : lo + 128]
-        at += w
-
-def unproject(core, low, parts, blocks):
+    q, k, v = [mm(low_t, g_ref[part]).astype(BF).reshape(blocks, r, w) for part in range(3)]
+    for half, refs in ((0, (keep_ref, send_ref)), (1, (send_ref, keep_ref))):
+        @pl.when(core[0] == half)
+        def _():
+            refs[0][:, :, :w] = q
+            refs[0][:, :, w:] = k[:, :, :h]
+            refs[1][:, :, :h] = k[:, :, h:]
+            refs[1][:, :, h:] = v
+    for part in range(3):
+        sums_ref[part : part + 1] = jnp.sum(g_ref[part].astype(F32), axis=0, keepdims=True)
+
+def unproject(core, low, g, blocks):
     t, d = low.shape
-    piece = jax.ShapeDtypeStruct((blocks, d // blocks, d // 2 * 3), BF)
+    w = g.shape[2]
+    piece = jax.ShapeDtypeStruct((blocks, d // blocks, w // 2 * 3), BF)
     return pl.pallas_call(
         functools.partial(unproject_kernel, blocks),
         name="unproject",
-        in_specs=[pl.BlockSpec(memory_space=pltpu.SMEM)] + [pl.BlockSpec(memory_space=pltpu.VMEM)] * (1 + len(parts)),
-        out_shape=[piece, piece, jax.ShapeDtypeStruct((3, d), F32)],
+        in_specs=[pl.BlockSpec(memory_space=pltpu.SMEM)] + [pl.BlockSpec(memory_space=pltpu.VMEM)] * 2,
+        out_shape=[piece, piece, jax.ShapeDtypeStruct((3, w), F32)],
         compiler_params=params(0),
-        cost_estimate=cost(6 * t * d * d, 10e6),
-    )(core, low, *parts)
+        cost_estimate=cost(6 * t * d * w, 10e6 * w / d),
+    )(core, low, g)
 
 def route_kernel(count, steps, table, *refs):
     keeps, gots, (away_ref, stay_ref) = refs[:count], refs[count : 2 * count], refs[2 * count :]
@@ -775,9 +769,10 @@
         self.got = [
             grid.up(pick(self.own, (z + k) % grid.z, 0), k) for k in range(1, grid.z)
         ]
+        self.base = pick(self.own, z, 0)
 
     def rows(self):
-        total = pick(self.own, self.grid.here()[0], 0).astype(F32)
+        total = self.base.astype(F32)
         for g in self.got:
             total = total + g.astype(F32)
         return total
@@ -851,10 +846,9 @@
         near_qkv, far_qkv, first, little_all = stage(near_qkv, far_qkv, first, little_all)
         last_qkv = grid.along(near_qkv, 1)
         stack_first = spread_z(grid, first)
-        last_qkv, stack_first = stage(last_qkv, stack_first)
         qkv_sources = with_other(grid, [stack_qkv, near_qkv, far_qkv, last_qkv])
+        *qkv_sources, stack_first, second = stage(*qkv_sources, stack_first, second)
         near_first, far_first = grid.along(stack_first, 0), grid.along(stack_first, 1)
-        *qkv_sources, second = stage(*qkv_sources, second)
         stack_second = spread_z(grid, second)
     else:
         place = jnp.asarray(np.array([[0, 0], [1, 0]], np.int32))
@@ -867,24 +861,30 @@
         place, tokens, gain_one, shift_one, bias_qkv, qkv_sources, blocks
     )
     if grid.paired:
-        qkv, near_first, far_first, stack_second = stage(qkv, near_first, far_first, stack_second)
+        qkv, stack_second = stage(qkv, stack_second)
+        near_second, far_second = grid.along(stack_second, 0), grid.along(stack_second, 1)
+        others = [grid.other_core(stack_first)]
+    attended = [list(attend(seq_lengths, qkv, 4, 0, 512))]
+    if grid.paired:
+        attended[0][2], qkv, near_first, far_first, *others = stage(
+            attended[0][2], qkv, near_first, far_first, *others
+        )
         last_first = grid.along(near_first, 1)
-        near_second, far_second = grid.along(stack_second, 0), grid.along(stack_second, 1)
-    attended = [attend(seq_lengths, qkv, 4, 0, 512)]
-    if grid.paired:
-        qkv, near_second, far_second, last_first, _ = stage(
-            qkv, near_second, far_second, last_first, attended[0][2]
-        )
-        last_second = grid.along(near_second, 1)
-        outs = with_other(grid, [stack_first, near_first, far_first, last_first])
-        seconds = with_other(grid, [stack_second, near_second, far_second, last_second])
-        fcs, out_at, projs = [(s, 0) for s in outs], 4, [(s, 0) for s in seconds]
+        others += [grid.other_core(near_first), grid.other_core(far_first)]
     else:
         fcs = [(s, 0) for s in halves_of(full(fc_weight))]
         outs, out_at = halves_of(full(out_weight)), 0
         projs = [(to_chunks(s[0])[None], 0) for s in halves_of(full(proj_weight))]
     attended.append(attend(seq_lengths, qkv, 2, 4, 512))
     mixed = [a[1] for a in attended]
+    if grid.paired:
+        mixed[1], near_second, far_second, last_first, *others = stage(
+            mixed[1], near_second, far_second, last_first, *others
+        )
+        last_second = grid.along(near_second, 1)
+        outs = [stack_first, near_first, far_first, last_first, *others, grid.other_core(last_first)]
+        seconds = with_other(grid, [stack_second, near_second, far_second, last_second])
+        fcs, out_at, projs = [(s, 0) for s in outs], 4, [(s, 0) for s in seconds]
     middle, low_two, out_full = mix(
         place, mixed, tokens, bias_out, gain_two, shift_two, outs, blocks, out_at
     )
@@ -898,58 +898,70 @@
         proj_sum = Sum(grid, [proj_send, out_send], [proj_keep, out_keep])
         grad_mixed, fc_sum.away, fc_sum.stay = stage(grad_mixed, fc_sum.core(), fc_sum.stay)
         fc_sum.near()
+        grad_mixed, proj_sum.away, proj_sum.stay = stage(grad_mixed, proj_sum.core(), proj_sum.stay)
+        proj_sum.near()
     grad_one = attend_grad(qkv, grad_mixed, attended[0][0], attended[0][2], 0)
+    qkv_one = list(unproject(core, low_one, grad_one, blocks))
     if grid.paired:
-        fc_sum.got, grad_one, grad_mixed = stage(fc_sum.got, grad_one, grad_mixed)
+        qkv_one[2], fc_sum.got, proj_sum.got, grad_mixed = stage(
+            qkv_one[2], fc_sum.got, proj_sum.got, grad_mixed
+        )
         fc_sum.middle()
-        proj_sum.core()
-        grad_mixed, fc_sum.away, fc_sum.stay, proj_sum.away, proj_sum.stay = stage(
-            grad_mixed, fc_sum.away, fc_sum.stay, proj_sum.away, proj_sum.stay
-        )
         fc_sum.far()
-        proj_sum.near()
+        proj_sum.middle()
+        grad_mixed, fc_sum.stay, proj_sum.away, proj_sum.stay = stage(
+            grad_mixed, fc_sum.stay, proj_sum.away, proj_sum.stay
+        )
+        proj_sum.far()
     grad_two = attend_grad(qkv, grad_mixed, attended[1][0], attended[1][2], 4)
     if grid.paired:
         fc_sum.got, grad_two = stage(fc_sum.got, grad_two)
-        fc_sum.own, grad_two = stage(fc_sum.last(), grad_two)
+        fc_sum.last()
         fc_sum.up()
     grads = [grad_one, grad_two]
-    qkv_send, qkv_keep, qkv_sums = unproject(core, low_one, grads, blocks)
+    qkv_two = unproject(core, low_one, grad_two, blocks)
     if grid.paired:
-        qkv_send, proj_sum.got = stage(qkv_send, proj_sum.got)
-        qkv_sum = Sum(grid, [qkv_send], [qkv_keep])
-        proj_sum.away, proj_sum.stay, *qkv_sum.got = stage(proj_sum.middle(), proj_sum.stay, *qkv_sum.got)
-        proj_sum.far()
+        qkv_sum = Sum(grid, [qkv_one[0], qkv_two[0]], [qkv_one[1], qkv_two[1]])
+        *qkv_sum.got, proj_sum.got = stage(*qkv_sum.got, proj_sum.got)
         grad_middle, qkv_sum.away, qkv_sum.stay = stage(grad_middle, qkv_sum.core(), qkv_sum.stay)
         qkv_sum.near()
+        grad_middle, proj_sum.own = stage(grad_middle, proj_sum.last())
+        proj_sum.up()
     input_grad, first_sums = final(tokens, grads, qkv_full, grad_middle, gain_one)
+    qkv_sums = jnp.concatenate([qkv_one[2], qkv_two[2]], 1)
     cut = fold(first_sums, sums, qkv_sums, fc_bias_term, grid.count)
     if grid.paired:
-        first_sums, proj_sum.got, fc_sum.got = stage(first_sums, proj_sum.got, fc_sum.got)
-        first_sums, proj_sum.own, qkv_sum.got = stage(first_sums, proj_sum.last(), qkv_sum.got)
-        proj_sum.up()
+        cut, qkv_sum.got, proj_sum.got[0], proj_sum.got[2], *fc_sum.got = stage(
+            cut, qkv_sum.got, proj_sum.got[0], proj_sum.got[2], *fc_sum.got
+        )
         cut, qkv_sum.away, qkv_sum.stay = stage(cut, qkv_sum.middle(), qkv_sum.stay)
         qkv_sum.far()
     little = scatter_small(cut)
     if grid.paired:
         little, qkv_sum.got = stage(little, qkv_sum.got)
-        proj_sum.own = after(proj_sum.own, qkv_sum.last())
+        proj_sum.got[1], proj_sum.base, fc_sum.base, qkv_sum.own = stage(
+            proj_sum.got[1], proj_sum.base, fc_sum.base, qkv_sum.last()
+        )
         qkv_sum.up()
         fc_weight_grad = own_rows(grid, fc_sum.rows())
         total = proj_sum.rows()
         proj_wide = proj_keep.shape[2]
         proj_weight_grad = own_rows(grid, from_chunks(total[:, :proj_wide]))
         out_weight_grad = own_rows(grid, total[:, proj_wide:])
-        qkv_weight_grad = own_rows(grid, qkv_sum.rows())
+        total = qkv_sum.rows()
+        wide = qkv_one[1].shape[2]
+        ends = [own_rows(grid, total[:, :wide]), own_rows(grid, total[:, wide:])]
     else:
         reduce = lambda v: lax.psum_scatter(v.astype(F32), AXES, scatter_dimension=0, tiled=True)
         side = lambda k, s: jnp.concatenate([k[0], s[0]], 1)
         fc_weight_grad = reduce(side(fc_keep, fc_send))
         out_weight_grad = reduce(side(out_keep, out_send))
-        qkv_weight_grad = reduce(side(qkv_keep, qkv_send))
+        ends = [reduce(side(u[1], u[0])) for u in (qkv_one, qkv_two)]
         proj_weight_grad = reduce(
             jnp.concatenate([from_chunks(proj_keep[0]), from_chunks(proj_send[0])], 1)
         )
+    third = lambda e, i: e[:, i * e.shape[1] // 3 : (i + 1) * e.shape[1] // 3]
+    qkv_weight_grad = jnp.concatenate([third(e, i) for i in range(3) for e in ends], 1)
     shard = lambda s: little[s, : vectors[s].shape[0]]
     return (
         layer_out,

time: 333 us -> 336 us (level)
  local copies, waits for them, and re-layouts: 27.6 us -> 19.3 us
  waiting for transfers between devices: 55.7 us -> 62.7 us
  Pallas kernels: 166 us -> 170 us
  starting transfers between devices: 57.8 us -> 61.6 us
  other arithmetic: 7.98 us -> 4.42 us
    all_to_all x1, waiting for transfers between devices: 0.01 us -> 8.05 us  [scatter_small(): return jnp.sum(lax.all_to_all(cut, AXES, 1, 1, tiled=True), axis=1)]
    unnamed x88 -> x105, local copies, waits for them, and re-layouts: 15.6 us -> 9.66 us
    pallas_call x6, Pallas kernels: 13.8 us -> 17.3 us  [route(): pl.pallas_call(functools.partial(route_kernel, len(keeps), steps), name='...]
    ppermute x57 -> x59, starting transfers between devices: 53.2 us -> 56 us  [send(): return lax.ppermute(value, AXES, self.perm(target))]
    ppermute x57 -> x59, waiting for transfers between devices: 55.7 us -> 54.6 us  [send(): return lax.ppermute(value, AXES, self.perm(target))]
    pallas_call x1 -> x2, Pallas kernels: 11.6 us -> 11.3 us  [unproject(): pl.pallas_call(functools.partial(unproject_kernel, blocks), name='unproje...]
  transfers between devices with their start and end apart: 58 -> 60, of which waited for: 20 -> 19; matrix products, arithmetic and copies ran while one was open for 5% -> 4% of each run, Pallas kernels for 32% -> 31%
where the time goes in v4:
time: 336 us; the launch traced here: 331 us
  Pallas kernels  170 us (51%)
  waiting for transfers between devices  62.7 us (19%)
  starting transfers between devices  61.6 us (18%)
  local copies, waits for them, and re-layouts  19.3 us (6%)
  blocking collectives  11.3 us (3%)
  other arithmetic  4.42 us (1%)
    pallas_call x1, Pallas kernels, mlp(): pl.pallas_call(functools.partial(mlp_kernel, len(fcs), blocks, rb), name=...  59 us
    ppermute x59, starting transfers between devices, send(): return lax.ppermute(value, AXES, self.perm(target))  56 us
    ppermute x59, waiting for transfers between devices, send(): return lax.ppermute(value, AXES, self.perm(target))  54.6 us
    pallas_call x2, Pallas kernels, attend_grad(): pl.pallas_call(functools.partial(attend_grad_kernel, qb), name='attend_gr...  26.9 us
    pallas_call x2, Pallas kernels, attend(): pl.pallas_call(functools.partial(attend_kernel, qb), name='attend', grid=...  19.3 us
    pallas_call x6, Pallas kernels, route(): pl.pallas_call(functools.partial(route_kernel, len(keeps), steps), name='...  17.3 us
    pallas_call x2, Pallas kernels, unproject(): pl.pallas_call(functools.partial(unproject_kernel, blocks), name='unproje...  11.3 us
    all_to_all x1, blocking collectives, gather_small(): lax.all_to_all(jnp.broadcast_to(flat[:, None], (8, count, 128)), AXES, 1,...  11.3 us
  transfers between devices with their start and end apart: 60, of which 19 were waited for; matrix products, arithmetic and copies ran while one was open for 4% of the time, Pallas kernels for 31%

profile of v4, /device:TPU:9, one launch (start us, length us, event | category | flops | bytes accessed | tf_op | source)
XLA Modules:
  0.0 331.5 jit_solution(15679989351518641401)
XLA Ops:
  3.3 1.3 collective-permute-start.1
  4.6 1.1 collective-permute-start.2
  5.7 1.4 collective-permute-start.3
  7.1 0.9 constant_dynamic-slice_fusion.13
  8.0 1.3 collective-permute-start.6
  10.0 0.9 constant_dynamic-slice_fusion.17
  12.6 1.2 collective-permute-done.2
  13.8 2.4 collective-permute-done.3
  16.3 1.3 collective-permute-start.7
  17.6 1.2 collective-permute-start.8
  19.0 11.3 %all_to_all.10 = bf16[8,32,128]{2,0,1:T(8,128)(2,1)S(1)} all-to-all(bf16[8,32,128]{2,0,1:T(8,128)(2,1)S(1)} %broadcast_in_dim.2), channel_id=1, replica_groups=mesh['wide'=8,'narrow'=4] {'wide','narrow'}, dimensions={1} | all-to-all | bytes 131072 | tf_op jit(solution)/shard_map/all_to_all | solution.py:801
  30.3 1.5 collective-permute-start.9
  31.7 0.9 collective-permute-start.15
  32.6 1.0 collective-permute-start.10
  33.6 3.9 %collective-permute-done.14 = bf16[48,1920]{1,0:T(8,128)(2,1)S(1)} collective-permute-done((bf16[48,1920]{1,0:T(8,128)(2,1)S(1)}, bf16[48,1920]{1,0:T(8,128)(2,1)S(1)}, u32[]{:S(2)}, u32[]{:S(2)}) %collective-permute-start.14) | collective-permute-done | bytes 184352 | tf_op jit(solution)/shard_map/ppermute | solution.py:685
  37.6 2.1 collective-permute-start.12
  39.7 3.9 %collective-permute-done.15 = bf16[48,1920]{1,0:T(8,128)(2,1)S(1)} collective-permute-done((bf16[48,1920]{1,0:T(8,128)(2,1)S(1)}, bf16[48,1920]{1,0:T(8,128)(2,1)S(1)}, u32[]{:S(2)}, u32[]{:S(2)}) %collective-permute-start.15) | collective-permute-done | bytes 184352 | tf_op jit(solution)/shard_map/ppermute | solution.py:685
  43.6 3.2 collective-permute-start.16
  46.8 3.5 %collective-permute-done.16 = bf16[48,1920]{1,0:T(8,128)(2,1)S(1)} collective-permute-done((bf16[48,1920]{1,0:T(8,128)(2,1)S(1)}, bf16[48,1920]{1,0:T(8,128)(2,1)S(1)}, u32[]{:S(2)}, u32[]{:S(2)}) %collective-permute-start.16) | collective-permute-done | bytes 184352 | tf_op jit(solution)/shard_map/ppermute | solution.py:685
  53.7 1.3 fusion.4.place
  60.1 3.5 %collective-permute-start.18 = (bf16[48,1536]{1,0:T(8,128)(2,1)S(1)}, bf16[48,1536]{1,0:T(8,128)(2,1)S(1)}, u32[]{:S(2)}, u32[]{:S(2)}) collective-permute-start(bf16[48,1536]{1,0:T(8,128)(2,1)S(1)} %pad_maximum_fusion.5), channel_id=1, source_target_pairs={{0,16},{1,17},{2,18},{3,19},{4,20},{5,21},{6,22},{7,23},{8,24},{9,... | collective-permute-start | bytes 442376 | tf_op jit(solution)/shard_map/ppermute | solution.py:685
  63.7 1.1 collective-permute-start.19
  65.5 3.0 collective-permute-start.22
  68.6 11.0 %project.1 = (bf16[3,1024,768]{2,1,0:T(8,128)(2,1)}, bf16[1024,768]{1,0:T(8,128)(2,1)}, bf16[16,48,2304]{2,1,0:T(8,128)(2,1)}) custom-call(s32[8,5]{1,0:T(8,128)} %fusion.4.place, bf16[1024,768]{1,0:T(8,128)(2,1)} %x_ref.5, f32[1,768]{1,0:T(1,128)} %copy-done.17, f32[1,768]{1,0:T(1,128)} %copy-done.19, f32[3,768]{1,0:T(4,128)} %copy-done.16, ...), custom_call_target="tpu_custom_call" | custom-call | flops 3623878656 | bytes 18000000 | tf_op jit(solution)/shard_map/project/pallas_call | solution.py:225
  79.6 12.3 %attend.2 = (f32[512,1024]{1,0:T(8,128)}, bf16[1024,512]{1,0:T(8,128)(2,1)}, f32[4,2,1024]{2,1,0:T(2,128)}) custom-call(s32[1]{0:T(128)S(6)} %copy.55.len_ref.lens, bf16[3,1024,768]{2,1,0:T(8,128)(2,1)} %get-tuple-element.175.qkv_ref), custom_call_target="tpu_custom_call" | custom-call | flops 2147483648 | bytes 5333333 | tf_op jit(solution)/shard_map/attend/pallas_call | solution.py:66
  92.0 1.7 collective-permute-start.25
  95.4 7.0 %attend.3 = (f32[256,1024]{1,0:T(8,128)}, bf16[1024,256]{1,0:T(8,128)(2,1)}, f32[2,2,1024]{2,1,0:T(2,128)}) custom-call(s32[1]{0:T(128)S(6)} %copy.55.len_ref.lens, bf16[3,1024,768]{2,1,0:T(8,128)(2,1)} %get-tuple-element.175.qkv_ref), custom_call_target="tpu_custom_call" | custom-call | flops 1073741824 | bytes 2666666 | tf_op jit(solution)/shard_map/attend/pallas_call | solution.py:66
  102.4 7.1 %collective-permute-done.23.rest_9_ = bf16[4,48,1536]{2,1,0:T(8,128)(2,1)S(1)} collective-permute-done((bf16[4,48,1536]{2,1,0:T(8,128)(2,1)S(1)}, bf16[4,48,1536]{2,1,0:T(8,128)(2,1)S(1)}, u32[]{:S(2)}, u32[]{:S(2)}) %collective-permute-start.23) | collective-permute-done | bytes 589856 | tf_op jit(solution)/shard_map/ppermute | solution.py:685
  109.5 5.9 %collective-permute-done.24.rest_10_ = bf16[4,48,1536]{2,1,0:T(8,128)(2,1)S(1)} collective-permute-done((bf16[4,48,1536]{2,1,0:T(8,128)(2,1)S(1)}, bf16[4,48,1536]{2,1,0:T(8,128)(2,1)S(1)}, u32[]{:S(2)}, u32[]{:S(2)}) %collective-permute-start.24) | collective-permute-done | bytes 589856 | tf_op jit(solution)/shard_map/ppermute | solution.py:685
  115.4 1.5 collective-permute-start.29
  118.0 6.5 %collective-permute-done.29.rest_11_ = bf16[4,48,1536]{2,1,0:T(8,128)(2,1)S(1)} collective-permute-done((bf16[4,48,1536]{2,1,0:T(8,128)(2,1)S(1)}, bf16[4,48,1536]{2,1,0:T(8,128)(2,1)S(1)}, u32[]{:S(2)}, u32[]{:S(2)}) %collective-permute-start.29) | collective-permute-done | bytes 589856 | tf_op jit(solution)/shard_map/ppermute | solution.py:685
  124.5 1.6 collective-permute-start.33
  127.0 6.9 %mix.1 = (f32[1024,768]{1,0:T(8,128)}, bf16[1024,768]{1,0:T(8,128)(2,1)}, bf16[16,48,768]{2,1,0:T(8,128)(2,1)}) custom-call(s32[8,5]{1,0:T(8,128)} %fusion.4.place, bf16[1024,768]{1,0:T(8,128)(2,1)} %x_ref.5, f32[1,768]{1,0:T(1,128)} %copy-done.10, f32[1,768]{1,0:T(1,128)} %copy-done.9, f32[1,768]{1,0:T(1,128)} %copy-done.11, ...), custom_call_target="tpu_custom_call" | custom-call | flops 1207959552 | bytes 9000000 | tf_op jit(solution)/shard_map/mix/pallas_call | solution.py:266
  134.8 59.0 %mlp.1 = (bf16[1024,768]{1,0:T(8,128)(2,1)}, f32[1024,768]{1,0:T(8,128)}, bf16[1024,768]{1,0:T(8,128)(2,1)}, bf16[16,48,1536]{2,1,0:T(8,128)(2,1)}, bf16[16,48,1...) custom-call(s32[1]{0:T(128)} %bitcast.core, ...), custom_call_target="tpu_custom_call" | custom-call | flops 28991029248 | bytes 40000000 | tf_op jit(solution)/shard_map/mlp/pallas_call | solution.py:393
  194.4 6.7 %unmix.1 = (bf16[1024,768]{1,0:T(8,128)(2,1)}, bf16[16,48,384]{2,1,0:T(8,128)(2,1)}, bf16[16,48,384]{2,1,0:T(8,128)(2,1)}) custom-call(s32[1]{0:T(128)} %bitcast.core, s32[1]{0:T(128)S(6)} %copy.55.len_ref.lens, bf16[1024,768]{1,0:T(8,128)(2,1)} %get-tuple-element.195.gbr_ref, bf16[16,48,768]{2,1,0:T(8,128)(2,1)} %get-tuple-element.196.w_ref, ...), custom_call_target="tpu_custom_call" | custom-call | flops 2415919104 | bytes 9000000 | tf_op jit(solution)/shard_map/unmix/pallas_call | solution.py:449
  202.0 5.0 %route.6 = (bf16[2,4,48,1536]{3,2,1,0:T(8,128)(2,1)}, bf16[2,4,48,1536]{3,2,1,0:T(8,128)(2,1)S(1)}) custom-call(s32[4,2]{1,0:T(4,128)S(1)} %copy.47.table, bf16[4,2,2,48,1536]{4,3,2,1,0:T(8,128)(2,1)S(1)} %bitcast.91, bf16[4,2,2,48,1536]{4,3,2,1,0:T(8,128)(2,1)} %bitcast.24.refs_1_), custom_call_target="tpu_custom_call" | custom-call | flops 1000000 | bytes 7077888 | tf_op jit(solution)/shard_map/route/pallas_call | solution.py:512
  207.0 5.0 %route.7 = (bf16[2,4,48,1920]{3,2,1,0:T(8,128)(2,1)}, bf16[2,4,48,1920]{3,2,1,0:T(8,128)(2,1)S(1)}) custom-call(s32[4,2]{1,0:T(4,128)S(1)} %copy.47.table, bf16[4,2,2,48,1536]{4,3,2,1,0:T(8,128)(2,1)S(1)} %bitcast.90, bf16[4,2,2,48,384]{4,3,2,1,0:T(8,128)(2,1)S(1)} %bitcast.96, bf16[4,2,2,48,1536]{4,3,2,1,0:T(8,128)(2,1)} %bitcast.27.refs_2_, ...), custom_call_target="tpu_custom_call" | custom-call | flops 1000000 | bytes 8847360 | tf_op jit(solution)/shard_map/route/pallas_call | solution.py:512
  214.3 17.1 %attend_grad.2.g_ref.rest_0_ = bf16[3,1024,512]{2,1,0:T(8,128)(2,1)} custom-call(bf16[3,1024,768]{2,1,0:T(8,128)(2,1)} %get-tuple-element.175.qkv_ref, bf16[1024,768]{1,0:T(8,128)(2,1)} %get-tuple-element.225.grad_ref, f32[512,1024]{1,0:T(8,128)} %get-tuple-element.210.out_t_ref, f32[4,2,1024]{2,1,0:T(2,128)} %get-tuple-element.211.stat_ref), custom_call_target="tpu_custom_call" | custom-call | flops 5368709120 | bytes 10666666 | tf_op jit(solution)/shard_map/attend_grad/pallas_call | solution.py:139
  231.4 6.8 %unproject.2 = (bf16[16,48,768]{2,1,0:T(8,128)(2,1)}, bf16[16,48,768]{2,1,0:T(8,128)(2,1)}, f32[3,512]{1,0:T(4,128)}) custom-call(s32[1]{0:T(128)} %bitcast.core, bf16[1024,768]{1,0:T(8,128)(2,1)} %get-tuple-element.194.low_ref, bf16[3,1024,512]{2,1,0:T(8,128)(2,1)} %attend_grad.2.g_ref.rest_0_), custom_call_target="tpu_custom_call" | custom-call | flops 2415919104 | bytes 6666666 | tf_op jit(solution)/shard_map/unproject/pallas_call | solution.py:477
  238.2 5.3 %collective-permute-done.37.refs_1_ = bf16[2,4,48,1536]{3,2,1,0:T(8,128)(2,1)} collective-permute-done((bf16[2,4,48,1536]{3,2,1,0:T(8,128)(2,1)}, bf16[2,4,48,1536]{3,2,1,0:T(8,128)(2,1)}, u32[]{:S(2)}, u32[]{:S(2)}) %collective-permute-start.37) | collective-permute-done | bytes 1179680 | tf_op jit(solution)/shard_map/ppermute | solution.py:685
  243.5 3.0 route.8
  246.5 1.6 collective-permute-start.39
  248.9 1.8 route.9
  250.8 1.5 collective-permute-start.42
  252.3 9.7 %attend_grad.3.g_ref.rest_1_ = bf16[3,1024,256]{2,1,0:T(8,128)(2,1)} custom-call(bf16[3,1024,768]{2,1,0:T(8,128)(2,1)} %get-tuple-element.175.qkv_ref, bf16[1024,768]{1,0:T(8,128)(2,1)} %get-tuple-element.225.grad_ref, f32[256,1024]{1,0:T(8,128)} %get-tuple-element.226.out_t_ref, f32[2,2,1024]{2,1,0:T(2,128)} %get-tuple-element.227.stat_ref), custom_call_target="tpu_custom_call" | custom-call | flops 2684354560 | bytes 5333333 | tf_op jit(solution)/shard_map/attend_grad/pallas_call | solution.py:139
  262.0 4.5 %unproject.3 = (bf16[16,48,384]{2,1,0:T(8,128)(2,1)}, bf16[16,48,384]{2,1,0:T(8,128)(2,1)}, f32[3,256]{1,0:T(4,128)}) custom-call(s32[1]{0:T(128)} %bitcast.core, bf16[1024,768]{1,0:T(8,128)(2,1)} %get-tuple-element.194.low_ref, bf16[3,1024,256]{2,1,0:T(8,128)(2,1)} %attend_grad.3.g_ref.rest_1_), custom_call_target="tpu_custom_call" | custom-call | flops 1207959552 | bytes 3333333 | tf_op jit(solution)/shard_map/unproject/pallas_call | solution.py:477
  266.6 1.3 add_convert_fusion.1
  268.5 1.5 collective-permute-start.47
  270.2 1.6 route.10
  271.8 1.3 collective-permute-start.43
  273.4 1.5 collective-permute-start.44
  275.5 9.7 %final.1 = (bf16[1024,768]{1,0:T(8,128)(2,1)}, f32[2,768]{1,0:T(2,128)}) custom-call(bf16[1024,768]{1,0:T(8,128)(2,1)} %x_ref.5, bf16[16,48,2304]{2,1,0:T(8,128)(2,1)} %get-tuple-element.192.w_ref, f32[1024,768]{1,0:T(8,128)} %get-tuple-element.240.gmid_ref, f32[1,768]{1,0:T(1,128)} %copy-done.17, bf16[3,1024,512]{2,1,0:T(8,128)(2,1)} %attend_grad.2.g_ref.rest_0_, ...), custom_call_target="tpu_custom_call" | custom-call | flops 3623878656 | bytes 15000000 | tf_op jit(solution)/shard_map/final/pallas_call | solution.py:549
  285.9 1.3 fold.1
  287.8 0.9 collective-permute-done.44
  288.8 3.0 collective-permute-done.45
  292.6 1.3 collective-permute-start.49
  294.7 5.6 %all-to-all-start.1 = ((f32[8,32,128]{2,0,1:T(8,128)}), f32[8,32,128]{2,0,1:T(8,128)S(1)}, u32[]{:S(2)}, u32[]{:S(2)}) async-start(f32[8,32,128]{2,0,1:T(8,128)} %copy.49), calls=%async_computation.1 | async-start | bytes 262144 | tf_op jit(solution)/shard_map/all_to_all | solution.py:805
  300.4 2.2 collective-permute-start.50
  302.6 8.0 %all-to-all-done.1 = f32[8,32,128]{2,0,1:T(8,128)S(1)} async-done(((f32[8,32,128]{2,0,1:T(8,128)}), f32[8,32,128]{2,0,1:T(8,128)S(1)}, u32[]{:S(2)}, u32[]{:S(2)}) %all-to-all-start.1) | async-done | bytes 131104 | tf_op jit(solution)/shard_map/all_to_all | solution.py:805
  313.4 1.0 collective-permute-start.51
  314.4 3.9 %collective-permute-start.52 = (bf16[48,1152]{1,0:T(8,128)(2,1)S(1)}, bf16[48,1152]{1,0:T(8,128)(2,1)S(1)}, u32[]{:S(2)}, u32[]{:S(2)}) collective-permute-start(bf16[48,1152]{1,0:T(8,128)(2,1)S(1)} %get-tuple-element.280), channel_id=1, source_target_pairs={{0,16},{1,17},{2,18},{3,19},{4,20},{5,21},{6,22},{7,23},{8,24},{9,... | collective-permute-start | bytes 331784 | tf_op jit(solution)/shard_map/ppermute | solution.py:685
  319.5 6.0 %collective-permute-done.52 = bf16[48,1152]{1,0:T(8,128)(2,1)S(1)} collective-permute-done((bf16[48,1152]{1,0:T(8,128)(2,1)S(1)}, bf16[48,1152]{1,0:T(8,128)(2,1)S(1)}, u32[]{:S(2)}, u32[]{:S(2)}) %collective-permute-start.52) | collective-permute-done | bytes 110624 | tf_op jit(solution)/shard_map/ppermute | solution.py:685
  325.5 2.2 collective-permute-done.53
  327.9 0.9 collective-permute-start.55
  (237 shorter events, 33.7 us)
Async XLA Ops:
  1.5 1.6 collective-permute-start
  3.3 9.3 %collective-permute-start.1 = (bf16[48,1152]{1,0:T(8,128)(2,1)S(1)}, bf16[48,1152]{1,0:T(8,128)(2,1)S(1)}, u32[]{:S(2)}, u32[]{:S(2)}) collective-permute-start(bf16[48,1152]{1,0:T(8,128)(2,1)S(1)} %maximum_select_fusion.5), channel_id=1, source_target_pairs={{0,8},{1,9},{2,10},{3,11},{4,12},{5,13},{6,14},{7,15},{8,16},{9,17... | collective-permute-start | bytes 331784 | tf_op jit(solution)/shard_map/ppermute | solution.py:685
  4.6 9.2 %collective-permute-start.2 = (bf16[48,1152]{1,0:T(8,128)(2,1)S(1)}, bf16[48,1152]{1,0:T(8,128)(2,1)S(1)}, u32[]{:S(2)}, u32[]{:S(2)}) collective-permute-start(bf16[48,1152]{1,0:T(8,128)(2,1)S(1)} %maximum_select_fusion.5), channel_id=1, source_target_pairs={{0,16},{1,17},{2,18},{3,19},{4,20},{5,21},{6,22},{7,23},{8,24},{9,... | collective-permute-start | bytes 331784 | tf_op jit(solution)/shard_map/ppermute | solution.py:685
  5.7 10.6 %collective-permute-start.3 = (bf16[48,1152]{1,0:T(8,128)(2,1)S(1)}, bf16[48,1152]{1,0:T(8,128)(2,1)S(1)}, u32[]{:S(2)}, u32[]{:S(2)}) collective-permute-start(bf16[48,1152]{1,0:T(8,128)(2,1)S(1)} %maximum_select_fusion.5), channel_id=1, source_target_pairs={{0,24},{1,25},{2,26},{3,27},{4,28},{5,29},{6,30},{7,31},{8,0},{9,1... | collective-permute-start | bytes 331784 | tf_op jit(solution)/shard_map/ppermute | solution.py:685
  8.0 3.5 %collective-permute-start.6 = (bf16[96,384]{1,0:T(8,128)(2,1)S(1)}, bf16[96,384]{1,0:T(8,128)(2,1)S(1)}, u32[]{:S(2)}, u32[]{:S(2)}) collective-permute-start(bf16[96,384]{1,0:T(8,128)(2,1)S(1)} %get-tuple-element.297), channel_id=1, source_target_pairs={{0,1},{1,0},{2,3},{3,2},{4,5},{5,4},{6,7},{7,6},{8,9},{9,8},{10,11... | collective-permute-start | bytes 221192 | tf_op jit(solution)/shard_map/ppermute | solution.py:685
  10.0 1.2 collective-permute-start.5
  11.2 1.3 collective-permute-start.4
  16.3 52.2 %copy-start.29 = (bf16[4,48,1152]{2,1,0:T(8,128)(2,1)}, bf16[4,48,1152]{2,1,0:T(8,128)(2,1)S(1)}, u32[]{:S(2)}) copy-start(bf16[4,48,1152]{2,1,0:T(8,128)(2,1)S(1)} %pad_maximum_fusion.2.rest_0_) | copy-start | bytes 1327108
  16.3 13.9 %collective-permute-start.7 = (bf16[4,48,1152]{2,1,0:T(8,128)(2,1)S(1)}, bf16[4,48,1152]{2,1,0:T(8,128)(2,1)S(1)}, u32[]{:S(2)}, u32[]{:S(2)}) collective-permute-start(bf16[4,48,1152]{2,1,0:T(8,128)(2,1)S(1)} %pad_maximum_fusion.2.rest_0_), channel_id=1, source_target_pairs={{0,4},{1,3},{2,6},{3,1},{4,0},{5,7},{6,2},{7,5},{8,12},{9,11},{10,... | collective-permute-start | bytes 1327112 | tf_op jit(solution)/shard_map/ppermute | solution.py:685
  17.6 12.6 %collective-permute-start.8 = (bf16[4,48,1152]{2,1,0:T(8,128)(2,1)S(1)}, bf16[4,48,1152]{2,1,0:T(8,128)(2,1)S(1)}, u32[]{:S(2)}, u32[]{:S(2)}) collective-permute-start(bf16[4,48,1152]{2,1,0:T(8,128)(2,1)S(1)} %pad_maximum_fusion.2.rest_0_), channel_id=1, source_target_pairs={{0,2},{1,5},{2,0},{3,7},{4,6},{5,1},{6,4},{7,3},{8,10},{9,13},{10,... | collective-permute-start | bytes 1327112 | tf_op jit(solution)/shard_map/ppermute | solution.py:685
  30.2 38.3 %copy-start.43 = (bf16[4,48,1152]{2,1,0:T(8,128)(2,1)}, bf16[4,48,1152]{2,1,0:T(8,128)(2,1)S(1)}, u32[]{:S(2)}) copy-start(bf16[4,48,1152]{2,1,0:T(8,128)(2,1)S(1)} %collective-permute-done.7.rest_1_) | copy-start | bytes 1327108
  30.3 38.3 %copy-start.44 = (bf16[4,48,1152]{2,1,0:T(8,128)(2,1)}, bf16[4,48,1152]{2,1,0:T(8,128)(2,1)S(1)}, u32[]{:S(2)}) copy-start(bf16[4,48,1152]{2,1,0:T(8,128)(2,1)S(1)} %collective-permute-done.8.rest_2_) | copy-start | bytes 1327108
  30.3 9.3 %collective-permute-start.9 = (bf16[4,48,1152]{2,1,0:T(8,128)(2,1)S(1)}, bf16[4,48,1152]{2,1,0:T(8,128)(2,1)S(1)}, u32[]{:S(2)}, u32[]{:S(2)}) collective-permute-start(bf16[4,48,1152]{2,1,0:T(8,128)(2,1)S(1)} %collective-permute-done.7.rest_1_), channel_id=1, source_target_pairs={{0,2},{1,5},{2,0},{3,7},{4,6},{5,1},{6,4},{7,3},{8,10},{9,13},{10,... | collective-permute-start | bytes 1327112 | tf_op jit(solution)/shard_map/ppermute | solution.py:685
  31.7 5.8 %collective-permute-start.14 = (bf16[48,1920]{1,0:T(8,128)(2,1)S(1)}, bf16[48,1920]{1,0:T(8,128)(2,1)S(1)}, u32[]{:S(2)}, u32[]{:S(2)}) collective-permute-start(bf16[48,1920]{1,0:T(8,128)(2,1)S(1)} %pad_maximum_fusion.4), channel_id=1, source_target_pairs={{0,8},{1,9},{2,10},{3,11},{4,12},{5,13},{6,14},{7,15},{8,16},{9,17... | collective-permute-start | bytes 552968 | tf_op jit(solution)/shard_map/ppermute | solution.py:685
  31.7 11.8 %collective-permute-start.15 = (bf16[48,1920]{1,0:T(8,128)(2,1)S(1)}, bf16[48,1920]{1,0:T(8,128)(2,1)S(1)}, u32[]{:S(2)}, u32[]{:S(2)}) collective-permute-start(bf16[48,1920]{1,0:T(8,128)(2,1)S(1)} %pad_maximum_fusion.4), channel_id=1, source_target_pairs={{0,16},{1,17},{2,18},{3,19},{4,20},{5,21},{6,22},{7,23},{8,24},{9,... | collective-permute-start | bytes 552968 | tf_op jit(solution)/shard_map/ppermute | solution.py:685
  32.6 17.8 %collective-permute-start.10 = (bf16[4,48,1152]{2,1,0:T(8,128)(2,1)S(1)}, bf16[4,48,1152]{2,1,0:T(8,128)(2,1)S(1)}, u32[]{:S(2)}, u32[]{:S(2)}) collective-permute-start(bf16[4,48,1152]{2,1,0:T(8,128)(2,1)S(1)} %pad_maximum_fusion.2.rest_0_), channel_id=1, source_target_pairs={{0,1},{1,0},{2,3},{3,2},{4,5},{5,4},{6,7},{7,6},{8,9},{9,8},{10,11... | collective-permute-start | bytes 1327112 | tf_op jit(solution)/shard_map/ppermute | solution.py:685
  33.6 16.8 %collective-permute-start.11 = (bf16[4,48,1152]{2,1,0:T(8,128)(2,1)S(1)}, bf16[4,48,1152]{2,1,0:T(8,128)(2,1)S(1)}, u32[]{:S(2)}, u32[]{:S(2)}) collective-permute-start(bf16[4,48,1152]{2,1,0:T(8,128)(2,1)S(1)} %collective-permute-done.7.rest_1_), channel_id=1, source_target_pairs={{0,1},{1,0},{2,3},{3,2},{4,5},{5,4},{6,7},{7,6},{8,9},{9,8},{10,11... | collective-permute-start | bytes 1327112 | tf_op jit(solution)/shard_map/ppermute | solution.py:685
  37.6 12.9 %collective-permute-start.12 = (bf16[4,48,1152]{2,1,0:T(8,128)(2,1)S(1)}, bf16[4,48,1152]{2,1,0:T(8,128)(2,1)S(1)}, u32[]{:S(2)}, u32[]{:S(2)}) collective-permute-start(bf16[4,48,1152]{2,1,0:T(8,128)(2,1)S(1)} %collective-permute-done.8.rest_2_), channel_id=1, source_target_pairs={{0,1},{1,0},{2,3},{3,2},{4,5},{5,4},{6,7},{7,6},{8,9},{9,8},{10,11... | collective-permute-start | bytes 1327112 | tf_op jit(solution)/shard_map/ppermute | solution.py:685
  39.6 10.9 %collective-permute-start.13 = (bf16[4,48,1152]{2,1,0:T(8,128)(2,1)S(1)}, bf16[4,48,1152]{2,1,0:T(8,128)(2,1)S(1)}, u32[]{:S(2)}, u32[]{:S(2)}) collective-permute-start(bf16[4,48,1152]{2,1,0:T(8,128)(2,1)S(1)} %collective-permute-done.9.rest_3_), channel_id=1, source_target_pairs={{0,1},{1,0},{2,3},{3,2},{4,5},{5,4},{6,7},{7,6},{8,9},{9,8},{10,11... | collective-permute-start | bytes 1327112 | tf_op jit(solution)/shard_map/ppermute | solution.py:685
  43.6 6.7 %collective-permute-start.16 = (bf16[48,1920]{1,0:T(8,128)(2,1)S(1)}, bf16[48,1920]{1,0:T(8,128)(2,1)S(1)}, u32[]{:S(2)}, u32[]{:S(2)}) collective-permute-start(bf16[48,1920]{1,0:T(8,128)(2,1)S(1)} %pad_maximum_fusion.4), channel_id=1, source_target_pairs={{0,24},{1,25},{2,26},{3,27},{4,28},{5,29},{6,30},{7,31},{8,0},{9,1... | collective-permute-start | bytes 552968 | tf_op jit(solution)/shard_map/ppermute | solution.py:685
  52.3 13.2 %collective-permute-start.17 = (bf16[48,1536]{1,0:T(8,128)(2,1)S(1)}, bf16[48,1536]{1,0:T(8,128)(2,1)S(1)}, u32[]{:S(2)}, u32[]{:S(2)}) collective-permute-start(bf16[48,1536]{1,0:T(8,128)(2,1)S(1)} %pad_maximum_fusion.5), channel_id=1, source_target_pairs={{0,8},{1,9},{2,10},{3,11},{4,12},{5,13},{6,14},{7,15},{8,16},{9,17... | collective-permute-start | bytes 442376 | tf_op jit(solution)/shard_map/ppermute | solution.py:685
  60.1 19.4 %collective-permute-start.18 = (bf16[48,1536]{1,0:T(8,128)(2,1)S(1)}, bf16[48,1536]{1,0:T(8,128)(2,1)S(1)}, u32[]{:S(2)}, u32[]{:S(2)}) collective-permute-start(bf16[48,1536]{1,0:T(8,128)(2,1)S(1)} %pad_maximum_fusion.5), channel_id=1, source_target_pairs={{0,16},{1,17},{2,18},{3,19},{4,20},{5,21},{6,22},{7,23},{8,24},{9,... | collective-permute-start | bytes 442376 | tf_op jit(solution)/shard_map/ppermute | solution.py:685
  63.7 15.9 %collective-permute-start.19 = (bf16[48,1536]{1,0:T(8,128)(2,1)S(1)}, bf16[48,1536]{1,0:T(8,128)(2,1)S(1)}, u32[]{:S(2)}, u32[]{:S(2)}) collective-permute-start(bf16[48,1536]{1,0:T(8,128)(2,1)S(1)} %pad_maximum_fusion.5), channel_id=1, source_target_pairs={{0,24},{1,25},{2,26},{3,27},{4,28},{5,29},{6,30},{7,31},{8,0},{9,1... | collective-permute-start | bytes 442376 | tf_op jit(solution)/shard_map/ppermute | solution.py:685
  64.7 27.2 %collective-permute-start.20 = (bf16[4,48,1920]{2,1,0:T(8,128)(2,1)S(1)}, bf16[4,48,1920]{2,1,0:T(8,128)(2,1)S(1)}, u32[]{:S(2)}, u32[]{:S(2)}) collective-permute-start(bf16[4,48,1920]{2,1,0:T(8,128)(2,1)S(1)} %pad_maximum_fusion.rest_0_), channel_id=1, source_target_pairs={{0,4},{1,3},{2,6},{3,1},{4,0},{5,7},{6,2},{7,5},{8,12},{9,11},{10,... | collective-permute-start | bytes 2211848 | tf_op jit(solution)/shard_map/ppermute | solution.py:685
  65.5 26.4 %collective-permute-start.21 = (bf16[4,48,1920]{2,1,0:T(8,128)(2,1)S(1)}, bf16[4,48,1920]{2,1,0:T(8,128)(2,1)S(1)}, u32[]{:S(2)}, u32[]{:S(2)}) collective-permute-start(bf16[4,48,1920]{2,1,0:T(8,128)(2,1)S(1)} %pad_maximum_fusion.rest_0_), channel_id=1, source_target_pairs={{0,2},{1,5},{2,0},{3,7},{4,6},{5,1},{6,4},{7,3},{8,10},{9,13},{10,... | collective-permute-start | bytes 2211848 | tf_op jit(solution)/shard_map/ppermute | solution.py:685
  65.5 26.4 %collective-permute-start.22 = (bf16[4,48,1920]{2,1,0:T(8,128)(2,1)S(1)}, bf16[4,48,1920]{2,1,0:T(8,128)(2,1)S(1)}, u32[]{:S(2)}, u32[]{:S(2)}) collective-permute-start(bf16[4,48,1920]{2,1,0:T(8,128)(2,1)S(1)} %pad_maximum_fusion.rest_0_), channel_id=1, source_target_pairs={{0,1},{1,0},{2,3},{3,2},{4,5},{5,4},{6,7},{7,6},{8,9},{9,8},{10,11... | collective-permute-start | bytes 2211848 | tf_op jit(solution)/shard_map/ppermute | solution.py:685
  79.6 37.8 %copy-start.28 = (bf16[4,48,1536]{2,1,0:T(8,128)(2,1)}, bf16[4,48,1536]{2,1,0:T(8,128)(2,1)S(1)}, u32[]{:S(2)}) copy-start(bf16[4,48,1536]{2,1,0:T(8,128)(2,1)S(1)} %pad_maximum_fusion.1.rest_8_) | copy-start | bytes 1769476
  92.0 23.4 %collective-permute-start.25 = (bf16[4,48,1920]{2,1,0:T(8,128)(2,1)S(1)}, bf16[4,48,1920]{2,1,0:T(8,128)(2,1)S(1)}, u32[]{:S(2)}, u32[]{:S(2)}) collective-permute-start(bf16[4,48,1920]{2,1,0:T(8,128)(2,1)S(1)} %collective-permute-done.20.rest_1_), channel_id=1, source_target_pairs={{0,2},{1,5},{2,0},{3,7},{4,6},{5,1},{6,4},{7,3},{8,10},{9,13},{10,... | collective-permute-start | bytes 2211848 | tf_op jit(solution)/shard_map/ppermute | solution.py:685
  93.6 21.8 %collective-permute-start.26 = (bf16[4,48,1920]{2,1,0:T(8,128)(2,1)S(1)}, bf16[4,48,1920]{2,1,0:T(8,128)(2,1)S(1)}, u32[]{:S(2)}, u32[]{:S(2)}) collective-permute-start(bf16[4,48,1920]{2,1,0:T(8,128)(2,1)S(1)} %collective-permute-done.20.rest_1_), channel_id=1, source_target_pairs={{0,1},{1,0},{2,3},{3,2},{4,5},{5,4},{6,7},{7,6},{8,9},{9,8},{10,11... | collective-permute-start | bytes 2211848 | tf_op jit(solution)/shard_map/ppermute | solution.py:685
  93.6 21.8 %collective-permute-start.27 = (bf16[4,48,1920]{2,1,0:T(8,128)(2,1)S(1)}, bf16[4,48,1920]{2,1,0:T(8,128)(2,1)S(1)}, u32[]{:S(2)}, u32[]{:S(2)}) collective-permute-start(bf16[4,48,1920]{2,1,0:T(8,128)(2,1)S(1)} %collective-permute-done.21.rest_2_), channel_id=1, source_target_pairs={{0,1},{1,0},{2,3},{3,2},{4,5},{5,4},{6,7},{7,6},{8,9},{9,8},{10,11... | collective-permute-start | bytes 2211848 | tf_op jit(solution)/shard_map/ppermute | solution.py:685
  94.1 15.4 %collective-permute-start.23 = (bf16[4,48,1536]{2,1,0:T(8,128)(2,1)S(1)}, bf16[4,48,1536]{2,1,0:T(8,128)(2,1)S(1)}, u32[]{:S(2)}, u32[]{:S(2)}) collective-permute-start(bf16[4,48,1536]{2,1,0:T(8,128)(2,1)S(1)} %pad_maximum_fusion.1.rest_8_), channel_id=1, source_target_pairs={{0,4},{1,3},{2,6},{3,1},{4,0},{5,7},{6,2},{7,5},{8,12},{9,11},{10,... | collective-permute-start | bytes 1769480 | tf_op jit(solution)/shard_map/ppermute | solution.py:685
  94.9 20.5 %collective-permute-start.24 = (bf16[4,48,1536]{2,1,0:T(8,128)(2,1)S(1)}, bf16[4,48,1536]{2,1,0:T(8,128)(2,1)S(1)}, u32[]{:S(2)}, u32[]{:S(2)}) collective-permute-start(bf16[4,48,1536]{2,1,0:T(8,128)(2,1)S(1)} %pad_maximum_fusion.1.rest_8_), channel_id=1, source_target_pairs={{0,2},{1,5},{2,0},{3,7},{4,6},{5,1},{6,4},{7,3},{8,10},{9,13},{10,... | collective-permute-start | bytes 1769480 | tf_op jit(solution)/shard_map/ppermute | solution.py:685
  115.4 9.1 %collective-permute-start.29 = (bf16[4,48,1536]{2,1,0:T(8,128)(2,1)S(1)}, bf16[4,48,1536]{2,1,0:T(8,128)(2,1)S(1)}, u32[]{:S(2)}, u32[]{:S(2)}) collective-permute-start(bf16[4,48,1536]{2,1,0:T(8,128)(2,1)S(1)} %collective-permute-done.23.rest_9_), channel_id=1, source_target_pairs={{0,2},{1,5},{2,0},{3,7},{4,6},{5,1},{6,4},{7,3},{8,10},{9,13},{10,... | collective-permute-start | bytes 1769480 | tf_op jit(solution)/shard_map/ppermute | solution.py:685
  117.0 9.2 %collective-permute-start.28 = (bf16[4,48,1920]{2,1,0:T(8,128)(2,1)S(1)}, bf16[4,48,1920]{2,1,0:T(8,128)(2,1)S(1)}, u32[]{:S(2)}, u32[]{:S(2)}) collective-permute-start(bf16[4,48,1920]{2,1,0:T(8,128)(2,1)S(1)} %collective-permute-done.25.rest_3_), channel_id=1, source_target_pairs={{0,1},{1,0},{2,3},{3,2},{4,5},{5,4},{6,7},{7,6},{8,9},{9,8},{10,11... | collective-permute-start | bytes 2211848 | tf_op jit(solution)/shard_map/ppermute | solution.py:685
  117.4 16.5 %collective-permute-start.30 = (bf16[4,48,1536]{2,1,0:T(8,128)(2,1)S(1)}, bf16[4,48,1536]{2,1,0:T(8,128)(2,1)S(1)}, u32[]{:S(2)}, u32[]{:S(2)}) collective-permute-start(bf16[4,48,1536]{2,1,0:T(8,128)(2,1)S(1)} %pad_maximum_fusion.1.rest_8_), channel_id=1, source_target_pairs={{0,1},{1,0},{2,3},{3,2},{4,5},{5,4},{6,7},{7,6},{8,9},{9,8},{10,11... | collective-permute-start | bytes 1769480 | tf_op jit(solution)/shard_map/ppermute | solution.py:685
  117.5 16.5 %collective-permute-start.31 = (bf16[4,48,1536]{2,1,0:T(8,128)(2,1)S(1)}, bf16[4,48,1536]{2,1,0:T(8,128)(2,1)}, u32[]{:S(2)}, u32[]{:S(2)}) collective-permute-start(bf16[4,48,1536]{2,1,0:T(8,128)(2,1)S(1)} %collective-permute-done.23.rest_9_), channel_id=1, source_target_pairs={{0,1},{1,0},{2,3},{3,2},{4,5},{5,4},{6,7},{7,6},{8,9},{9,8},{10,11... | collective-permute-start | bytes 1769480 | tf_op jit(solution)/shard_map/ppermute | solution.py:685
  118.0 16.1 %collective-permute-start.32 = (bf16[4,48,1536]{2,1,0:T(8,128)(2,1)S(1)}, bf16[4,48,1536]{2,1,0:T(8,128)(2,1)}, u32[]{:S(2)}, u32[]{:S(2)}) collective-permute-start(bf16[4,48,1536]{2,1,0:T(8,128)(2,1)S(1)} %collective-permute-done.24.rest_10_), channel_id=1, source_target_pairs={{0,1},{1,0},{2,3},{3,2},{4,5},{5,4},{6,7},{7,6},{8,9},{9,8},{10,11... | collective-permute-start | bytes 1769480 | tf_op jit(solution)/shard_map/ppermute | solution.py:685
  124.5 9.5 %collective-permute-start.33 = (bf16[4,48,1536]{2,1,0:T(8,128)(2,1)S(1)}, bf16[4,48,1536]{2,1,0:T(8,128)(2,1)}, u32[]{:S(2)}, u32[]{:S(2)}) collective-permute-start(bf16[4,48,1536]{2,1,0:T(8,128)(2,1)S(1)} %collective-permute-done.29.rest_11_), channel_id=1, source_target_pairs={{0,1},{1,0},{2,3},{3,2},{4,5},{5,4},{6,7},{7,6},{8,9},{9,8},{10,11... | collective-permute-start | bytes 1769480 | tf_op jit(solution)/shard_map/ppermute | solution.py:685
  193.9 8.1 %collective-permute-start.34 = (bf16[16,48,1536]{2,1,0:T(8,128)(2,1)}, bf16[16,48,1536]{2,1,0:T(8,128)(2,1)}, u32[]{:S(2)}, u32[]{:S(2)}) collective-permute-start(bf16[16,48,1536]{2,1,0:T(8,128)(2,1)} %get-tuple-element.199), channel_id=1, source_target_pairs={{0,1},{1,0},{2,3},{3,2},{4,5},{5,4},{6,7},{7,6},{8,9},{9,8},{10,11... | collective-permute-start | bytes 7077896 | tf_op jit(solution)/shard_map/ppermute | solution.py:685
  194.0 13.0 %collective-permute-start.35 = (bf16[16,48,1536]{2,1,0:T(8,128)(2,1)}, bf16[16,48,1536]{2,1,0:T(8,128)(2,1)}, u32[]{:S(2)}, u32[]{:S(2)}) collective-permute-start(bf16[16,48,1536]{2,1,0:T(8,128)(2,1)} %get-tuple-element.205), channel_id=1, source_target_pairs={{0,1},{1,0},{2,3},{3,2},{4,5},{5,4},{6,7},{7,6},{8,9},{9,8},{10,11... | collective-permute-start | bytes 7077896 | tf_op jit(solution)/shard_map/ppermute | solution.py:685
  201.1 5.9 %collective-permute-start.36 = (bf16[16,48,384]{2,1,0:T(8,128)(2,1)}, bf16[16,48,384]{2,1,0:T(8,128)(2,1)S(1)}, u32[]{:S(2)}, u32[]{:S(2)}) collective-permute-start(bf16[16,48,384]{2,1,0:T(8,128)(2,1)} %get-tuple-element.206), channel_id=1, source_target_pairs={{0,1},{1,0},{2,3},{3,2},{4,5},{5,4},{6,7},{7,6},{8,9},{9,8},{10,11... | collective-permute-start | bytes 1769480 | tf_op jit(solution)/shard_map/ppermute | solution.py:685
  212.0 31.5 %collective-permute-start.38 = (bf16[2,4,48,1920]{3,2,1,0:T(8,128)(2,1)}, bf16[2,4,48,1920]{3,2,1,0:T(8,128)(2,1)S(1)}, u32[]{:S(2)}, u32[]{:S(2)}) collective-permute-start(bf16[2,4,48,1920]{3,2,1,0:T(8,128)(2,1)} %get-tuple-element.216), channel_id=1, source_target_pairs={{0,4},{1,3},{2,6},{3,1},{4,0},{5,7},{6,2},{7,5},{8,12},{9,11},{10,... | collective-permute-start | bytes 4423688 | tf_op jit(solution)/shard_map/ppermute | solution.py:685
  212.9 30.6 %collective-permute-start.37 = (bf16[2,4,48,1536]{3,2,1,0:T(8,128)(2,1)}, bf16[2,4,48,1536]{3,2,1,0:T(8,128)(2,1)}, u32[]{:S(2)}, u32[]{:S(2)}) collective-permute-start(bf16[2,4,48,1536]{3,2,1,0:T(8,128)(2,1)} %get-tuple-element.215), channel_id=1, source_target_pairs={{0,4},{1,3},{2,6},{3,1},{4,0},{5,7},{6,2},{7,5},{8,12},{9,11},{10,... | collective-permute-start | bytes 3538952 | tf_op jit(solution)/shard_map/ppermute | solution.py:685
  246.5 15.5 %collective-permute-start.39 = (bf16[1,4,48,1536]{3,2,1,0:T(8,128)(2,1)}, bf16[1,4,48,1536]{3,2,1,0:T(8,128)(2,1)}, u32[]{:S(2)}, u32[]{:S(2)}) collective-permute-start(bf16[1,4,48,1536]{3,2,1,0:T(8,128)(2,1)} %get-tuple-element.218), channel_id=1, source_target_pairs={{0,2},{1,5},{2,0},{3,7},{4,6},{5,1},{6,4},{7,3},{8,10},{9,13},{10,... | collective-permute-start | bytes 1769480 | tf_op jit(solution)/shard_map/ppermute | solution.py:685
  248.1 21.9 %collective-permute-start.40 = (bf16[16,48,768]{2,1,0:T(8,128)(2,1)}, bf16[16,48,768]{2,1,0:T(8,128)(2,1)S(1)}, u32[]{:S(2)}, u32[]{:S(2)}) collective-permute-start(bf16[16,48,768]{2,1,0:T(8,128)(2,1)} %get-tuple-element.230), channel_id=1, source_target_pairs={{0,1},{1,0},{2,3},{3,2},{4,5},{5,4},{6,7},{7,6},{8,9},{9,8},{10,11... | collective-permute-start | bytes 3538952 | tf_op jit(solution)/shard_map/ppermute | solution.py:685
  250.8 19.3 %collective-permute-start.42 = (bf16[1,4,48,1920]{3,2,1,0:T(8,128)(2,1)}, bf16[1,4,48,1920]{3,2,1,0:T(8,128)(2,1)S(1)}, u32[]{:S(2)}, u32[]{:S(2)}) collective-permute-start(bf16[1,4,48,1920]{3,2,1,0:T(8,128)(2,1)} %get-tuple-element.232), channel_id=1, source_target_pairs={{0,2},{1,5},{2,0},{3,7},{4,6},{5,1},{6,4},{7,3},{8,10},{9,13},{10,... | collective-permute-start | bytes 2211848 | tf_op jit(solution)/shard_map/ppermute | solution.py:685
  266.5 3.6 %collective-permute-start.41 = (bf16[16,48,384]{2,1,0:T(8,128)(2,1)}, bf16[16,48,384]{2,1,0:T(8,128)(2,1)S(1)}, u32[]{:S(2)}, u32[]{:S(2)}) collective-permute-start(bf16[16,48,384]{2,1,0:T(8,128)(2,1)} %get-tuple-element.231), channel_id=1, source_target_pairs={{0,1},{1,0},{2,3},{3,2},{4,5},{5,4},{6,7},{7,6},{8,9},{9,8},{10,11... | collective-permute-start | bytes 1769480 | tf_op jit(solution)/shard_map/ppermute | solution.py:685
  268.0 6.9 %collective-permute-start.46 = (bf16[48,1536]{1,0:T(8,128)(2,1)S(1)}, bf16[48,1536]{1,0:T(8,128)(2,1)S(1)}, u32[]{:S(2)}, u32[]{:S(2)}) collective-permute-start(bf16[48,1536]{1,0:T(8,128)(2,1)S(1)} %get-tuple-element.277), channel_id=1, source_target_pairs={{0,8},{1,9},{2,10},{3,11},{4,12},{5,13},{6,14},{7,15},{8,16},{9,17... | collective-permute-start | bytes 442376 | tf_op jit(solution)/shard_map/ppermute | solution.py:685
  268.5 18.6 %collective-permute-start.47 = (bf16[48,1536]{1,0:T(8,128)(2,1)S(1)}, bf16[48,1536]{1,0:T(8,128)(2,1)S(1)}, u32[]{:S(2)}, u32[]{:S(2)}) collective-permute-start(bf16[48,1536]{1,0:T(8,128)(2,1)S(1)} %get-tuple-element.276), channel_id=1, source_target_pairs={{0,16},{1,17},{2,18},{3,19},{4,20},{5,21},{6,22},{7,23},{8,24},{9,... | collective-permute-start | bytes 442376 | tf_op jit(solution)/shard_map/ppermute | solution.py:685
  270.0 17.8 %collective-permute-start.48 = (bf16[48,1536]{1,0:T(8,128)(2,1)S(1)}, bf16[48,1536]{1,0:T(8,128)(2,1)S(1)}, u32[]{:S(2)}, u32[]{:S(2)}) collective-permute-start(bf16[48,1536]{1,0:T(8,128)(2,1)S(1)} %get-tuple-element.275), channel_id=1, source_target_pairs={{0,24},{1,25},{2,26},{3,27},{4,28},{5,29},{6,30},{7,31},{8,0},{9,1... | collective-permute-start | bytes 442376 | tf_op jit(solution)/shard_map/ppermute | solution.py:685
  271.8 20.0 %collective-permute-start.43 = (bf16[2,4,48,1152]{3,2,1,0:T(8,128)(2,1)S(1)}, bf16[2,4,48,1152]{3,2,1,0:T(8,128)(2,1)S(1)}, u32[]{:S(2)}, u32[]{:S(2)}) collective-permute-start(bf16[2,4,48,1152]{3,2,1,0:T(8,128)(2,1)S(1)} %get-tuple-element.247), channel_id=1, source_target_pairs={{0,4},{1,3},{2,6},{3,1},{4,0},{5,7},{6,2},{7,5},{8,12},{9,11},{10,... | collective-permute-start | bytes 2654216 | tf_op jit(solution)/shard_map/ppermute | solution.py:685
  273.4 15.4 %collective-permute-start.44 = (bf16[48,1920]{1,0:T(8,128)(2,1)S(1)}, bf16[48,1920]{1,0:T(8,128)(2,1)S(1)}, u32[]{:S(2)}, u32[]{:S(2)}) collective-permute-start(bf16[48,1920]{1,0:T(8,128)(2,1)S(1)} %get-tuple-element.273), channel_id=1, source_target_pairs={{0,8},{1,9},{2,10},{3,11},{4,12},{5,13},{6,14},{7,15},{8,16},{9,17... | collective-permute-start | bytes 552968 | tf_op jit(solution)/shard_map/ppermute | solution.py:685
  274.9 16.9 %collective-permute-start.45 = (bf16[48,1920]{1,0:T(8,128)(2,1)S(1)}, bf16[48,1920]{1,0:T(8,128)(2,1)S(1)}, u32[]{:S(2)}, u32[]{:S(2)}) collective-permute-start(bf16[48,1920]{1,0:T(8,128)(2,1)S(1)} %get-tuple-element.272), channel_id=1, source_target_pairs={{0,24},{1,25},{2,26},{3,27},{4,28},{5,29},{6,30},{7,31},{8,0},{9,1... | collective-permute-start | bytes 552968 | tf_op jit(solution)/shard_map/ppermute | solution.py:685
  292.6 18.0 %collective-permute-start.49 = (bf16[1,4,48,1152]{3,2,1,0:T(8,128)(2,1)S(1)}, bf16[1,4,48,1152]{3,2,1,0:T(8,128)(2,1)S(1)}, u32[]{:S(2)}, u32[]{:S(2)}) collective-permute-start(bf16[1,4,48,1152]{3,2,1,0:T(8,128)(2,1)S(1)} %get-tuple-element.257), channel_id=1, source_target_pairs={{0,2},{1,5},{2,0},{3,7},{4,6},{5,1},{6,4},{7,3},{8,10},{9,13},{10,... | collective-permute-start | bytes 1327112 | tf_op jit(solution)/shard_map/ppermute | solution.py:685
  294.7 15.9 %all-to-all-start.1 = ((f32[8,32,128]{2,0,1:T(8,128)}), f32[8,32,128]{2,0,1:T(8,128)S(1)}, u32[]{:S(2)}, u32[]{:S(2)}) async-start(f32[8,32,128]{2,0,1:T(8,128)} %copy.49), calls=%async_computation.1 | async-start | bytes 262144 | tf_op jit(solution)/shard_map/all_to_all | solution.py:805
  300.4 12.0 %collective-permute-start.50 = (bf16[48,1920]{1,0:T(8,128)(2,1)S(1)}, bf16[48,1920]{1,0:T(8,128)(2,1)S(1)}, u32[]{:S(2)}, u32[]{:S(2)}) collective-permute-start(bf16[48,1920]{1,0:T(8,128)(2,1)S(1)} %get-tuple-element.271), channel_id=1, source_target_pairs={{0,16},{1,17},{2,18},{3,19},{4,20},{5,21},{6,22},{7,23},{8,24},{9,... | collective-permute-start | bytes 552968 | tf_op jit(solution)/shard_map/ppermute | solution.py:685
  312.5 17.1 %collective-permute-start.58 = (f32[96,384]{1,0:T(8,128)S(1)}, f32[96,384]{1,0:T(8,128)S(1)}, u32[]{:S(2)}, u32[]{:S(2)}) collective-permute-start(f32[96,384]{1,0:T(8,128)S(1)} %get-tuple-element.287), channel_id=1, source_target_pairs={{0,1},{1,0},{2,3},{3,2},{4,5},{5,4},{6,7},{7,6},{8,9},{9,8},{10,11... | collective-permute-start | bytes 442376 | tf_op jit(solution)/shard_map/ppermute | solution.py:685
  312.7 16.2 %collective-permute-start.57 = (f32[24,1536]{1,0:T(8,128)S(1)}, f32[24,1536]{1,0:T(8,128)S(1)}, u32[]{:S(2)}, u32[]{:S(2)}) collective-permute-start(f32[24,1536]{1,0:T(8,128)S(1)} %get-tuple-element.289), channel_id=1, source_target_pairs={{0,1},{1,0},{2,3},{3,2},{4,5},{5,4},{6,7},{7,6},{8,9},{9,8},{10,11... | collective-permute-start | bytes 442376 | tf_op jit(solution)/shard_map/ppermute | solution.py:685
  313.3 5.0 %collective-permute-start.56 = (f32[24,384]{1,0:T(8,128)S(1)}, f32[24,384]{1,0:T(8,128)S(1)}, u32[]{:S(2)}, u32[]{:S(2)}) collective-permute-start(f32[24,384]{1,0:T(8,128)S(1)} %get-tuple-element.303), channel_id=1, source_target_pairs={{0,1},{1,0},{2,3},{3,2},{4,5},{5,4},{6,7},{7,6},{8,9},{9,8},{10,11... | collective-permute-start | bytes 110600 | tf_op jit(solution)/shard_map/ppermute | solution.py:685
  313.4 6.1 %collective-permute-start.51 = (bf16[48,1152]{1,0:T(8,128)(2,1)S(1)}, bf16[48,1152]{1,0:T(8,128)(2,1)S(1)}, u32[]{:S(2)}, u32[]{:S(2)}) collective-permute-start(bf16[48,1152]{1,0:T(8,128)(2,1)S(1)} %get-tuple-element.278), channel_id=1, source_target_pairs={{0,8},{1,9},{2,10},{3,11},{4,12},{5,13},{6,14},{7,15},{8,16},{9,17... | collective-permute-start | bytes 331784 | tf_op jit(solution)/shard_map/ppermute | solution.py:685
  314.4 11.1 %collective-permute-start.52 = (bf16[48,1152]{1,0:T(8,128)(2,1)S(1)}, bf16[48,1152]{1,0:T(8,128)(2,1)S(1)}, u32[]{:S(2)}, u32[]{:S(2)}) collective-permute-start(bf16[48,1152]{1,0:T(8,128)(2,1)S(1)} %get-tuple-element.280), channel_id=1, source_target_pairs={{0,16},{1,17},{2,18},{3,19},{4,20},{5,21},{6,22},{7,23},{8,24},{9,... | collective-permute-start | bytes 331784 | tf_op jit(solution)/shard_map/ppermute | solution.py:685
  318.3 9.4 %collective-permute-start.53 = (bf16[48,1152]{1,0:T(8,128)(2,1)S(1)}, bf16[48,1152]{1,0:T(8,128)(2,1)S(1)}, u32[]{:S(2)}, u32[]{:S(2)}) collective-permute-start(bf16[48,1152]{1,0:T(8,128)(2,1)S(1)} %get-tuple-element.279), channel_id=1, source_target_pairs={{0,24},{1,25},{2,26},{3,27},{4,28},{5,29},{6,30},{7,31},{8,0},{9,1... | collective-permute-start | bytes 331784 | tf_op jit(solution)/shard_map/ppermute | solution.py:685
  327.9 2.5 collective-permute-start.55
  328.8 1.6 collective-permute-start.54
  (46 other events, 379.6 us)
